TPU v7x, 512 devices: a whole 4x8x8 slice. The times are simulated.
512 devices in a mesh: dp: 16 (over z, core), mp: 32 (over y, x).
Axes of the slice: x: 4, y: 8, z: 8, core: 2. Of those that a mesh axis runs over, the one named last changes fastest.
Arguments:
- inputs: bfloat16 [32768, 4096], P('dp', 'mp'), may hold values from -6 to 6
- out_grad: bfloat16 [32768, 4096], P('dp', 'mp'), may hold values from -6 to 6
- mean_state: float32 [6, 64, 64, 64], P(None, 'mp', 'dp'), may hold values from -0.75 to 0.75
- hess_state: float32 [6, 64, 64, 64], P(None, 'mp', 'dp'), may hold values from 2 to 20
- grad_state: float32 [6, 64, 64, 64], P(None, 'mp', 'dp'), may hold values from -1.8 to 1.8
- noise_draw: float32 [16, 6, 64, 64, 64], P('dp', None, 'mp'), may hold values from -6 to 6
Outputs:
- new_mean: float32 [6, 64, 64, 64], P(None, 'mp', 'dp')
- new_hess: float32 [6, 64, 64, 64], P(None, 'mp', 'dp')
- new_grad: float32 [6, 64, 64, 64], P(None, 'mp', 'dp')
All inputs are finite; a program needn't handle non-finite values.
Results may differ from a plain program's by a relative error of at most 0.0018.
Values may be sent and summed in bfloat16 or wider, within the bound.
No kernel may reach another device: no remote copies, remote signals or barrier semaphores. Data moves between devices by JAX's collectives and lax.ppermute only.
A program may use at most 64 MiB of HBM per device.

v0:
```python
import jax
import jax.numpy as jnp
from jax import lax
from jax.sharding import PartitionSpec as P

LAMBDA_SIZE = 100.0
DELTA_DAMP = 0.001
BETA_GRAD = 0.9
BETA_HESS = 0.9
STEP_RATE = 1.0


def bdot(form, left, right):
    return jnp.einsum(form, left, right, preferred_element_type=jnp.float32)


def silu_slope(value):
    sigm = jax.nn.sigmoid(value)
    return sigm * (1.0 + value * (1.0 - sigm))


def per_device(inputs, out_grad, mean_state, hess_state, grad_state, noise_draw):
    tokens = inputs.shape[0]
    local_blocks = mean_state.shape[1]
    width = mean_state.shape[3]
    scale = tokens ** (-0.5)
    full_mean, full_hess = (
        lax.all_gather(mean_state, "dp", axis=2, tiled=True),
        lax.all_gather(hess_state, "dp", axis=2, tiled=True),
    )
    spread = jnp.sqrt(LAMBDA_SIZE * (full_hess + DELTA_DAMP))
    noise = noise_draw[0]
    sampled = (full_mean + noise / spread).astype(jnp.bfloat16)
    in_rows = inputs.reshape(tokens, local_blocks, width)
    grad_rows = out_grad.reshape(tokens, local_blocks, width)
    y_left = bdot("tbr,brc->tcb", in_rows, sampled[0]).astype(jnp.bfloat16)
    y_right = bdot("tbr,brc->tcb", in_rows, sampled[2]).astype(jnp.bfloat16)
    perm_left = lax.all_to_all(y_left, "mp", split_axis=1, concat_axis=2, tiled=True)
    perm_right = lax.all_to_all(y_right, "mp", split_axis=1, concat_axis=2, tiled=True)
    u_left = bdot("tji,jic->tjc", perm_left, sampled[1])
    u_right = bdot("tji,jic->tjc", perm_right, sampled[3])
    hidden = (jax.nn.silu(u_left) * u_right).astype(jnp.bfloat16)
    outer = bdot("tbr,brc->tcb", hidden, sampled[4]).astype(jnp.bfloat16)
    perm_left, perm_right, u_left, u_right, hidden, outer = (
        perm_left,
        perm_right,
        u_left,
        u_right,
        hidden,
        outer,
    )
    mixed_rows = lax.all_to_all(outer, "mp", split_axis=1, concat_axis=2, tiled=True)
    back_outer = bdot("tjc,jic->tij", grad_rows, sampled[5]).astype(jnp.bfloat16)
    back_hidden = lax.all_to_all(back_outer, "mp", split_axis=1, concat_axis=2, tiled=True)
    grad_five = bdot("tji,tjc->jic", mixed_rows, grad_rows) * scale
    grad_four = bdot("tbr,tbc->brc", hidden, back_hidden) * scale
    d_hidden = bdot("tbc,brc->tbr", back_hidden, sampled[4])
    gate_grad = (d_hidden * u_right * silu_slope(u_left)).astype(jnp.bfloat16)
    value_grad = (d_hidden * jax.nn.silu(u_left)).astype(jnp.bfloat16)
    grad_one = bdot("tji,tjc->jic", perm_left, gate_grad) * scale
    grad_three = bdot("tji,tjc->jic", perm_right, value_grad) * scale
    back_left = bdot("tjc,jic->tij", gate_grad, sampled[1]).astype(jnp.bfloat16)
    back_right = bdot("tjc,jic->tij", value_grad, sampled[3]).astype(jnp.bfloat16)
    rows_left, rows_right = (
        lax.all_to_all(back_left, "mp", split_axis=1, concat_axis=2, tiled=True),
        lax.all_to_all(back_right, "mp", split_axis=1, concat_axis=2, tiled=True),
    )
    grad_zero = bdot("tbr,tbc->brc", in_rows, rows_left) * scale
    grad_two = bdot("tbr,tbc->brc", in_rows, rows_right) * scale
    all_grads = jnp.stack([grad_zero, grad_one, grad_two, grad_three, grad_four, grad_five])
    grad_sum, hess_sum = (
        lax.psum_scatter(all_grads, "dp", scatter_dimension=2, tiled=True),
        lax.psum_scatter(all_grads * noise * spread, "dp", scatter_dimension=2, tiled=True),
    )
    groups = lax.axis_size("dp")
    grad_avg = grad_sum / groups
    hess_avg = hess_sum / groups
    new_grad = BETA_GRAD * grad_state + (1.0 - BETA_GRAD) * grad_avg
    new_hess = (
        BETA_HESS * hess_state
        + (1.0 - BETA_HESS) * hess_avg
        + 0.5 * (1.0 - BETA_HESS) ** 2 * (hess_state - hess_avg) ** 2 / (hess_state + DELTA_DAMP)
    )
    new_mean = mean_state - STEP_RATE * (new_grad + DELTA_DAMP * mean_state) / (
        new_hess + DELTA_DAMP
    )
    return (new_mean, new_hess, new_grad)


def solution(mesh):
    return jax.shard_map(
        per_device,
        mesh=mesh,
        in_specs=(
            P("dp", "mp"),
            P("dp", "mp"),
            P(None, "mp", "dp", None),
            P(None, "mp", "dp", None),
            P(None, "mp", "dp", None),
            P("dp", None, "mp", None, None),
        ),
        out_specs=(P(None, "mp", "dp", None), P(None, "mp", "dp", None), P(None, "mp", "dp", None)),
        check_vma=False,
    )
```

profile of v0, /device:TPU:1, one launch (start us, length us, event | category | flops | bytes accessed | tf_op | source)
XLA Modules:
  0.0 319.1 jit_solution(12250809010809188880)
XLA Ops:
  7.2 0.8 copy.44
  8.0 25.6 %all_gather.7 = f32[6,2,64,64]{3,1,0,2:T(2,128)S(1)} all-gather(f32[6,2,4,64]{3,1,0,2:T(2,128)S(1)} %copy.44), channel_id=1, replica_groups=mesh['dp'=16,'mp'=32] {'dp'}, dimensions={2}, use_global_device_ids=true | all-gather | bytes 208896 | tf_op jit(solution)/shard_map/all_gather | solution.py:29
  33.5 0.8 copy.43
  34.3 15.5 %all_gather.6 = f32[6,2,64,64]{3,1,0,2:T(2,128)S(1)} all-gather(f32[6,2,4,64]{3,1,0,2:T(2,128)S(1)} %copy.43), channel_id=1, replica_groups=mesh['dp'=16,'mp'=32] {'dp'}, dimensions={2}, use_global_device_ids=true | all-gather | bytes 208896 | tf_op jit(solution)/shard_map/all_gather | solution.py:28
  49.8 0.2 copy.50
  50.1 0.8 copy-done.2
  50.8 0.2 fusion.18
  51.0 0.3 fusion.2
  51.4 1.4 copy.56
  52.7 9.8 %all-to-all-start.2 = ((bf16[2048,64,2]{0,2,1:T(2,128)(2,1)}), bf16[2048,64,2]{0,2,1:T(2,128)(2,1)S(1)}, u32[]{:S(2)}, u32[]{:S(2)}) async-start(bf16[2048,64,2]{0,2,1:T(2,128)(2,1)} %copy.56), calls=%async_computation.2 | async-start | bytes 1048576 | tf_op jit(solution)/shard_map/all_to_all | solution.py:38
  62.6 0.2 copy.47
  62.8 0.3 fusion
  63.1 1.4 copy.48
  64.4 14.8 %all-to-all-done.2 = bf16[2048,64,2]{0,2,1:T(2,128)(2,1)S(1)} async-done(((bf16[2048,64,2]{0,2,1:T(2,128)(2,1)}), bf16[2048,64,2]{0,2,1:T(2,128)(2,1)S(1)}, u32[]{:S(2)}, u32[]{:S(2)}) %all-to-all-start.2) | async-done | bytes 524320 | tf_op jit(solution)/shard_map/all_to_all | solution.py:38
  79.2 5.1 %all-to-all-start = ((bf16[2048,64,2]{0,2,1:T(2,128)(2,1)}), bf16[2048,64,2]{0,2,1:T(2,128)(2,1)S(1)}, u32[]{:S(2)}, u32[]{:S(2)}) async-start(bf16[2048,64,2]{0,2,1:T(2,128)(2,1)} %copy.48), calls=%async_computation | async-start | bytes 1048576 | tf_op jit(solution)/shard_map/all_to_all | solution.py:54
  84.3 0.3 fusion.1
  84.7 1.3 copy.52
  86.0 13.7 %all-to-all-done = bf16[2048,64,2]{0,2,1:T(2,128)(2,1)S(1)} async-done(((bf16[2048,64,2]{0,2,1:T(2,128)(2,1)}), bf16[2048,64,2]{0,2,1:T(2,128)(2,1)S(1)}, u32[]{:S(2)}, u32[]{:S(2)}) %all-to-all-start) | async-done | bytes 524320 | tf_op jit(solution)/shard_map/all_to_all | solution.py:54
  99.8 6.1 %all-to-all-start.1 = ((bf16[2048,64,2]{0,2,1:T(2,128)(2,1)}), bf16[2048,64,2]{0,2,1:T(2,128)(2,1)S(1)}, u32[]{:S(2)}, u32[]{:S(2)}) async-start(bf16[2048,64,2]{0,2,1:T(2,128)(2,1)} %copy.52), calls=%async_computation.1 | async-start | bytes 1048576 | tf_op jit(solution)/shard_map/all_to_all | solution.py:39
  105.9 0.4 copy.96
  106.2 0.2 all_to_all.89
  106.4 0.4 copy.98
  106.8 0.2 all_to_all.81
  107.0 2.1 convolution_bitcast_fusion
  109.1 2.0 convolution_bitcast_fusion.2
  111.1 10.0 %all-to-all-done.1 = bf16[2048,64,2]{0,2,1:T(2,128)(2,1)S(1)} async-done(((bf16[2048,64,2]{0,2,1:T(2,128)(2,1)}), bf16[2048,64,2]{0,2,1:T(2,128)(2,1)S(1)}, u32[]{:S(2)}, u32[]{:S(2)}) %all-to-all-start.1) | async-done | bytes 524320 | tf_op jit(solution)/shard_map/all_to_all | solution.py:39
  121.1 0.4 copy.97
  121.5 0.2 all_to_all.85
  121.7 3.1 multiply_convert_fusion
  124.7 1.0 fusion.3
  125.8 1.4 copy.59
  127.1 6.4 %all-to-all-start.3 = ((bf16[2048,64,2]{0,2,1:T(2,128)(2,1)}), bf16[2048,64,2]{0,2,1:T(2,128)(2,1)}, u32[]{:S(2)}, u32[]{:S(2)}) async-start(bf16[2048,64,2]{0,2,1:T(2,128)(2,1)} %copy.59), calls=%async_computation.3 | async-start | bytes 1048576 | tf_op jit(solution)/shard_map/all_to_all | solution.py:65
  133.6 1.3 fusion.4
  134.9 1.3 copy.61
  136.2 12.5 %all-to-all-done.3 = bf16[2048,64,2]{0,2,1:T(2,128)(2,1)} async-done(((bf16[2048,64,2]{0,2,1:T(2,128)(2,1)}), bf16[2048,64,2]{0,2,1:T(2,128)(2,1)}, u32[]{:S(2)}, u32[]{:S(2)}) %all-to-all-start.3) | async-done | bytes 524320 | tf_op jit(solution)/shard_map/all_to_all | solution.py:65
  148.7 6.6 %all-to-all-start.4 = ((bf16[2048,64,2]{0,2,1:T(2,128)(2,1)}), bf16[2048,64,2]{0,2,1:T(2,128)(2,1)}, u32[]{:S(2)}, u32[]{:S(2)}) async-start(bf16[2048,64,2]{0,2,1:T(2,128)(2,1)} %copy.61), calls=%async_computation.4 | async-start | bytes 1048576 | tf_op jit(solution)/shard_map/all_to_all | solution.py:66
  155.4 1.1 fusion.5
  156.5 1.4 copy.64
  157.8 2.2 copy.95
  160.0 2.0 all_to_all.93
  162.1 1.9 fusion.15
  164.0 6.4 %all-to-all-done.4 = bf16[2048,64,2]{0,2,1:T(2,128)(2,1)} async-done(((bf16[2048,64,2]{0,2,1:T(2,128)(2,1)}), bf16[2048,64,2]{0,2,1:T(2,128)(2,1)}, u32[]{:S(2)}, u32[]{:S(2)}) %all-to-all-start.4) | async-done | bytes 524320 | tf_op jit(solution)/shard_map/all_to_all | solution.py:66
  170.4 6.3 %all-to-all-start.5 = ((bf16[2048,64,2]{0,2,1:T(2,128)(2,1)}), bf16[2048,64,2]{0,2,1:T(2,128)(2,1)}, u32[]{:S(2)}, u32[]{:S(2)}) async-start(bf16[2048,64,2]{0,2,1:T(2,128)(2,1)} %copy.64), calls=%async_computation.5 | async-start | bytes 1048576 | tf_op jit(solution)/shard_map/all_to_all | solution.py:52
  176.6 0.0 all-reduce.5.cloned.1.call-start
  176.7 2.2 copy.94
  178.9 2.0 all_to_all.97
  180.9 2.0 fusion.12
  182.9 0.9 copy.66
  183.9 0.7 copy.67
  184.6 0.6 constant_dynamic-update-slice_fusion.1
  185.2 2.0 fusion.14
  187.2 0.6 constant_dynamic-update-slice_fusion
  187.9 0.9 fusion.11
  188.8 0.9 fusion.9
  189.7 2.0 all-to-all-done.5
  191.7 1.4 copy.93
  193.1 0.2 all_to_all.101
  193.3 0.9 fusion.7
  194.2 0.1 copy-done.3
  194.3 1.9 fusion.19
  196.2 0.0 all-reduce.5.cloned.1.call-update
  196.2 1.3 dynamic-slice
  198.2 112.6 %all-reduce.5.cloned.1.call-done = (f32[6,2,64,64]{3,2,1,0:T(8,128)}, f32[6,2,64,64]{3,2,1,0:T(8,128)}) async-done(((f32[6,2,64,64]{3,2,1,0:T(8,128)}, f32[6,2,64,64]{3,2,1,0:T(8,128)}), (f32[6,2,64,64]{3,2,1,0:T(8,128)}, f32[6,2,64,64]{3,2,1,0:T(8,128)})) %all-reduce.5.cloned.1.call-update) | async-done | bytes 393232
  310.7 1.5 divide_subtract_fusion
  (22 shorter events, 0.0 us)
Async XLA Ops:
  7.2 42.7 %copy-start.5 = (bf16[2048,128]{1,0:T(8,128)(2,1)S(1)}, bf16[2048,128]{1,0:T(8,128)(2,1)}, u32[]{:S(2)}) copy-start(bf16[2048,128]{1,0:T(8,128)(2,1)} %param.6) | copy-start | bytes 1572868
  49.8 1.0 copy-start.2
  51.0 33.3 %copy-start.4 = (bf16[6,2,64,64]{3,2,1,0:T(8,128)(2,1)}, bf16[6,2,64,64]{3,2,1,0:T(8,128)(2,1)S(1)}, u32[]{:S(2)}) copy-start(bf16[6,2,64,64]{3,2,1,0:T(8,128)(2,1)S(1)} %fusion.18) | copy-start | bytes 294916
  52.7 9.8 %copy-start.6 = (bf16[2048,128]{1,0:T(8,128)(2,1)S(1)}, bf16[2048,128]{1,0:T(8,128)(2,1)}, u32[]{:S(2)}) copy-start(bf16[2048,128]{1,0:T(8,128)(2,1)} %param.7) | copy-start | bytes 1572868
  52.7 26.5 %all-to-all-start.2 = ((bf16[2048,64,2]{0,2,1:T(2,128)(2,1)}), bf16[2048,64,2]{0,2,1:T(2,128)(2,1)S(1)}, u32[]{:S(2)}, u32[]{:S(2)}) async-start(bf16[2048,64,2]{0,2,1:T(2,128)(2,1)} %copy.56), calls=%async_computation.2 | async-start | bytes 1048576 | tf_op jit(solution)/shard_map/all_to_all | solution.py:38
  79.2 20.5 %all-to-all-start = ((bf16[2048,64,2]{0,2,1:T(2,128)(2,1)}), bf16[2048,64,2]{0,2,1:T(2,128)(2,1)S(1)}, u32[]{:S(2)}, u32[]{:S(2)}) async-start(bf16[2048,64,2]{0,2,1:T(2,128)(2,1)} %copy.48), calls=%async_computation | async-start | bytes 1048576 | tf_op jit(solution)/shard_map/all_to_all | solution.py:54
  99.8 21.3 %all-to-all-start.1 = ((bf16[2048,64,2]{0,2,1:T(2,128)(2,1)}), bf16[2048,64,2]{0,2,1:T(2,128)(2,1)S(1)}, u32[]{:S(2)}, u32[]{:S(2)}) async-start(bf16[2048,64,2]{0,2,1:T(2,128)(2,1)} %copy.52), calls=%async_computation.1 | async-start | bytes 1048576 | tf_op jit(solution)/shard_map/all_to_all | solution.py:39
  124.7 1.0 copy-start.1
  127.1 21.6 %all-to-all-start.3 = ((bf16[2048,64,2]{0,2,1:T(2,128)(2,1)}), bf16[2048,64,2]{0,2,1:T(2,128)(2,1)}, u32[]{:S(2)}, u32[]{:S(2)}) async-start(bf16[2048,64,2]{0,2,1:T(2,128)(2,1)} %copy.59), calls=%async_computation.3 | async-start | bytes 1048576 | tf_op jit(solution)/shard_map/all_to_all | solution.py:65
  148.7 21.6 %all-to-all-start.4 = ((bf16[2048,64,2]{0,2,1:T(2,128)(2,1)}), bf16[2048,64,2]{0,2,1:T(2,128)(2,1)}, u32[]{:S(2)}, u32[]{:S(2)}) async-start(bf16[2048,64,2]{0,2,1:T(2,128)(2,1)} %copy.61), calls=%async_computation.4 | async-start | bytes 1048576 | tf_op jit(solution)/shard_map/all_to_all | solution.py:66
  170.4 21.3 %all-to-all-start.5 = ((bf16[2048,64,2]{0,2,1:T(2,128)(2,1)}), bf16[2048,64,2]{0,2,1:T(2,128)(2,1)}, u32[]{:S(2)}, u32[]{:S(2)}) async-start(bf16[2048,64,2]{0,2,1:T(2,128)(2,1)} %copy.64), calls=%async_computation.5 | async-start | bytes 1048576 | tf_op jit(solution)/shard_map/all_to_all | solution.py:52
  176.6 134.1 %all-reduce.5.cloned.1.call-start = ((), (), s32[]{:S(2)}) async-start(), calls=%async_computation.6 | async-start | bytes 1572864
  182.9 1.0 copy-start.7
  185.2 2.0 copy-start.8
  185.2 2.7 copy-start
  193.3 1.0 copy-start.3
  196.2 114.5 %copy-start.10 = (f32[6,2,4,64]{3,2,1,0:T(4,128)S(1)}, f32[6,2,4,64]{3,2,1,0:T(4,128)}, u32[]{:S(2)}) copy-start(f32[6,2,4,64]{3,2,1,0:T(4,128)} %param.9) | copy-start | bytes 36868
  196.2 114.5 %copy-start.11 = (f32[6,2,4,64]{3,2,1,0:T(4,128)S(1)}, f32[6,2,4,64]{3,2,1,0:T(4,128)}, u32[]{:S(2)}) copy-start(f32[6,2,4,64]{3,2,1,0:T(4,128)} %param.10) | copy-start | bytes 36868
  196.2 114.5 %copy-start.9 = (f32[6,2,4,64]{3,2,1,0:T(4,128)S(1)}, f32[6,2,4,64]{3,2,1,0:T(4,128)}, u32[]{:S(2)}) copy-start(f32[6,2,4,64]{3,2,1,0:T(4,128)} %param.8) | copy-start | bytes 36868
Sparse Core Ops, SparseCore 0:
  196.3 114.3 all-reduce.4
where the time goes:
time: 321 us; the launch traced here: 319 us
  waiting for transfers between devices  172 us (54%)
  blocking collectives  41.1 us (13%)
  starting transfers between devices  40.3 us (13%)
  local copies, waits for them, and re-layouts  27 us (8%)
  matrix products  20.2 us (6%)
  between operations  14.9 us (5%)
  other arithmetic  3.57 us (1%)
    unnamed x2, waiting for transfers between devices  113 us
    all_gather x1, blocking collectives, per_device(): lax.all_gather(hess_state, 'dp', axis=2, tiled=True)  25.6 us
    dot_general x15, matrix products, bdot(): return jnp.einsum(form, left, right, preferred_element_type=jnp.float32)  20.2 us
    all_gather x1, blocking collectives, per_device(): lax.all_gather(mean_state, 'dp', axis=2, tiled=True)  15.5 us
    all_to_all x1, waiting for transfers between devices, per_device(): lax.all_to_all(y_left, 'mp', split_axis=1, concat_axis=2, tiled=True)  14.8 us
    all_to_all x1, waiting for transfers between devices, per_device(): lax.all_to_all(back_outer, 'mp', split_axis=1, concat_axis=2, tiled=True)  13.7 us
    all_to_all x1, waiting for transfers between devices, per_device(): lax.all_to_all(back_left, 'mp', split_axis=1, concat_axis=2, tiled=True)  12.5 us
    all_to_all x1, waiting for transfers between devices, per_device(): lax.all_to_all(y_right, 'mp', split_axis=1, concat_axis=2, tiled=True)  9.96 us
  transfers between devices with their start and end apart: 7, of which 7 were waited for; matrix products, arithmetic and copies ran while one was open for 9% of the time, Pallas kernels for 0%

commit v1 on v0

v1 whole, which is shorter than its diff:
```python
import jax
import jax.numpy as jnp
from jax import lax
from jax.sharding import PartitionSpec as P

LAMBDA_SIZE = 100.0
DELTA_DAMP = 0.001
BETA_GRAD = 0.9
BETA_HESS = 0.9
STEP_RATE = 1.0

REDUCE_MODE = "a2a"


def bdot(form, left, right):
    return jnp.einsum(form, left, right, preferred_element_type=jnp.float32)


def silu_slope(value):
    sigm = jax.nn.sigmoid(value)
    return sigm * (1.0 + value * (1.0 - sigm))


def gather_rows(stacked, groups):
    moved = jnp.moveaxis(stacked, 3, 0)
    full = lax.all_gather(moved, "dp", axis=0, tiled=True)
    return jnp.moveaxis(full, 0, 3)


def scatter_rows(stacked, groups):
    s, f, b, r, w = stacked.shape
    split = stacked.reshape(s, f, b, groups, r // groups, w)
    split = jnp.moveaxis(split, 3, 0)
    if REDUCE_MODE == "a2a":
        got = lax.all_to_all(split, "dp", split_axis=0, concat_axis=0, tiled=True)
        summed = jnp.sum(got, axis=0)
    else:
        summed = lax.psum_scatter(split, "dp", scatter_dimension=0, tiled=False)
    return summed


def per_device(inputs, out_grad, mean_state, hess_state, grad_state, noise_draw):
    tokens = inputs.shape[0]
    local_blocks = mean_state.shape[1]
    width = mean_state.shape[3]
    groups = lax.axis_size("dp")
    scale = tokens ** (-0.5)
    full = gather_rows(jnp.stack([mean_state, hess_state]), groups)
    full_mean, full_hess = full[0], full[1]
    spread = jnp.sqrt(LAMBDA_SIZE * (full_hess + DELTA_DAMP))
    noise = noise_draw[0]
    sampled = (full_mean + noise / spread).astype(jnp.bfloat16)
    in_rows = inputs.reshape(tokens, local_blocks, width)
    grad_rows = out_grad.reshape(tokens, local_blocks, width)
    y_left = bdot("tbr,brc->tcb", in_rows, sampled[0]).astype(jnp.bfloat16)
    y_right = bdot("tbr,brc->tcb", in_rows, sampled[2]).astype(jnp.bfloat16)
    back_outer = bdot("tjc,jic->tij", grad_rows, sampled[5]).astype(jnp.bfloat16)
    first = lax.all_to_all(
        jnp.stack([y_left, y_right, back_outer], axis=1), "mp", split_axis=2, concat_axis=3, tiled=True
    )
    perm_left, perm_right, back_hidden = first[:, 0], first[:, 1], first[:, 2]
    u_left = bdot("tji,jic->tjc", perm_left, sampled[1])
    u_right = bdot("tji,jic->tjc", perm_right, sampled[3])
    hidden = (jax.nn.silu(u_left) * u_right).astype(jnp.bfloat16)
    outer = bdot("tbr,brc->tcb", hidden, sampled[4]).astype(jnp.bfloat16)
    grad_four = bdot("tbr,tbc->brc", hidden, back_hidden) * scale
    d_hidden = bdot("tbc,brc->tbr", back_hidden, sampled[4])
    gate_grad = (d_hidden * u_right * silu_slope(u_left)).astype(jnp.bfloat16)
    value_grad = (d_hidden * jax.nn.silu(u_left)).astype(jnp.bfloat16)
    grad_one = bdot("tji,tjc->jic", perm_left, gate_grad) * scale
    grad_three = bdot("tji,tjc->jic", perm_right, value_grad) * scale
    back_left = bdot("tjc,jic->tij", gate_grad, sampled[1]).astype(jnp.bfloat16)
    back_right = bdot("tjc,jic->tij", value_grad, sampled[3]).astype(jnp.bfloat16)
    second = lax.all_to_all(
        jnp.stack([outer, back_left, back_right], axis=1), "mp", split_axis=2, concat_axis=3, tiled=True
    )
    mixed_rows, rows_left, rows_right = second[:, 0], second[:, 1], second[:, 2]
    grad_five = bdot("tji,tjc->jic", mixed_rows, grad_rows) * scale
    grad_zero = bdot("tbr,tbc->brc", in_rows, rows_left) * scale
    grad_two = bdot("tbr,tbc->brc", in_rows, rows_right) * scale
    all_grads = jnp.stack([grad_zero, grad_one, grad_two, grad_three, grad_four, grad_five])
    sums = scatter_rows(jnp.stack([all_grads, all_grads * noise * spread]), groups)
    grad_avg = sums[0] / groups
    hess_avg = sums[1] / groups
    new_grad = BETA_GRAD * grad_state + (1.0 - BETA_GRAD) * grad_avg
    new_hess = (
        BETA_HESS * hess_state
        + (1.0 - BETA_HESS) * hess_avg
        + 0.5 * (1.0 - BETA_HESS) ** 2 * (hess_state - hess_avg) ** 2 / (hess_state + DELTA_DAMP)
    )
    new_mean = mean_state - STEP_RATE * (new_grad + DELTA_DAMP * mean_state) / (
        new_hess + DELTA_DAMP
    )
    return (new_mean, new_hess, new_grad)


def solution(mesh):
    return jax.shard_map(
        per_device,
        mesh=mesh,
        in_specs=(
            P("dp", "mp"),
            P("dp", "mp"),
            P(None, "mp", "dp", None),
            P(None, "mp", "dp", None),
            P(None, "mp", "dp", None),
            P("dp", None, "mp", None, None),
        ),
        out_specs=(P(None, "mp", "dp", None), P(None, "mp", "dp", None), P(None, "mp", "dp", None)),
        check_vma=False,
    )
```

time: 321 us -> 177 us (0.55)
  waiting for transfers between devices: 172 us -> 0 us
  blocking collectives: 41.1 us -> 138 us
  starting transfers between devices: 40.3 us -> 0 us
  between operations: 14.9 us -> 1.04 us
  local copies, waits for them, and re-layouts: 27 us -> 17.1 us
  matrix products: 20.2 us -> 14.9 us
    unnamed x2 -> x0, waiting for transfers between devices: 113 us -> none
    all_to_all x0 -> x3, blocking collectives: none -> 112 us  [the longest x1 48.9 us: per_device(): lax.all_to_all(jnp.stack([y_left, y_right, back_outer], axis=1), 'mp', sp...]
    all_to_all x6 -> x0, waiting for transfers between devices: 59.4 us -> none  [the longest x1 14.8 us: per_device(): lax.all_to_all(y_left, 'mp', split_axis=1, concat_axis=2, tiled=True)]
    all_to_all x6 -> x0, starting transfers between devices: 40.3 us -> none  [the longest x1 9.8 us: per_device(): lax.all_to_all(y_left, 'mp', split_axis=1, concat_axis=2, tiled=True)]
    all_gather x2 -> x1, blocking collectives: 41.1 us -> 26.8 us  [gather_rows(): full = lax.all_gather(moved, 'dp', axis=0, tiled=True)]
    convert_element_type x6 -> x0, local copies, waits for them, and re-layouts: 8.09 us -> none  [the longest x1 1.36 us: per_device(): y_left = bdot('tbr,brc->tcb', in_rows, sampled[0]).astype(jnp.bfloat16)]
    dot_general x15, matrix products: 20.2 us -> 14.9 us  [bdot(): return jnp.einsum(form, left, right, preferred_element_type=jnp.float32)]
    all_to_all x12 -> x5, local copies, waits for them, and re-layouts: 11.8 us -> 7.09 us  [the longest x2 3.3 us: per_device(): lax.all_to_all(jnp.stack([outer, back_left, back_right], axis=1), 'mp', s...]
  transfers between devices with their start and end apart: 7 -> 0, of which waited for: 7 -> 0; matrix products, arithmetic and copies ran while one was open for 9% -> 0% of each run, Pallas kernels for 0% -> 0%
where the time goes in v1:
time: 177 us
  blocking collectives  138 us (78%)
  local copies, waits for them, and re-layouts  17.1 us (10%)
  matrix products  14.9 us (8%)
  other arithmetic  5.01 us (3%)
    all_to_all x1, blocking collectives, per_device(): lax.all_to_all(jnp.stack([y_left, y_right, back_outer], axis=1), 'mp', sp...  48.9 us
    all_to_all x1, blocking collectives, per_device(): lax.all_to_all(jnp.stack([outer, back_left, back_right], axis=1), 'mp', s...  42.3 us
    all_gather x1, blocking collectives, gather_rows(): full = lax.all_gather(moved, 'dp', axis=0, tiled=True)  26.8 us
    all_to_all x1, blocking collectives, scatter_rows(): got = lax.all_to_all(split, 'dp', split_axis=0, concat_axis=0, tiled=True)  20.5 us
    dot_general x15, matrix products, bdot(): return jnp.einsum(form, left, right, preferred_element_type=jnp.float32)  14.9 us
    unnamed x38, local copies, waits for them, and re-layouts  5.49 us

profile of v1, /device:TPU:1, one launch (start us, length us, event | category | flops | bytes accessed | tf_op | source)
XLA Modules:
  0.0 176.5 jit_solution(16778097129029193267)
XLA Ops:
  0.6 0.0 copy-start.9
  0.6 0.8 pad_maximum_fusion.2
  1.5 0.0 copy-start.5
  1.5 26.8 %all_gather.3 = f32[64,2,6,2,64]{4,3,2,1,0:T(2,128)S(1)} all-gather(f32[4,2,6,2,64]{4,3,2,1,0:T(2,128)S(1)} %bitcast.183), channel_id=1, replica_groups=mesh['dp'=16,'mp'=32] {'dp'}, dimensions={0}, use_global_device_ids=true | all-gather | bytes 417792 | tf_op jit(solution)/shard_map/all_gather | solution.py:26
  28.3 0.4 copy.61
  28.7 0.0 copy-done.9
  28.7 0.2 copy.62
  28.9 0.0 copy-done.5
  28.9 0.2 copy.63
  29.1 0.1 fusion.8
  29.2 0.3 fusion
  29.5 0.3 fusion.1
  29.8 1.2 copy.64
  31.1 0.0 copy-start.2
  31.1 0.3 fusion.2
  31.4 0.2 pad_maximum_fusion
  31.6 0.3 copy-done.2
  31.9 1.6 copy.66
  33.5 48.9 %all_to_all.41 = bf16[2048,3,64,2]{0,3,1,2:T(2,128)(2,1)S(1)} all-to-all(bf16[2048,3,64,2]{0,3,1,2:T(2,128)(2,1)S(1)} %copy.66), channel_id=1, replica_groups=mesh['dp'=16,'mp'=32] {'mp'}, dimensions={2} | all-to-all | bytes 3145728 | tf_op jit(solution)/shard_map/all_to_all | solution.py:58
  82.4 1.3 copy.102
  83.6 2.0 %all_to_all.32 = bf16[2048,3,2,64]{0,3,2,1:T(8,128)(2,1)} reshape(bf16[2048,3,2,32,2]{0,4,3,2,1:T(2,128)(2,1)S(1)} %bitcast.163) | data formatting | bytes 3145728 | tf_op jit(solution)/shard_map/all_to_all | solution.py:58
  85.7 1.5 convolution_bitcast_fusion
  87.2 0.1 copy-done
  87.2 0.3 convolution_bitcast_fusion.2
  87.5 0.6 multiply_convert_fusion.2
  88.1 0.0 copy-start.8
  88.2 0.3 fusion.3
  88.5 0.3 fusion.4
  88.8 0.1 copy-done.8
  88.9 0.2 copy-done.7
  89.1 0.3 fusion.5
  89.5 0.2 pad_maximum_fusion.1
  89.7 1.6 copy.71
  91.3 42.3 %all_to_all.42 = bf16[2048,3,64,2]{0,3,1,2:T(2,128)(2,1)S(1)} all-to-all(bf16[2048,3,64,2]{0,3,1,2:T(2,128)(2,1)S(1)} %copy.71), channel_id=1, replica_groups=mesh['dp'=16,'mp'=32] {'mp'}, dimensions={2} | all-to-all | bytes 3145728 | tf_op jit(solution)/shard_map/all_to_all | solution.py:74
  133.6 1.3 copy.101
  134.9 2.0 %all_to_all.36 = bf16[2048,3,2,64]{0,3,2,1:T(8,128)(2,1)} reshape(bf16[2048,3,2,32,2]{0,4,3,2,1:T(2,128)(2,1)S(1)} %bitcast.165) | data formatting | bytes 3145728 | tf_op jit(solution)/shard_map/all_to_all | solution.py:74
  136.9 1.4 convolution_multiply_fusion.5
  138.4 1.3 convolution_multiply_fusion.3
  139.7 0.1 copy.83
  139.8 0.6 constant_dynamic-update-slice_fusion.7
  140.4 2.0 %bitcast_dynamic-update-slice_fusion.3 = (f32[1,6,2,64,64]{3,4,2,1,0:T(8,128)}, f32[2,64,64]{1,2,0:T(8,128)S(1)}) fusion(f32[1,6,2,64,64]{3,4,2,1,0:T(8,128)} %constant_dynamic-update-slice_fusion.7, bf16[2048,2,64]{0,2,1:T(8,128)(2,1)} %copy-done.8, bf16[2048,3,2,64]{0,3,2,1:T(8,128)(2,1)S(1)} %copy-done.1), kind=kOutput, calls=%fused_computation.45 | convolution fusion | flops 33562624 | bytes 1146880 | tf_op jit(solution)/shard_map/tji,tjc->jic/dot_general | solution.py:16
  142.4 0.1 copy.75
  142.5 0.6 constant_dynamic-update-slice_fusion.5
  143.1 0.1 copy.84
  143.2 0.6 constant_dynamic-update-slice_fusion.6
  143.8 1.9 %bitcast_dynamic-update-slice_fusion.2 = (f32[1,6,2,64,64]{3,4,2,1,0:T(8,128)}, f32[2,64,64]{1,2,0:T(8,128)S(1)}) fusion(f32[1,6,2,64,64]{3,4,2,1,0:T(8,128)} %constant_dynamic-update-slice_fusion.6, bf16[2048,2,64]{0,2,1:T(8,128)(2,1)} %copy-done.7, bf16[2048,3,2,64]{0,3,2,1:T(8,128)(2,1)S(1)} %copy-done.1), kind=kOutput, calls=%fused_computation.44 | convolution fusion | flops 33562624 | bytes 1146880 | tf_op jit(solution)/shard_map/tji,tjc->jic/dot_general | solution.py:16
  145.8 0.1 copy.78
  145.8 1.9 %bitcast_dynamic-update-slice_fusion.1 = (f32[1,6,2,64,64]{3,4,2,1,0:T(8,128)}, f32[2,64,64]{1,2,0:T(8,128)S(1)}) fusion(f32[1,6,2,64,64]{3,4,2,1,0:T(8,128)} %get-tuple-element.11, bf16[2048,2,64]{0,2,1:T(8,128)(2,1)} %copy-done.6, bf16[2048,3,2,64]{0,3,2,1:T(8,128)(2,1)S(1)} %copy-done.1), kind=kOutput, calls=%fused_computation.43 | convolution fusion | flops 33562624 | bytes 1146880 | tf_op jit(solution)/shard_map/tbr,tbc->brc/dot_general | solution.py:16
  147.8 0.1 copy.80
  147.9 0.0 copy-done.3
  147.9 0.0 copy-start.4
  147.9 2.0 %bitcast_dynamic-update-slice_fusion = (f32[1,6,2,64,64]{3,4,2,1,0:T(8,128)}, f32[2,64,64]{1,2,0:T(8,128)S(1)}) fusion(f32[1,6,2,64,64]{3,4,2,1,0:T(8,128)} %get-tuple-element.13, bf16[2048,2,64]{0,2,1:T(8,128)(2,1)S(1)} %bitcast.173, bf16[2048,3,2,64]{0,3,2,1:T(8,128)(2,1)} %all_to_all.36), kind=kOutput, calls=%fused_computation.42 | convolution fusion | flops 33562624 | bytes 1146880 | tf_op jit(solution)/shard_map/tji,tjc->jic/dot_general | solution.py:16
  149.9 0.1 copy.82
  150.0 1.1 sqrt_multiply_fusion
  151.1 0.2 copy.86
  151.4 0.2 maximum_bitcast_fusion
  151.6 0.2 copy.87
  151.8 0.7 reshape.68
  152.6 20.5 %all_to_all.43 = f32[16,1,6144]{2,1,0:T(1,128)S(1)} all-to-all(f32[16,1,6144]{2,1,0:T(1,128)S(1)} %reshape.68), channel_id=1, replica_groups=mesh['dp'=16,'mp'=32] {'dp'}, dimensions={0} | all-to-all | bytes 786432 | tf_op jit(solution)/shard_map/all_to_all | solution.py:35
  173.0 0.5 broadcast.54
  173.6 1.6 reduce
  175.1 0.5 reshape.69
  175.6 0.2 reduce_sum.9
  175.9 0.7 divide_subtract_fusion
  (20 shorter events, 0.1 us)
Async XLA Ops:
  0.6 28.1 %copy-start.9 = (f32[1,6,2,64,64]{4,3,2,1,0:T(8,128)S(1)}, f32[1,6,2,64,64]{4,3,2,1,0:T(8,128)}, u32[]{:S(2)}) copy-start(f32[1,6,2,64,64]{4,3,2,1,0:T(8,128)} %param.11) | copy-start | bytes 589828
  1.5 27.4 %copy-start.5 = (bf16[2048,128]{1,0:T(8,128)(2,1)S(1)}, bf16[2048,128]{1,0:T(8,128)(2,1)}, u32[]{:S(2)}) copy-start(bf16[2048,128]{1,0:T(8,128)(2,1)} %param.6) | copy-start | bytes 1572868
  31.1 0.8 copy-start.2
  85.7 1.6 copy-start
  88.1 0.8 copy-start.8
  88.2 1.0 copy-start.7
  88.2 1.3 copy-start.6
  136.9 3.5 %copy-start.1 = (bf16[2048,3,2,64]{0,3,2,1:T(8,128)(2,1)S(1)}, bf16[2048,3,2,64]{0,3,2,1:T(8,128)(2,1)}, u32[]{:S(2)}) copy-start(bf16[2048,3,2,64]{0,3,2,1:T(8,128)(2,1)} %all_to_all.32) | copy-start | bytes 4718596
  142.5 5.4 %copy-start.3 = (bf16[2048,128]{0,1:T(8,128)(2,1)S(1)}, bf16[2048,128]{0,1:T(8,128)(2,1)}, u32[]{:S(2)}) copy-start(bf16[2048,128]{0,1:T(8,128)(2,1)} %copy-done.2) | copy-start | bytes 1572868
  147.9 3.4 %copy-start.4 = (f32[1,6,2,16,4,64]{5,4,3,2,1,0:T(4,128)S(1)}, f32[1,6,2,16,4,64]{5,4,3,2,1,0:T(4,128)}, u32[]{:S(2)}) copy-start(f32[1,6,2,16,4,64]{5,4,3,2,1,0:T(4,128)} %constant_dynamic-update-slice_fusion.5) | copy-start | bytes 589828
  173.0 2.8 %copy-start.10 = (f32[6,2,4,64]{3,2,1,0:T(4,128)S(1)}, f32[6,2,4,64]{3,2,1,0:T(4,128)}, u32[]{:S(2)}) copy-start(f32[6,2,4,64]{3,2,1,0:T(4,128)} %param.8) | copy-start | bytes 36868
  173.0 2.8 %copy-start.11 = (f32[6,2,4,64]{3,2,1,0:T(4,128)S(1)}, f32[6,2,4,64]{3,2,1,0:T(4,128)}, u32[]{:S(2)}) copy-start(f32[6,2,4,64]{3,2,1,0:T(4,128)} %param.9) | copy-start | bytes 36868
  173.0 2.8 %copy-start.12 = (f32[6,2,4,64]{3,2,1,0:T(4,128)S(1)}, f32[6,2,4,64]{3,2,1,0:T(4,128)}, u32[]{:S(2)}) copy-start(f32[6,2,4,64]{3,2,1,0:T(4,128)} %param.10) | copy-start | bytes 36868

commit v2 on v1

--- a/solution.py
+++ b/solution.py
@@ -1,7 +1,7 @@
 import jax
 import jax.numpy as jnp
 from jax import lax
-from jax.sharding import PartitionSpec as P
+from jax.sharding import Mesh, PartitionSpec as P
 
 LAMBDA_SIZE = 100.0
 DELTA_DAMP = 0.001
@@ -39,6 +39,16 @@
     return summed
 
 
+def mp_exchange(send):
+    t, s, nb, b = send.shape
+    ny, nx = lax.axis_size("my"), lax.axis_size("mx")
+    parts = send.reshape(t, s, ny, nx, nb // (ny * nx), b)
+    parts = lax.all_to_all(parts, "mx", split_axis=3, concat_axis=3, tiled=False)
+    parts = lax.all_to_all(parts, "my", split_axis=2, concat_axis=2, tiled=False)
+    parts = jnp.transpose(parts, (0, 1, 4, 2, 3, 5))
+    return parts.reshape(t, s, nb // (ny * nx), ny * nx * b)
+
+
 def per_device(inputs, out_grad, mean_state, hess_state, grad_state, noise_draw):
     tokens = inputs.shape[0]
     local_blocks = mean_state.shape[1]
@@ -55,9 +65,7 @@
     y_left = bdot("tbr,brc->tcb", in_rows, sampled[0]).astype(jnp.bfloat16)
     y_right = bdot("tbr,brc->tcb", in_rows, sampled[2]).astype(jnp.bfloat16)
     back_outer = bdot("tjc,jic->tij", grad_rows, sampled[5]).astype(jnp.bfloat16)
-    first = lax.all_to_all(
-        jnp.stack([y_left, y_right, back_outer], axis=1), "mp", split_axis=2, concat_axis=3, tiled=True
-    )
+    first = mp_exchange(jnp.stack([y_left, y_right, back_outer], axis=1))
     perm_left, perm_right, back_hidden = first[:, 0], first[:, 1], first[:, 2]
     u_left = bdot("tji,jic->tjc", perm_left, sampled[1])
     u_right = bdot("tji,jic->tjc", perm_right, sampled[3])
@@ -71,9 +79,7 @@
     grad_three = bdot("tji,tjc->jic", perm_right, value_grad) * scale
     back_left = bdot("tjc,jic->tij", gate_grad, sampled[1]).astype(jnp.bfloat16)
     back_right = bdot("tjc,jic->tij", value_grad, sampled[3]).astype(jnp.bfloat16)
-    second = lax.all_to_all(
-        jnp.stack([outer, back_left, back_right], axis=1), "mp", split_axis=2, concat_axis=3, tiled=True
-    )
+    second = mp_exchange(jnp.stack([outer, back_left, back_right], axis=1))
     mixed_rows, rows_left, rows_right = second[:, 0], second[:, 1], second[:, 2]
     grad_five = bdot("tji,tjc->jic", mixed_rows, grad_rows) * scale
     grad_zero = bdot("tbr,tbc->brc", in_rows, rows_left) * scale
@@ -95,17 +101,21 @@
 
 
 def solution(mesh):
+    n_dp, n_mp = mesh.shape["dp"], mesh.shape["mp"]
+    n_x = 4 if n_mp % 4 == 0 else 1
+    split = Mesh(mesh.devices.reshape(n_dp, n_mp // n_x, n_x), ("dp", "my", "mx"))
+    mp = ("my", "mx")
     return jax.shard_map(
         per_device,
-        mesh=mesh,
+        mesh=split,
         in_specs=(
-            P("dp", "mp"),
-            P("dp", "mp"),
-            P(None, "mp", "dp", None),
-            P(None, "mp", "dp", None),
-            P(None, "mp", "dp", None),
-            P("dp", None, "mp", None, None),
+            P("dp", mp),
+            P("dp", mp),
+            P(None, mp, "dp", None),
+            P(None, mp, "dp", None),
+            P(None, mp, "dp", None),
+            P("dp", None, mp, None, None),
         ),
-        out_specs=(P(None, "mp", "dp", None), P(None, "mp", "dp", None), P(None, "mp", "dp", None)),
+        out_specs=(P(None, mp, "dp", None), P(None, mp, "dp", None), P(None, mp, "dp", None)),
         check_vma=False,
     )

time: 177 us -> 235 us (1.33)
  blocking collectives: 138 us -> 178 us
  local copies, waits for them, and re-layouts: 17.1 us -> 25.3 us
  other arithmetic: 5.01 us -> 12.2 us
  matrix products: 14.9 us -> 17.9 us
    all_to_all x2 -> x4, blocking collectives: 91.2 us -> 130 us  [the longest x2 85.8 us: mp_exchange(): lax.all_to_all(parts, 'my', split_axis=2, concat_axis=2, tiled=False)]
    another operation x2, other arithmetic: 0.35 us -> 7.48 us  [the longest x1 3.82 us: per_device(): first = mp_exchange(jnp.stack([y_left, y_right, back_outer], axis=1))]
    another operation x2 -> x8, local copies, waits for them, and re-layouts: 3.24 us -> 7.63 us  [the longest x4 4.2 us: per_device(): first = mp_exchange(jnp.stack([y_left, y_right, back_outer], axis=1))]
    reshape x0 -> x2, local copies, waits for them, and re-layouts: none -> 4.03 us  [mp_exchange(): return parts.reshape(t, s, nb // (ny * nx), ny * nx * b)]
    transpose x0 -> x2, local copies, waits for them, and re-layouts: none -> 3.24 us  [mp_exchange(): parts = jnp.transpose(parts, (0, 1, 4, 2, 3, 5))]
    dot_general x15, matrix products: 14.9 us -> 17.9 us  [bdot(): return jnp.einsum(form, left, right, preferred_element_type=jnp.float32)]
    all_to_all x4 -> x2, local copies, waits for them, and re-layouts: 6.58 us -> 3.57 us  [mp_exchange(): lax.all_to_all(parts, 'mx', split_axis=3, concat_axis=3, tiled=False)]
    unnamed x38 -> x34, local copies, waits for them, and re-layouts: 5.49 us -> 5.06 us
where the time goes in v2:
time: 235 us; the launch traced here: 234 us
  blocking collectives  178 us (76%)
  local copies, waits for them, and re-layouts  25.3 us (11%)
  matrix products  17.9 us (8%)
  other arithmetic  12.2 us (5%)
    all_to_all x2, blocking collectives, mp_exchange(): lax.all_to_all(parts, 'my', split_axis=2, concat_axis=2, tiled=False)  85.8 us
    all_to_all x2, blocking collectives, mp_exchange(): lax.all_to_all(parts, 'mx', split_axis=3, concat_axis=3, tiled=False)  44.3 us
    all_gather x1, blocking collectives, gather_rows(): full = lax.all_gather(moved, 'dp', axis=0, tiled=True)  26.8 us
    all_to_all x1, blocking collectives, scatter_rows(): got = lax.all_to_all(split, 'dp', split_axis=0, concat_axis=0, tiled=True)  21 us
    dot_general x15, matrix products, bdot(): return jnp.einsum(form, left, right, preferred_element_type=jnp.float32)  17.9 us
    unnamed x34, local copies, waits for them, and re-layouts  5.06 us

profile of v2, /device:TPU:1, one launch (start us, length us, event | category | flops | bytes accessed | tf_op | source)
XLA Modules:
  0.0 234.4 jit_solution(3299456120567317426)
XLA Ops:
  0.6 0.8 pad_maximum_fusion.2
  1.5 26.8 %all_gather.3 = f32[64,2,6,2,64]{4,3,2,1,0:T(2,128)S(1)} all-gather(f32[4,2,6,2,64]{4,3,2,1,0:T(2,128)S(1)} %bitcast.175), channel_id=1, replica_groups=mesh['dp'=16,'my'=8,'mx'=4] {'dp'}, dimensions={0}, use_global_device_ids=true | all-gather | bytes 417792 | tf_op jit(solution)/shard_map/all_gather | solution.py:26
  28.3 0.4 copy.61
  28.7 0.2 copy.62
  28.9 0.2 copy.63
  29.1 0.1 fusion.8
  29.2 0.3 fusion
  29.5 0.3 fusion.1
  29.8 0.3 stack.78
  30.2 1.1 stack.79
  31.3 1.2 copy.64
  32.5 0.3 fusion.2
  32.9 1.1 stack.80
  34.0 3.8 %pad_maximum_fusion = bf16[2048,3,8,4,2,2]{0,4,3,2,5,1:T(2,128)(2,1)S(1)} fusion(bf16[2048,1,8,4,2,2]{0,4,3,2,5,1:T(2,128)(2,1)} %stack.80, bf16[2048,1,8,4,2,2]{0,4,3,2,5,1:T(2,128)(2,1)} %stack.79, bf16[2048,1,8,4,2,2]{0,4,3,2,5,1:T(2,128)(2,1)S(1)} %stack.78), kind=kLoop, calls=%fused_computation.15 | loop fusion | flops 1572864 | bytes 3145728 | tf_op jit(solution)/shard_map/stack | solution.py:68
  37.9 1.6 copy.104
  39.5 24.2 %all_to_all.25 = bf16[2048,3,8,4,2,2]{0,4,2,5,1,3:T(2,128)(2,1)S(1)} all-to-all(bf16[2048,3,8,4,2,2]{0,4,2,5,1,3:T(2,128)(2,1)S(1)} %copy.104), channel_id=1, replica_groups=mesh['dp'=16,'my'=8,'mx'=4] {'mx'}, dimensions={3} | all-to-all | bytes 3145728 | tf_op jit(solution)/shard_map/all_to_all | solution.py:46
  63.6 1.8 copy.69
  65.4 44.4 %all_to_all.26 = bf16[2048,3,8,4,2,2]{0,4,3,5,1,2:T(2,128)(2,1)S(1)} all-to-all(bf16[2048,3,8,4,2,2]{0,4,3,5,1,2:T(2,128)(2,1)S(1)} %copy.69), channel_id=1, replica_groups=mesh['dp'=16,'my'=8,'mx'=4] {'my'}, dimensions={2} | all-to-all | bytes 3145728 | tf_op jit(solution)/shard_map/all_to_all | solution.py:47
  109.8 1.6 copy.70
  111.4 2.0 reshape.74
  113.5 1.5 convolution_bitcast_fusion
  115.0 0.1 copy-done
  115.0 0.3 convolution_bitcast_fusion.2
  115.3 1.6 multiply_convert_fusion.2
  116.9 0.3 fusion.3
  117.2 0.3 stack.82
  117.5 0.2 copy-done.6
  117.7 1.4 fusion.4
  119.1 0.3 stack.83
  119.4 1.4 fusion.5
  120.8 1.1 stack.84
  122.0 3.7 %pad_maximum_fusion.1 = bf16[2048,3,8,4,2,2]{0,4,3,2,5,1:T(2,128)(2,1)S(1)} fusion(bf16[2048,1,8,4,2,2]{0,4,3,2,5,1:T(2,128)(2,1)} %stack.84, bf16[2048,1,8,4,2,2]{0,4,3,2,5,1:T(2,128)(2,1)S(1)} %stack.83, bf16[2048,1,8,4,2,2]{0,4,3,2,5,1:T(2,128)(2,1)S(1)} %stack.82), kind=kLoop, calls=%fused_computation.16 | loop fusion | flops 1572864 | bytes 3145728 | tf_op jit(solution)/shard_map/stack | solution.py:82
  125.6 1.6 copy.105
  127.2 20.1 %all_to_all.27 = bf16[2048,3,8,4,2,2]{0,4,2,5,1,3:T(2,128)(2,1)S(1)} all-to-all(bf16[2048,3,8,4,2,2]{0,4,2,5,1,3:T(2,128)(2,1)S(1)} %copy.105), channel_id=1, replica_groups=mesh['dp'=16,'my'=8,'mx'=4] {'mx'}, dimensions={3} | all-to-all | bytes 3145728 | tf_op jit(solution)/shard_map/all_to_all | solution.py:46
  147.3 1.8 copy.77
  149.1 41.5 %all_to_all.28 = bf16[2048,3,8,4,2,2]{0,4,3,5,1,2:T(2,128)(2,1)S(1)} all-to-all(bf16[2048,3,8,4,2,2]{0,4,3,5,1,2:T(2,128)(2,1)S(1)} %copy.77), channel_id=1, replica_groups=mesh['dp'=16,'my'=8,'mx'=4] {'my'}, dimensions={2} | all-to-all | bytes 3145728 | tf_op jit(solution)/shard_map/all_to_all | solution.py:47
  190.6 1.6 copy.78
  192.2 2.0 reshape.75
  194.2 1.4 convolution_multiply_fusion.5
  195.7 1.3 convolution_multiply_fusion.3
  197.0 0.1 copy.89
  197.1 0.6 constant_dynamic-update-slice_fusion.7
  197.7 2.0 bitcast_dynamic-update-slice_fusion.3
  199.7 0.1 copy.81
  199.8 0.6 constant_dynamic-update-slice_fusion.5
  200.4 0.1 copy.90
  200.5 0.6 constant_dynamic-update-slice_fusion.6
  201.1 1.9 bitcast_dynamic-update-slice_fusion.2
  203.0 0.1 copy.84
  203.1 1.9 bitcast_dynamic-update-slice_fusion.1
  205.1 0.1 copy.86
  205.2 2.0 bitcast_dynamic-update-slice_fusion
  207.2 0.1 copy.88
  207.3 1.1 sqrt_multiply_fusion
  208.4 0.2 copy.92
  208.7 0.2 maximum_bitcast_fusion
  208.9 0.2 copy.93
  209.1 0.7 reshape.90
  209.9 21.0 %all_to_all.29 = f32[16,1,6144]{2,1,0:T(1,128)S(1)} all-to-all(f32[16,1,6144]{2,1,0:T(1,128)S(1)} %reshape.90), channel_id=1, replica_groups=mesh['dp'=16,'my'=8,'mx'=4] {'dp'}, dimensions={0} | all-to-all | bytes 786432 | tf_op jit(solution)/shard_map/all_to_all | solution.py:35
  230.9 0.5 broadcast.54
  231.4 1.6 reduce
  233.0 0.5 reshape.91
  233.5 0.2 reduce_sum.9
  233.7 0.7 divide_subtract_fusion
  (26 shorter events, 0.1 us)
Async XLA Ops:
  0.6 28.1 %copy-start.7 = (f32[1,6,2,64,64]{4,3,2,1,0:T(8,128)S(1)}, f32[1,6,2,64,64]{4,3,2,1,0:T(8,128)}, u32[]{:S(2)}) copy-start(f32[1,6,2,64,64]{4,3,2,1,0:T(8,128)} %param.11) | copy-start | bytes 589828
  1.5 27.4 %copy-start.5 = (bf16[2048,128]{1,0:T(8,128)(2,1)S(1)}, bf16[2048,128]{1,0:T(8,128)(2,1)}, u32[]{:S(2)}) copy-start(bf16[2048,128]{1,0:T(8,128)(2,1)} %param.6) | copy-start | bytes 1572868
  32.5 5.3 %copy-start.2 = (bf16[2048,128]{0,1:T(8,128)(2,1)}, bf16[2048,128]{0,1:T(8,128)(2,1)S(1)}, u32[]{:S(2)}) copy-start(bf16[2048,128]{0,1:T(8,128)(2,1)S(1)} %copy.64) | copy-start | bytes 1572868
  113.5 1.6 copy-start
  116.9 0.8 copy-start.6
  194.2 3.5 %copy-start.1 = (bf16[2048,3,2,64]{0,3,2,1:T(8,128)(2,1)S(1)}, bf16[2048,3,2,64]{0,3,2,1:T(8,128)(2,1)}, u32[]{:S(2)}) copy-start(bf16[2048,3,2,64]{0,3,2,1:T(8,128)(2,1)} %reshape.74) | copy-start | bytes 4718596
  199.8 5.4 %copy-start.3 = (bf16[2048,128]{0,1:T(8,128)(2,1)S(1)}, bf16[2048,128]{0,1:T(8,128)(2,1)}, u32[]{:S(2)}) copy-start(bf16[2048,128]{0,1:T(8,128)(2,1)} %copy-done.2) | copy-start | bytes 1572868
  205.2 3.4 %copy-start.4 = (f32[1,6,2,16,4,64]{5,4,3,2,1,0:T(4,128)S(1)}, f32[1,6,2,16,4,64]{5,4,3,2,1,0:T(4,128)}, u32[]{:S(2)}) copy-start(f32[1,6,2,16,4,64]{5,4,3,2,1,0:T(4,128)} %constant_dynamic-update-slice_fusion.5) | copy-start | bytes 589828
  230.9 2.8 %copy-start.8 = (f32[6,2,4,64]{3,2,1,0:T(4,128)S(1)}, f32[6,2,4,64]{3,2,1,0:T(4,128)}, u32[]{:S(2)}) copy-start(f32[6,2,4,64]{3,2,1,0:T(4,128)} %param.8) | copy-start | bytes 36868
  230.9 2.8 %copy-start.9 = (f32[6,2,4,64]{3,2,1,0:T(4,128)S(1)}, f32[6,2,4,64]{3,2,1,0:T(4,128)}, u32[]{:S(2)}) copy-start(f32[6,2,4,64]{3,2,1,0:T(4,128)} %param.9) | copy-start | bytes 36868
  230.9 2.8 %copy-start.10 = (f32[6,2,4,64]{3,2,1,0:T(4,128)S(1)}, f32[6,2,4,64]{3,2,1,0:T(4,128)}, u32[]{:S(2)}) copy-start(f32[6,2,4,64]{3,2,1,0:T(4,128)} %param.10) | copy-start | bytes 36868

commit v3 on v1

--- a/solution.py
+++ b/solution.py
@@ -23,8 +23,19 @@
 
 def gather_rows(stacked, groups):
     moved = jnp.moveaxis(stacked, 3, 0)
-    full = lax.all_gather(moved, "dp", axis=0, tiled=True)
+    copies = jnp.broadcast_to(moved[None], (groups,) + moved.shape)
+    full = lax.all_to_all(copies, "dp", split_axis=0, concat_axis=0, tiled=True)
+    full = full.reshape((groups * moved.shape[0],) + moved.shape[1:])
     return jnp.moveaxis(full, 0, 3)
+
+
+def mp_exchange(send):
+    t, s, nb, b = send.shape
+    n = lax.axis_size("mp")
+    parts = send.reshape(t, s, n, nb // n, b)
+    parts = jnp.swapaxes(parts, 2, 3)
+    got = lax.all_to_all(parts, "mp", split_axis=3, concat_axis=3, tiled=True)
+    return got.reshape(t, s, nb // n, n * b)
 
 
 def scatter_rows(stacked, groups):
@@ -55,9 +66,7 @@
     y_left = bdot("tbr,brc->tcb", in_rows, sampled[0]).astype(jnp.bfloat16)
     y_right = bdot("tbr,brc->tcb", in_rows, sampled[2]).astype(jnp.bfloat16)
     back_outer = bdot("tjc,jic->tij", grad_rows, sampled[5]).astype(jnp.bfloat16)
-    first = lax.all_to_all(
-        jnp.stack([y_left, y_right, back_outer], axis=1), "mp", split_axis=2, concat_axis=3, tiled=True
-    )
+    first = mp_exchange(jnp.stack([y_left, y_right, back_outer], axis=1))
     perm_left, perm_right, back_hidden = first[:, 0], first[:, 1], first[:, 2]
     u_left = bdot("tji,jic->tjc", perm_left, sampled[1])
     u_right = bdot("tji,jic->tjc", perm_right, sampled[3])
@@ -71,9 +80,7 @@
     grad_three = bdot("tji,tjc->jic", perm_right, value_grad) * scale
     back_left = bdot("tjc,jic->tij", gate_grad, sampled[1]).astype(jnp.bfloat16)
     back_right = bdot("tjc,jic->tij", value_grad, sampled[3]).astype(jnp.bfloat16)
-    second = lax.all_to_all(
-        jnp.stack([outer, back_left, back_right], axis=1), "mp", split_axis=2, concat_axis=3, tiled=True
-    )
+    second = mp_exchange(jnp.stack([outer, back_left, back_right], axis=1))
     mixed_rows, rows_left, rows_right = second[:, 0], second[:, 1], second[:, 2]
     grad_five = bdot("tji,tjc->jic", mixed_rows, grad_rows) * scale
     grad_zero = bdot("tbr,tbc->brc", in_rows, rows_left) * scale

time: 177 us -> 186 us (1.051)
  blocking collectives: 138 us -> 112 us
  waiting for transfers between devices: 0 us -> 13.8 us
  starting transfers between devices: 0 us -> 12 us
  other arithmetic: 5.01 us -> 11.6 us
  matrix products: 14.9 us -> 16.9 us
    all_gather x1 -> x0, blocking collectives: 26.8 us -> none  [gather_rows(): full = lax.all_gather(moved, 'dp', axis=0, tiled=True)]
    all_to_all x0 -> x1, waiting for transfers between devices: none -> 13.8 us  [gather_rows(): full = lax.all_to_all(copies, 'dp', split_axis=0, concat_axis=0, tiled=True)]
    all_to_all x0 -> x1, starting transfers between devices: none -> 12 us  [gather_rows(): full = lax.all_to_all(copies, 'dp', split_axis=0, concat_axis=0, tiled=True)]
    transpose x0 -> x3, other arithmetic: none -> 7.04 us  [the longest x2 6.22 us: mp_exchange(): parts = jnp.swapaxes(parts, 2, 3)]
    reshape x0 -> x3, local copies, waits for them, and re-layouts: none -> 4.29 us  [the longest x2 4.03 us: mp_exchange(): return got.reshape(t, s, nb // n, n * b)]
    all_to_all x5 -> x4, local copies, waits for them, and re-layouts: 7.09 us -> 3.15 us  [the longest x2 2.43 us: mp_exchange(): got = lax.all_to_all(parts, 'mp', split_axis=3, concat_axis=3, tiled=True)]
    dot_general x15, matrix products: 14.9 us -> 16.9 us  [bdot(): return jnp.einsum(form, left, right, preferred_element_type=jnp.float32)]
    all_to_all x2, blocking collectives: 91.2 us -> 93.2 us  [mp_exchange(): got = lax.all_to_all(parts, 'mp', split_axis=3, concat_axis=3, tiled=True)]
  transfers between devices with their start and end apart: 0 -> 1, of which waited for: 0 -> 1; matrix products, arithmetic and copies ran while one was open for 0% -> 0% of each run, Pallas kernels for 0% -> 0%
where the time goes in v3:
time: 186 us; the launch traced here: 185 us
  blocking collectives  112 us (60%)
  local copies, waits for them, and re-layouts  17.3 us (9%)
  matrix products  16.9 us (9%)
  waiting for transfers between devices  13.8 us (7%)
  starting transfers between devices  12 us (6%)
  other arithmetic  11.6 us (6%)
    all_to_all x2, blocking collectives, mp_exchange(): got = lax.all_to_all(parts, 'mp', split_axis=3, concat_axis=3, tiled=True)  93.2 us
    all_to_all x1, blocking collectives, scatter_rows(): got = lax.all_to_all(split, 'dp', split_axis=0, concat_axis=0, tiled=True)  19.1 us
    dot_general x15, matrix products, bdot(): return jnp.einsum(form, left, right, preferred_element_type=jnp.float32)  16.9 us
    all_to_all x1, waiting for transfers between devices, gather_rows(): full = lax.all_to_all(copies, 'dp', split_axis=0, concat_axis=0, tiled=True)  13.8 us
    all_to_all x1, starting transfers between devices, gather_rows(): full = lax.all_to_all(copies, 'dp', split_axis=0, concat_axis=0, tiled=True)  12 us
    transpose x2, other arithmetic, mp_exchange(): parts = jnp.swapaxes(parts, 2, 3)  6.22 us
    unnamed x39, local copies, waits for them, and re-layouts  4.31 us
    reshape x2, local copies, waits for them, and re-layouts, mp_exchange(): return got.reshape(t, s, nb // n, n * b)  4.03 us
  transfers between devices with their start and end apart: 1, of which 1 were waited for; matrix products, arithmetic and copies ran while one was open for 0% of the time, Pallas kernels for 0%

profile of v3, /device:TPU:1, one launch (start us, length us, event | category | flops | bytes accessed | tf_op | source)
XLA Modules:
  0.0 184.8 jit_solution(1060529365168472088)
XLA Ops:
  0.6 0.0 copy-start.7
  0.6 0.8 maximum_bitcast_fusion.1
  1.5 0.1 broadcast_bitcast_fusion
  1.6 0.0 copy-start.4
  1.6 1.5 reshape.95
  3.1 12.0 %all-to-all-start = ((f32[16,1,6144]{2,1,0:T(1,128)}), f32[16,1,6144]{2,1,0:T(1,128)S(1)}, u32[]{:S(2)}, u32[]{:S(2)}) async-start(f32[16,1,6144]{2,1,0:T(1,128)} %reshape.95), calls=%async_computation | async-start | bytes 786432 | tf_op jit(solution)/shard_map/all_to_all | solution.py:27
  15.1 0.2 copy.60
  15.2 0.2 copy.61
  15.5 0.0 copy-done.5
  15.5 0.2 copy.62
  15.7 13.8 %all-to-all-done = f32[16,1,6144]{2,1,0:T(1,128)S(1)} async-done(((f32[16,1,6144]{2,1,0:T(1,128)}), f32[16,1,6144]{2,1,0:T(1,128)S(1)}, u32[]{:S(2)}, u32[]{:S(2)}) %all-to-all-start) | async-done | bytes 393248 | tf_op jit(solution)/shard_map/all_to_all | solution.py:27
  29.6 0.5 broadcast.55
  30.1 1.6 reduce
  31.6 0.5 reshape.96
  32.2 0.2 copy.58
  32.4 0.3 copy.59
  32.7 0.1 fusion.8
  32.8 0.3 fusion.1
  33.0 0.3 fusion
  33.3 1.1 fusion.2
  34.5 1.4 stack.80
  35.8 1.1 stack.79
  37.0 0.3 stack.78
  37.3 3.1 %copy_bitcast_fusion.1 = bf16[2048,3,2,32,2]{0,2,4,1,3:T(2,128)(2,1)S(1)} fusion(bf16[2048,1,32,2,2]{0,3,2,4,1:T(2,128)(2,1)S(1)} %stack.80, bf16[2048,1,32,2,2]{0,3,2,4,1:T(2,128)(2,1)} %stack.79, bf16[2048,1,32,2,2]{0,3,2,4,1:T(2,128)(2,1)S(1)} %stack.78), kind=kLoop, calls=%fused_computation.18 | loop fusion | flops 1572864 | bytes 3145728 | tf_op jit(solution)/shard_map/transpose | solution.py:36
  40.4 50.4 %all_to_all.20 = bf16[2048,3,2,32,2]{0,2,4,1,3:T(2,128)(2,1)S(1)} all-to-all(bf16[2048,3,2,32,2]{0,2,4,1,3:T(2,128)(2,1)S(1)} %copy_bitcast_fusion.1), channel_id=1, replica_groups=mesh['dp'=16,'mp'=32] {'mp'}, dimensions={3} | all-to-all | bytes 3145728 | tf_op jit(solution)/shard_map/all_to_all | solution.py:37
  90.8 1.2 copy.67
  92.0 2.0 %reshape.79 = bf16[2048,3,2,64]{0,3,2,1:T(8,128)(2,1)} reshape(bf16[2048,3,2,32,2]{0,4,3,2,1:T(2,128)(2,1)S(1)} %copy.67) | data formatting | bytes 3145728 | tf_op jit(solution)/shard_map/reshape | solution.py:38
  94.1 1.5 convolution_bitcast_fusion
  95.6 0.1 copy-done
  95.6 0.3 convolution_bitcast_fusion.2
  95.9 1.6 multiply_convert_fusion.2
  97.5 0.3 fusion.3
  97.8 0.3 stack.82
  98.2 0.2 copy-done.6
  98.3 1.4 fusion.4
  99.7 0.3 stack.83
  100.0 1.4 fusion.5
  101.4 1.1 stack.84
  102.6 3.1 %copy_bitcast_fusion = bf16[2048,3,2,32,2]{0,2,4,1,3:T(2,128)(2,1)S(1)} fusion(bf16[2048,1,32,2,2]{0,3,2,4,1:T(2,128)(2,1)} %stack.84, bf16[2048,1,32,2,2]{0,3,2,4,1:T(2,128)(2,1)S(1)} %stack.83, bf16[2048,1,32,2,2]{0,3,2,4,1:T(2,128)(2,1)S(1)} %stack.82), kind=kLoop, calls=%fused_computation.17 | loop fusion | flops 1572864 | bytes 3145728 | tf_op jit(solution)/shard_map/transpose | solution.py:36
  105.7 42.8 %all_to_all.21 = bf16[2048,3,2,32,2]{0,2,4,1,3:T(2,128)(2,1)S(1)} all-to-all(bf16[2048,3,2,32,2]{0,2,4,1,3:T(2,128)(2,1)S(1)} %copy_bitcast_fusion), channel_id=1, replica_groups=mesh['dp'=16,'mp'=32] {'mp'}, dimensions={3} | all-to-all | bytes 3145728 | tf_op jit(solution)/shard_map/all_to_all | solution.py:37
  148.5 1.2 copy.74
  149.7 2.0 %reshape.80 = bf16[2048,3,2,64]{0,3,2,1:T(8,128)(2,1)} reshape(bf16[2048,3,2,32,2]{0,4,3,2,1:T(2,128)(2,1)S(1)} %copy.74) | data formatting | bytes 3145728 | tf_op jit(solution)/shard_map/reshape | solution.py:38
  151.7 1.4 convolution_multiply_fusion.3
  153.1 1.3 convolution_multiply_fusion.5
  154.5 0.1 copy.86
  154.6 0.1 copy.85
  154.7 1.3 bitcast_dynamic-update-slice_fusion.3
  156.0 1.4 bitcast_dynamic-update-slice_fusion.2
  157.4 1.9 %bitcast_dynamic-update-slice_fusion.1 = (f32[1,6,2,64,64]{3,4,2,1,0:T(8,128)S(1)}, f32[2,64,64]{1,2,0:T(8,128)}) fusion(f32[1,6,2,64,64]{3,4,2,1,0:T(8,128)S(1)} %get-tuple-element.11, bf16[2048,2,64]{0,2,1:T(8,128)(2,1)} %copy-done.6, bf16[2048,3,2,64]{0,3,2,1:T(8,128)(2,1)S(1)} %copy-done.1), kind=kOutput, calls=%fused_computation.43 | convolution fusion | flops 33562624 | bytes 1146880 | tf_op jit(solution)/shard_map/tbr,tbc->brc/dot_general | solution.py:16
  159.4 1.4 bitcast_dynamic-update-slice_fusion
  160.7 0.2 sqrt_multiply_fusion
  160.9 0.2 copy.88
  161.1 0.1 copy.84
  161.2 0.1 copy.82
  161.2 0.1 copy.80
  161.3 0.1 copy.77
  161.5 0.3 maximum_bitcast_fusion
  161.8 0.2 copy.89
  162.0 0.7 reshape.97
  162.8 19.1 %all_to_all.22 = f32[16,1,6144]{2,1,0:T(1,128)S(1)} all-to-all(f32[16,1,6144]{2,1,0:T(1,128)S(1)} %reshape.97), channel_id=1, replica_groups=mesh['dp'=16,'mp'=32] {'dp'}, dimensions={0} | all-to-all | bytes 786432 | tf_op jit(solution)/shard_map/all_to_all | solution.py:46
  181.8 1.6 reduce.1
  183.4 0.5 reshape.98
  184.0 0.2 reduce_sum.9
  184.2 0.7 divide_subtract_fusion
  (27 shorter events, 0.1 us)
Async XLA Ops:
  0.6 14.4 %copy-start.7 = (f32[1,6,2,64,64]{4,3,2,1,0:T(8,128)S(1)}, f32[1,6,2,64,64]{4,3,2,1,0:T(8,128)}, u32[]{:S(2)}) copy-start(f32[1,6,2,64,64]{4,3,2,1,0:T(8,128)} %param.11) | copy-start | bytes 589828
  1.6 13.6 %copy-start.4 = (bf16[2048,128]{1,0:T(8,128)(2,1)S(1)}, bf16[2048,128]{1,0:T(8,128)(2,1)}, u32[]{:S(2)}) copy-start(bf16[2048,128]{1,0:T(8,128)(2,1)} %param.6) | copy-start | bytes 1572868
  3.1 12.4 %copy-start.5 = (bf16[2048,128]{1,0:T(8,128)(2,1)S(1)}, bf16[2048,128]{1,0:T(8,128)(2,1)}, u32[]{:S(2)}) copy-start(bf16[2048,128]{1,0:T(8,128)(2,1)} %param.7) | copy-start | bytes 1572868
  3.1 26.4 %all-to-all-start = ((f32[16,1,6144]{2,1,0:T(1,128)}), f32[16,1,6144]{2,1,0:T(1,128)S(1)}, u32[]{:S(2)}, u32[]{:S(2)}) async-start(f32[16,1,6144]{2,1,0:T(1,128)} %reshape.95), calls=%async_computation | async-start | bytes 786432 | tf_op jit(solution)/shard_map/all_to_all | solution.py:27
  15.7 17.6 %copy-start.2 = (bf16[2048,128]{0,1:T(8,128)(2,1)}, bf16[2048,128]{0,1:T(8,128)(2,1)S(1)}, u32[]{:S(2)}) copy-start(bf16[2048,128]{0,1:T(8,128)(2,1)S(1)} %copy.62) | copy-start | bytes 1572868
  94.1 1.6 copy-start
  97.5 0.8 copy-start.6
  151.7 3.0 %copy-start.1 = (bf16[2048,3,2,64]{0,3,2,1:T(8,128)(2,1)S(1)}, bf16[2048,3,2,64]{0,3,2,1:T(8,128)(2,1)}, u32[]{:S(2)}) copy-start(bf16[2048,3,2,64]{0,3,2,1:T(8,128)(2,1)} %reshape.79) | copy-start | bytes 4718596
  156.0 3.4 %copy-start.3 = (bf16[2048,128]{0,1:T(8,128)(2,1)S(1)}, bf16[2048,128]{0,1:T(8,128)(2,1)}, u32[]{:S(2)}) copy-start(bf16[2048,128]{0,1:T(8,128)(2,1)} %copy-done.2) | copy-start | bytes 1572868
  159.4 1.8 copy-start.10
  181.8 2.3 %copy-start.8 = (f32[6,2,4,64]{3,2,1,0:T(4,128)S(1)}, f32[6,2,4,64]{3,2,1,0:T(4,128)}, u32[]{:S(2)}) copy-start(f32[6,2,4,64]{3,2,1,0:T(4,128)} %param.8) | copy-start | bytes 36868
  181.8 2.3 %copy-start.9 = (f32[6,2,4,64]{3,2,1,0:T(4,128)S(1)}, f32[6,2,4,64]{3,2,1,0:T(4,128)}, u32[]{:S(2)}) copy-start(f32[6,2,4,64]{3,2,1,0:T(4,128)} %param.9) | copy-start | bytes 36868
  181.8 2.3 %copy-start.11 = (f32[6,2,4,64]{3,2,1,0:T(4,128)S(1)}, f32[6,2,4,64]{3,2,1,0:T(4,128)}, u32[]{:S(2)}) copy-start(f32[6,2,4,64]{3,2,1,0:T(4,128)} %param.10) | copy-start | bytes 36868

commit v4 on v1

--- a/solution.py
+++ b/solution.py
@@ -1,6 +1,8 @@
 import jax
 import jax.numpy as jnp
 from jax import lax
+from jax.experimental import pallas as pl
+from jax.experimental.pallas import tpu as pltpu
 from jax.sharding import PartitionSpec as P
 
 LAMBDA_SIZE = 100.0
@@ -39,6 +41,57 @@
     return summed
 
 
+TOKEN_BLOCK = 512
+
+
+def nt_dot(a, b):
+    return lax.dot_general(a, b, (((1,), (1,)), ((), ())), preferred_element_type=jnp.float32)
+
+
+def grads_kernel(x_ref, c_ref, first_ref, second_ref, h_ref, gl_ref, gr_ref, noise_ref, spread_ref,
+                 out_ref, acc_ref, *, scale):
+    step = pl.program_id(0)
+
+    @pl.when(step == 0)
+    def _():
+        acc_ref[...] = jnp.zeros_like(acc_ref)
+
+    for b in range(acc_ref.shape[1]):
+        pairs = (
+            (x_ref[b], second_ref[1, b]),
+            (first_ref[0, b], gl_ref[b]),
+            (x_ref[b], second_ref[2, b]),
+            (first_ref[1, b], gr_ref[b]),
+            (h_ref[b], first_ref[2, b]),
+            (second_ref[0, b], c_ref[b]),
+        )
+        for f, (lhs, rhs) in enumerate(pairs):
+            acc_ref[f, b] += nt_dot(lhs, rhs)
+
+    @pl.when(step == pl.num_programs(0) - 1)
+    def _():
+        grads = acc_ref[...] * scale
+        out_ref[0] = grads
+        out_ref[1] = grads * noise_ref[...] * spread_ref[...]
+
+
+def grads_and_curvature(x_t, c_t, first_t, second_t, h_t, gl_t, gr_t, noise, spread, scale):
+    nb, width, tokens = x_t.shape
+    tb = min(TOKEN_BLOCK, tokens)
+    act = pl.BlockSpec((nb, width, tb), lambda i: (0, 0, i))
+    trio = pl.BlockSpec((3, nb, width, tb), lambda i: (0, 0, 0, i))
+    whole = pl.BlockSpec(noise.shape, lambda i: (0, 0, 0, 0))
+    return pl.pallas_call(
+        lambda *refs: grads_kernel(*refs, scale=scale),
+        grid=(tokens // tb,),
+        in_specs=[act, act, trio, trio, act, act, act, whole, whole],
+        out_specs=pl.BlockSpec((2,) + noise.shape, lambda i: (0, 0, 0, 0, 0)),
+        out_shape=jax.ShapeDtypeStruct((2,) + noise.shape, jnp.float32),
+        scratch_shapes=[pltpu.VMEM(noise.shape, jnp.float32)],
+        compiler_params=pltpu.CompilerParams(dimension_semantics=("arbitrary",)),
+    )(x_t, c_t, first_t, second_t, h_t, gl_t, gr_t, noise, spread)
+
+
 def per_device(inputs, out_grad, mean_state, hess_state, grad_state, noise_draw):
     tokens = inputs.shape[0]
     local_blocks = mean_state.shape[1]
@@ -63,23 +116,20 @@
     u_right = bdot("tji,jic->tjc", perm_right, sampled[3])
     hidden = (jax.nn.silu(u_left) * u_right).astype(jnp.bfloat16)
     outer = bdot("tbr,brc->tcb", hidden, sampled[4]).astype(jnp.bfloat16)
-    grad_four = bdot("tbr,tbc->brc", hidden, back_hidden) * scale
     d_hidden = bdot("tbc,brc->tbr", back_hidden, sampled[4])
     gate_grad = (d_hidden * u_right * silu_slope(u_left)).astype(jnp.bfloat16)
     value_grad = (d_hidden * jax.nn.silu(u_left)).astype(jnp.bfloat16)
-    grad_one = bdot("tji,tjc->jic", perm_left, gate_grad) * scale
-    grad_three = bdot("tji,tjc->jic", perm_right, value_grad) * scale
     back_left = bdot("tjc,jic->tij", gate_grad, sampled[1]).astype(jnp.bfloat16)
     back_right = bdot("tjc,jic->tij", value_grad, sampled[3]).astype(jnp.bfloat16)
     second = lax.all_to_all(
         jnp.stack([outer, back_left, back_right], axis=1), "mp", split_axis=2, concat_axis=3, tiled=True
     )
-    mixed_rows, rows_left, rows_right = second[:, 0], second[:, 1], second[:, 2]
-    grad_five = bdot("tji,tjc->jic", mixed_rows, grad_rows) * scale
-    grad_zero = bdot("tbr,tbc->brc", in_rows, rows_left) * scale
-    grad_two = bdot("tbr,tbc->brc", in_rows, rows_right) * scale
-    all_grads = jnp.stack([grad_zero, grad_one, grad_two, grad_three, grad_four, grad_five])
-    sums = scatter_rows(jnp.stack([all_grads, all_grads * noise * spread]), groups)
+    token_minor = lambda a: jnp.moveaxis(a, 0, -1)
+    stacked = grads_and_curvature(
+        token_minor(in_rows), token_minor(grad_rows), token_minor(first), token_minor(second),
+        token_minor(hidden), token_minor(gate_grad), token_minor(value_grad), noise, spread, scale,
+    )
+    sums = scatter_rows(stacked, groups)
     grad_avg = sums[0] / groups
     hess_avg = sums[1] / groups
     new_grad = BETA_GRAD * grad_state + (1.0 - BETA_GRAD) * grad_avg

time: 177 us -> 169 us (0.955)
  blocking collectives: 138 us -> 96 us
  waiting for transfers between devices: 0 us -> 35 us
  matrix products: 14.9 us -> 5.09 us
  Pallas kernels: 0 us -> 5.4 us
  starting transfers between devices: 0 us -> 5.08 us
    all_to_all x1 -> x0, blocking collectives: 42.3 us -> none  [per_device(): lax.all_to_all(jnp.stack([outer, back_left, back_right], axis=1), 'mp', s...]
    all_to_all x0 -> x1, waiting for transfers between devices: none -> 35 us  [per_device(): lax.all_to_all(jnp.stack([outer, back_left, back_right], axis=1), 'mp', s...]
    dot_general x15 -> x9, matrix products: 14.9 us -> 5.09 us  [bdot(): return jnp.einsum(form, left, right, preferred_element_type=jnp.float32)]
    pallas_call x0 -> x1, Pallas kernels: none -> 5.4 us  [grads_and_curvature(): pl.pallas_call(lambda *refs: grads_kernel(*refs, scale=scale), grid=(toke...]
    all_to_all x0 -> x1, starting transfers between devices: none -> 5.08 us  [per_device(): lax.all_to_all(jnp.stack([outer, back_left, back_right], axis=1), 'mp', s...]
    unnamed x38 -> x28, local copies, waits for them, and re-layouts: 5.49 us -> 4.4 us
  transfers between devices with their start and end apart: 0 -> 1, of which waited for: 0 -> 1; matrix products, arithmetic and copies ran while one was open for 0% -> 1% of each run, Pallas kernels for 0% -> 0%
where the time goes in v4:
time: 169 us; the launch traced here: 168 us
  blocking collectives  96 us (57%)
  waiting for transfers between devices  35 us (21%)
  local copies, waits for them, and re-layouts  16.8 us (10%)
  Pallas kernels  5.4 us (3%)
  matrix products  5.09 us (3%)
  starting transfers between devices  5.08 us (3%)
  other arithmetic  3.82 us (2%)
    all_to_all x1, blocking collectives, per_device(): lax.all_to_all(jnp.stack([y_left, y_right, back_outer], axis=1), 'mp', sp...  48.9 us
    all_to_all x1, waiting for transfers between devices, per_device(): lax.all_to_all(jnp.stack([outer, back_left, back_right], axis=1), 'mp', s...  35 us
    all_gather x1, blocking collectives, gather_rows(): full = lax.all_gather(moved, 'dp', axis=0, tiled=True)  26.6 us
    all_to_all x1, blocking collectives, scatter_rows(): got = lax.all_to_all(split, 'dp', split_axis=0, concat_axis=0, tiled=True)  20.5 us
    pallas_call x1, Pallas kernels, grads_and_curvature(): pl.pallas_call(lambda *refs: grads_kernel(*refs, scale=scale), grid=(toke...  5.4 us
    dot_general x9, matrix products, bdot(): return jnp.einsum(form, left, right, preferred_element_type=jnp.float32)  5.09 us
    all_to_all x1, starting transfers between devices, per_device(): lax.all_to_all(jnp.stack([outer, back_left, back_right], axis=1), 'mp', s...  5.08 us
    unnamed x28, local copies, waits for them, and re-layouts  4.4 us
  transfers between devices with their start and end apart: 1, of which 1 were waited for; matrix products, arithmetic and copies ran while one was open for 1% of the time, Pallas kernels for 0%

profile of v4, /device:TPU:1, one launch (start us, length us, event | category | flops | bytes accessed | tf_op | source)
XLA Modules:
  0.0 168.1 jit_solution(15194288567637424233)
XLA Ops:
  0.6 0.0 copy-start.5
  0.6 1.3 copy.18
  1.9 0.0 copy-start.1
  2.0 0.9 copy_bitcast_fusion.4
  2.8 26.6 %all_gather.3 = f32[64,2,6,2,64]{4,3,2,1,0:T(2,128)S(1)} all-gather(f32[4,2,6,2,64]{4,3,2,1,0:T(2,128)S(1)} %maximum_bitcast_fusion), channel_id=1, replica_groups=mesh['dp'=16,'mp'=32] {'dp'}, dimensions={0}, use_global_device_ids=true | all-gather | bytes 417792 | tf_op jit(solution)/shard_map/all_gather | solution.py:28
  29.5 0.2 copy.47
  29.7 0.0 copy-start.2
  29.7 0.9 copy-done.2
  30.5 0.0 copy-done.5
  30.5 0.0 copy-start.8
  30.6 0.2 fusion.26
  30.7 0.0 copy-start.6
  30.7 0.3 fusion.1
  31.1 0.0 copy-done.1
  31.1 0.3 fusion
  31.4 0.2 copy-done.8
  31.6 0.2 copy.19
  31.8 0.0 copy-start.4
  31.8 0.0 copy-done.6
  31.8 0.3 fusion.2
  32.1 0.2 pad_maximum_fusion
  32.3 0.3 copy-done.4
  32.6 1.6 copy.25
  34.2 48.9 %all_to_all.41 = bf16[2048,3,64,2]{0,3,1,2:T(2,128)(2,1)S(1)} all-to-all(bf16[2048,3,64,2]{0,3,1,2:T(2,128)(2,1)S(1)} %copy.25), channel_id=1, replica_groups=mesh['dp'=16,'mp'=32] {'mp'}, dimensions={2} | all-to-all | bytes 3145728 | tf_op jit(solution)/shard_map/all_to_all | solution.py:111
  83.1 1.3 copy.45
  84.4 0.0 copy-start.7
  84.4 0.6 all_to_all.32
  85.0 0.3 copy-done.7
  85.3 0.0 copy-start
  85.3 0.3 fusion.20
  85.6 0.3 fusion.19
  86.0 0.5 fusion.3
  86.5 0.0 copy-done
  86.5 1.8 %multiply_convert_fusion = (bf16[2,64,2048]{2,1,0:T(8,128)(2,1)}, bf16[2,64,2048]{2,1,0:T(8,128)(2,1)}, bf16[2,64,2048]{2,1,0:T(8,128)(2,1)}, f32[2,64,2048]{2,1,0:T(8,128)S(1)}) fusion(f32[2,64,2048]{2,1,0:T(8,128)S(1)} %fusion.20, f32[2,64,2048]{2,1,0:T(8,128)S(1)} %fusion.19, bf16[2048,3,2,64]{0,3,2,1:T(8,128)(2,1)S(1)} %all_to_all.32, ...), kind=kOutput, calls=%fused_computation.31 | convolution fusion | flops 37486592 | bytes 5275648 | tf_op jit(solution)/shard_map/tbc,brc->tbr/dot_general | solution.py:18
  88.3 0.6 fusion.4
  89.0 0.5 fusion.5
  89.5 0.2 pad_maximum_fusion.1
  89.6 2.8 %copy.30 = bf16[2048,3,64,2]{0,3,1,2:T(2,128)(2,1)} copy(bf16[2048,3,64,2]{0,2,3,1:T(8,128)(2,1)S(1)} %pad_maximum_fusion.1) | data formatting | bytes 3145728 | tf_op jit(solution)/shard_map/stack | solution.py:125
  92.4 0.0 copy-start.3
  92.4 5.1 %all-to-all-start.1 = ((bf16[2048,3,64,2]{0,3,1,2:T(2,128)(2,1)}), bf16[2048,3,64,2]{0,3,1,2:T(2,128)(2,1)S(1)}, u32[]{:S(2)}, u32[]{:S(2)}) async-start(bf16[2048,3,64,2]{0,3,1,2:T(2,128)(2,1)} %copy.30), calls=%async_computation.1 | async-start | bytes 3145728 | tf_op jit(solution)/shard_map/all_to_all | solution.py:124
  97.5 0.0 copy-done.3
  97.5 0.9 fusion.24.refs_8_
  98.4 35.0 %all-to-all-done.1 = bf16[2048,3,64,2]{0,3,1,2:T(2,128)(2,1)S(1)} async-done(((bf16[2048,3,64,2]{0,3,1,2:T(2,128)(2,1)}), bf16[2048,3,64,2]{0,3,1,2:T(2,128)(2,1)S(1)}, u32[]{:S(2)}, u32[]{:S(2)}) %all-to-all-start.1) | async-done | bytes 1572896 | tf_op jit(solution)/shard_map/all_to_all | solution.py:124
  133.4 1.3 copy.44
  134.7 2.0 %all_to_all.36 = bf16[2048,3,2,64]{0,3,2,1:T(8,128)(2,1)} reshape(bf16[2048,3,2,32,2]{0,4,3,2,1:T(2,128)(2,1)S(1)} %bitcast.180) | data formatting | bytes 3145728 | tf_op jit(solution)/shard_map/all_to_all | solution.py:124
  136.7 5.4 %shard_map.85 = f32[2,6,2,64,64]{4,3,2,1,0:T(8,128)} custom-call(bf16[2,64,2048]{2,1,0:T(8,128)(2,1)} %bitcast.175, bf16[2,64,2048]{2,1,0:T(8,128)(2,1)} %bitcast.184, bf16[3,2,64,2048]{3,2,1,0:T(8,128)(2,1)} %bitcast.172, bf16[3,2,64,2048]{3,2,1,0:T(8,128)(2,1)} %bitcast.177, bf16[2,64,2048]{2,1,0:T(8,128)(2,1)} %get-tuple-element.8.refs_4_, ...), custom_call_target="tpu_custom_call" | custom-call | tf_op jit(solution)/shard_map/pallas_call | solution.py:84
  142.1 1.3 copy.46
  143.4 0.7 reshape.29
  144.2 20.5 %all_to_all.42 = f32[16,1,6144]{2,1,0:T(1,128)S(1)} all-to-all(f32[16,1,6144]{2,1,0:T(1,128)S(1)} %reshape.29), channel_id=1, replica_groups=mesh['dp'=16,'mp'=32] {'dp'}, dimensions={0} | all-to-all | bytes 786432 | tf_op jit(solution)/shard_map/all_to_all | solution.py:37
  164.6 0.0 copy-start.9
  164.6 0.0 copy-start.10
  164.6 0.0 copy-start.11
  164.6 0.5 broadcast.42
  165.2 1.6 reduce
  166.7 0.5 reshape.30
  167.3 0.2 reduce_sum.9
  167.4 0.0 copy-done.9
  167.4 0.0 copy-done.10
  167.4 0.0 copy-done.11
  167.5 0.7 divide_subtract_fusion
  (1 shorter events, 0.0 us)
Async XLA Ops:
  0.6 29.9 %copy-start.5 = (f32[1,6,2,64,64]{4,3,2,1,0:T(8,128)S(1)}, f32[1,6,2,64,64]{4,3,2,1,0:T(8,128)}, u32[]{:S(2)}) copy-start(f32[1,6,2,64,64]{4,3,2,1,0:T(8,128)} %param.11) | copy-start | bytes 589828
  1.9 29.1 %copy-start.1 = (bf16[2048,128]{0,1:T(8,128)(2,1)}, bf16[2048,128]{0,1:T(8,128)(2,1)S(1)}, u32[]{:S(2)}) copy-start(bf16[2048,128]{0,1:T(8,128)(2,1)S(1)} %copy.18) | copy-start | bytes 1572868
  29.7 0.9 copy-start.2
  30.5 1.0 copy-start.8
  30.7 1.1 copy-start.6
  31.8 0.8 copy-start.4
  84.4 0.9 copy-start.7
  85.3 1.2 copy-start
  92.4 5.1 %copy-start.3 = (f32[64,2,6,2,64]{4,0,3,2,1:T(8,128)S(1)}, f32[64,2,6,2,64]{4,0,3,2,1:T(8,128)}, u32[]{:S(2)}) copy-start(f32[64,2,6,2,64]{4,0,3,2,1:T(8,128)} %copy-done.2) | copy-start | bytes 1179652
  92.4 41.0 %all-to-all-start.1 = ((bf16[2048,3,64,2]{0,3,1,2:T(2,128)(2,1)}), bf16[2048,3,64,2]{0,3,1,2:T(2,128)(2,1)S(1)}, u32[]{:S(2)}, u32[]{:S(2)}) async-start(bf16[2048,3,64,2]{0,3,1,2:T(2,128)(2,1)} %copy.30), calls=%async_computation.1 | async-start | bytes 3145728 | tf_op jit(solution)/shard_map/all_to_all | solution.py:124
  164.6 2.8 %copy-start.9 = (f32[6,2,4,64]{3,2,1,0:T(4,128)S(1)}, f32[6,2,4,64]{3,2,1,0:T(4,128)}, u32[]{:S(2)}) copy-start(f32[6,2,4,64]{3,2,1,0:T(4,128)} %param.8) | copy-start | bytes 36868
  164.6 2.8 %copy-start.10 = (f32[6,2,4,64]{3,2,1,0:T(4,128)S(1)}, f32[6,2,4,64]{3,2,1,0:T(4,128)}, u32[]{:S(2)}) copy-start(f32[6,2,4,64]{3,2,1,0:T(4,128)} %param.9) | copy-start | bytes 36868
  164.6 2.8 %copy-start.11 = (f32[6,2,4,64]{3,2,1,0:T(4,128)S(1)}, f32[6,2,4,64]{3,2,1,0:T(4,128)}, u32[]{:S(2)}) copy-start(f32[6,2,4,64]{3,2,1,0:T(4,128)} %param.10) | copy-start | bytes 36868

commit v5 on v4

--- a/solution.py
+++ b/solution.py
@@ -41,44 +41,52 @@
     return summed
 
 
-TOKEN_BLOCK = 512
+TOKEN_BLOCK = 1024
 
 
-def nt_dot(a, b):
-    return lax.dot_general(a, b, (((1,), (1,)), ((), ())), preferred_element_type=jnp.float32)
+def nn_dot(a, b):
+    return lax.dot_general(a, b, (((1,), (0,)), ((), ())), preferred_element_type=jnp.float32)
 
 
 def grads_kernel(x_ref, c_ref, first_ref, second_ref, h_ref, gl_ref, gr_ref, noise_ref, spread_ref,
                  out_ref, acc_ref, *, scale):
     step = pl.program_id(0)
+    nb, width = acc_ref.shape[1], acc_ref.shape[2]
 
     @pl.when(step == 0)
     def _():
         acc_ref[...] = jnp.zeros_like(acc_ref)
 
-    for b in range(acc_ref.shape[1]):
+    for b in range(nb):
+        cols = slice(b * width, (b + 1) * width)
         pairs = (
-            (x_ref[b], second_ref[1, b]),
-            (first_ref[0, b], gl_ref[b]),
-            (x_ref[b], second_ref[2, b]),
-            (first_ref[1, b], gr_ref[b]),
-            (h_ref[b], first_ref[2, b]),
-            (second_ref[0, b], c_ref[b]),
+            (second_ref[1, b], x_ref[:, cols]),
+            (first_ref[0, b], gl_ref[:, cols]),
+            (second_ref[2, b], x_ref[:, cols]),
+            (first_ref[1, b], gr_ref[:, cols]),
+            (first_ref[2, b], h_ref[:, cols]),
+            (second_ref[0, b], c_ref[:, cols]),
         )
         for f, (lhs, rhs) in enumerate(pairs):
-            acc_ref[f, b] += nt_dot(lhs, rhs)
+            acc_ref[f, b] += nn_dot(lhs, rhs)
 
     @pl.when(step == pl.num_programs(0) - 1)
     def _():
-        grads = acc_ref[...] * scale
-        out_ref[0] = grads
-        out_ref[1] = grads * noise_ref[...] * spread_ref[...]
+        for f in range(acc_ref.shape[0]):
+            for b in range(nb):
+                grad = acc_ref[f, b]
+                if f in (0, 2, 4):
+                    grad = grad.T
+                grad = grad * scale
+                out_ref[0, f, b] = grad
+                out_ref[1, f, b] = grad * noise_ref[f, b] * spread_ref[f, b]
 
 
-def grads_and_curvature(x_t, c_t, first_t, second_t, h_t, gl_t, gr_t, noise, spread, scale):
-    nb, width, tokens = x_t.shape
+def grads_and_curvature(x, c, first_t, second_t, h, gl, gr, noise, spread, scale):
+    tokens, feats = x.shape
+    nb, width = first_t.shape[1], first_t.shape[2]
     tb = min(TOKEN_BLOCK, tokens)
-    act = pl.BlockSpec((nb, width, tb), lambda i: (0, 0, i))
+    act = pl.BlockSpec((tb, feats), lambda i: (i, 0))
     trio = pl.BlockSpec((3, nb, width, tb), lambda i: (0, 0, 0, i))
     whole = pl.BlockSpec(noise.shape, lambda i: (0, 0, 0, 0))
     return pl.pallas_call(
@@ -89,7 +97,7 @@
         out_shape=jax.ShapeDtypeStruct((2,) + noise.shape, jnp.float32),
         scratch_shapes=[pltpu.VMEM(noise.shape, jnp.float32)],
         compiler_params=pltpu.CompilerParams(dimension_semantics=("arbitrary",)),
-    )(x_t, c_t, first_t, second_t, h_t, gl_t, gr_t, noise, spread)
+    )(x, c, first_t, second_t, h, gl, gr, noise, spread)
 
 
 def per_device(inputs, out_grad, mean_state, hess_state, grad_state, noise_draw):
@@ -125,9 +133,10 @@
         jnp.stack([outer, back_left, back_right], axis=1), "mp", split_axis=2, concat_axis=3, tiled=True
     )
     token_minor = lambda a: jnp.moveaxis(a, 0, -1)
+    flat = lambda a: a.reshape(tokens, -1)
     stacked = grads_and_curvature(
-        token_minor(in_rows), token_minor(grad_rows), token_minor(first), token_minor(second),
-        token_minor(hidden), token_minor(gate_grad), token_minor(value_grad), noise, spread, scale,
+        inputs, out_grad, token_minor(first), token_minor(second),
+        flat(hidden), flat(gate_grad), flat(value_grad), noise, spread, scale,
     )
     sums = scatter_rows(stacked, groups)
     grad_avg = sums[0] / groups

time: 169 us -> 167 us (0.988)
  waiting for transfers between devices: 35 us -> 30.9 us
  local copies, waits for them, and re-layouts: 16.8 us -> 20.7 us
    all_to_all x1, waiting for transfers between devices: 35 us -> 30.9 us  [per_device(): lax.all_to_all(jnp.stack([outer, back_left, back_right], axis=1), 'mp', s...]
    reshape x0 -> x3, local copies, waits for them, and re-layouts: none -> 4.04 us  [per_device(): flat = lambda a: a.reshape(tokens, -1)]
    unnamed x28 -> x26, local copies, waits for them, and re-layouts: 4.4 us -> 4.32 us
  transfers between devices with their start and end apart: 1 -> 1, of which waited for: 1 -> 1; matrix products, arithmetic and copies ran while one was open for 1% -> 3% of each run, Pallas kernels for 0% -> 0%
where the time goes in v5:
time: 167 us; the launch traced here: 166 us
  blocking collectives  96 us (57%)
  waiting for transfers between devices  30.9 us (19%)
  local copies, waits for them, and re-layouts  20.7 us (12%)
  starting transfers between devices  5.08 us (3%)
  Pallas kernels  4.75 us (3%)
  matrix products  4 us (2%)
  other arithmetic  3.83 us (2%)
    all_to_all x1, blocking collectives, per_device(): lax.all_to_all(jnp.stack([y_left, y_right, back_outer], axis=1), 'mp', sp...  48.9 us
    all_to_all x1, waiting for transfers between devices, per_device(): lax.all_to_all(jnp.stack([outer, back_left, back_right], axis=1), 'mp', s...  30.9 us
    all_gather x1, blocking collectives, gather_rows(): full = lax.all_gather(moved, 'dp', axis=0, tiled=True)  26.6 us
    all_to_all x1, blocking collectives, scatter_rows(): got = lax.all_to_all(split, 'dp', split_axis=0, concat_axis=0, tiled=True)  20.5 us
    all_to_all x1, starting transfers between devices, per_device(): lax.all_to_all(jnp.stack([outer, back_left, back_right], axis=1), 'mp', s...  5.08 us
    pallas_call x1, Pallas kernels, grads_and_curvature(): pl.pallas_call(lambda *refs: grads_kernel(*refs, scale=scale), grid=(toke...  4.75 us
    unnamed x26, local copies, waits for them, and re-layouts  4.32 us
    reshape x3, local copies, waits for them, and re-layouts, per_device(): flat = lambda a: a.reshape(tokens, -1)  4.04 us
  transfers between devices with their start and end apart: 1, of which 1 were waited for; matrix products, arithmetic and copies ran while one was open for 3% of the time, Pallas kernels for 0%

profile of v5, /device:TPU:1, one launch (start us, length us, event | category | flops | bytes accessed | tf_op | source)
XLA Modules:
  0.0 166.2 jit_solution(910144270058319476)
XLA Ops:
  0.6 0.0 copy-start.5
  0.6 1.3 copy.37
  1.9 0.8 copy_bitcast_fusion.4
  2.8 26.6 %all_gather.3 = f32[64,2,6,2,64]{4,3,2,1,0:T(2,128)S(1)} all-gather(f32[4,2,6,2,64]{4,3,2,1,0:T(2,128)S(1)} %maximum_bitcast_fusion), channel_id=1, replica_groups=mesh['dp'=16,'mp'=32] {'dp'}, dimensions={0}, use_global_device_ids=true | all-gather | bytes 417792 | tf_op jit(solution)/shard_map/all_gather | solution.py:28
  29.4 0.2 copy.66
  29.6 0.0 copy-start.1
  29.6 0.9 copy-done.1
  30.5 0.0 copy-done.5
  30.5 0.0 copy-start.3
  30.5 0.2 fusion.11
  30.6 0.0 copy-start.6
  30.7 0.3 fusion.1
  31.0 0.3 fusion
  31.4 0.1 copy-done.3
  31.5 0.2 copy.40
  31.7 0.3 fusion.2
  32.0 0.2 pad_maximum_fusion
  32.2 1.6 copy.41
  33.8 48.9 %all_to_all.41 = bf16[2048,3,64,2]{0,3,1,2:T(2,128)(2,1)S(1)} all-to-all(bf16[2048,3,64,2]{0,3,1,2:T(2,128)(2,1)S(1)} %copy.41), channel_id=1, replica_groups=mesh['dp'=16,'mp'=32] {'mp'}, dimensions={2} | all-to-all | bytes 3145728 | tf_op jit(solution)/shard_map/all_to_all | solution.py:119
  82.7 1.3 copy.64
  84.0 0.6 all_to_all.32
  84.6 0.0 copy-start
  84.6 0.3 convolution_bitcast_fusion
  84.9 0.0 copy-done.6
  84.9 0.3 convolution_bitcast_fusion.2
  85.3 0.5 copy-done
  85.8 0.0 copy-start.7
  85.8 1.5 multiply_convert_fusion.2
  87.3 0.0 copy-start.4
  87.3 0.0 copy-done.7
  87.3 0.3 fusion.3
  87.7 0.3 fusion.4
  87.9 0.3 fusion.5
  88.2 0.2 pad_maximum_fusion.1
  88.4 0.0 copy-done.4
  88.4 2.8 %copy.46 = bf16[2048,3,64,2]{0,3,1,2:T(2,128)(2,1)} copy(bf16[2048,3,64,2]{0,2,3,1:T(8,128)(2,1)S(1)} %pad_maximum_fusion.1) | data formatting | bytes 3145728 | tf_op jit(solution)/shard_map/stack | solution.py:133
  91.2 0.0 copy-start.2
  91.2 5.1 %all-to-all-start.1 = ((bf16[2048,3,64,2]{0,3,1,2:T(2,128)(2,1)}), bf16[2048,3,64,2]{0,3,1,2:T(2,128)(2,1)S(1)}, u32[]{:S(2)}, u32[]{:S(2)}) async-start(bf16[2048,3,64,2]{0,3,1,2:T(2,128)(2,1)} %copy.46), calls=%async_computation.1 | async-start | bytes 3145728 | tf_op jit(solution)/shard_map/all_to_all | solution.py:132
  96.3 0.0 copy-done.2
  96.3 0.9 fusion.9.refs_8_
  97.2 2.0 %copy.50.refs_6_ = bf16[2048,128]{1,0:T(8,128)(2,1)} copy(bf16[2048,128]{0,1:T(8,128)(2,1)} %bitcast.149) | data formatting | bytes 1048576 | tf_op jit(solution)/shard_map/reshape | solution.py:136
  99.2 1.0 copy.49.refs_5_
  100.2 1.0 copy.48.refs_4_
  101.2 30.9 %all-to-all-done.1 = bf16[2048,3,64,2]{0,3,1,2:T(2,128)(2,1)S(1)} async-done(((bf16[2048,3,64,2]{0,3,1,2:T(2,128)(2,1)}), bf16[2048,3,64,2]{0,3,1,2:T(2,128)(2,1)S(1)}, u32[]{:S(2)}, u32[]{:S(2)}) %all-to-all-start.1) | async-done | bytes 1572896 | tf_op jit(solution)/shard_map/all_to_all | solution.py:132
  132.2 1.3 copy.63
  133.4 2.0 %all_to_all.36 = bf16[2048,3,2,64]{0,3,2,1:T(8,128)(2,1)} reshape(bf16[2048,3,2,32,2]{0,4,3,2,1:T(2,128)(2,1)S(1)} %bitcast.140) | data formatting | bytes 3145728 | tf_op jit(solution)/shard_map/all_to_all | solution.py:132
  135.4 4.8 %shard_map.85 = f32[2,6,2,64,64]{4,3,2,1,0:T(8,128)} custom-call(bf16[2048,128]{1,0:T(8,128)(2,1)} %refs_0_.1, bf16[2048,128]{1,0:T(8,128)(2,1)} %refs_1_.1, bf16[3,2,64,2048]{3,2,1,0:T(8,128)(2,1)} %bitcast.135, bf16[3,2,64,2048]{3,2,1,0:T(8,128)(2,1)} %bitcast.137, bf16[2048,128]{1,0:T(8,128)(2,1)} %copy.48.refs_4_, bf16[2048,128]{1,0:T(8,128)(2,1)} %copy.49.refs_5_, ...), custom_call_target="tpu_custom_call" | custom-call | tf_op jit(solution)/shard_map/pallas_call | solution.py:92
  140.2 1.3 copy.65
  141.5 0.7 reshape.41
  142.3 20.5 %all_to_all.42 = f32[16,1,6144]{2,1,0:T(1,128)S(1)} all-to-all(f32[16,1,6144]{2,1,0:T(1,128)S(1)} %reshape.41), channel_id=1, replica_groups=mesh['dp'=16,'mp'=32] {'dp'}, dimensions={0} | all-to-all | bytes 786432 | tf_op jit(solution)/shard_map/all_to_all | solution.py:37
  162.8 0.0 copy-start.8
  162.8 0.0 copy-start.9
  162.8 0.0 copy-start.10
  162.8 0.5 broadcast.39
  163.3 1.6 reduce
  164.9 0.5 reshape.42
  165.4 0.2 reduce_sum.9
  165.5 0.0 copy-done.8
  165.6 0.0 copy-done.9
  165.6 0.0 copy-done.10
  165.6 0.7 divide_subtract_fusion
  (1 shorter events, 0.0 us)
Async XLA Ops:
  0.6 29.8 %copy-start.5 = (f32[1,6,2,64,64]{4,3,2,1,0:T(8,128)S(1)}, f32[1,6,2,64,64]{4,3,2,1,0:T(8,128)}, u32[]{:S(2)}) copy-start(f32[1,6,2,64,64]{4,3,2,1,0:T(8,128)} %param.11) | copy-start | bytes 589828
  29.6 0.9 copy-start.1
  30.5 1.0 copy-start.3
  30.6 54.3 %copy-start.6 = (bf16[6,2,64,64]{3,2,1,0:T(8,128)(2,1)}, bf16[6,2,64,64]{3,2,1,0:T(8,128)(2,1)S(1)}, u32[]{:S(2)}) copy-start(bf16[6,2,64,64]{3,2,1,0:T(8,128)(2,1)S(1)} %fusion.11) | copy-start | bytes 294916
  84.6 1.2 copy-start
  85.8 1.5 copy-start.7
  87.3 1.1 copy-start.4
  91.2 5.1 %copy-start.2 = (f32[64,2,6,2,64]{4,0,3,2,1:T(8,128)S(1)}, f32[64,2,6,2,64]{4,0,3,2,1:T(8,128)}, u32[]{:S(2)}) copy-start(f32[64,2,6,2,64]{4,0,3,2,1:T(8,128)} %copy-done.1) | copy-start | bytes 1179652
  91.2 41.0 %all-to-all-start.1 = ((bf16[2048,3,64,2]{0,3,1,2:T(2,128)(2,1)}), bf16[2048,3,64,2]{0,3,1,2:T(2,128)(2,1)S(1)}, u32[]{:S(2)}, u32[]{:S(2)}) async-start(bf16[2048,3,64,2]{0,3,1,2:T(2,128)(2,1)} %copy.46), calls=%async_computation.1 | async-start | bytes 3145728 | tf_op jit(solution)/shard_map/all_to_all | solution.py:132
  162.8 2.8 %copy-start.8 = (f32[6,2,4,64]{3,2,1,0:T(4,128)S(1)}, f32[6,2,4,64]{3,2,1,0:T(4,128)}, u32[]{:S(2)}) copy-start(f32[6,2,4,64]{3,2,1,0:T(4,128)} %param.8) | copy-start | bytes 36868
  162.8 2.8 %copy-start.9 = (f32[6,2,4,64]{3,2,1,0:T(4,128)S(1)}, f32[6,2,4,64]{3,2,1,0:T(4,128)}, u32[]{:S(2)}) copy-start(f32[6,2,4,64]{3,2,1,0:T(4,128)} %param.9) | copy-start | bytes 36868
  162.8 2.8 %copy-start.10 = (f32[6,2,4,64]{3,2,1,0:T(4,128)S(1)}, f32[6,2,4,64]{3,2,1,0:T(4,128)}, u32[]{:S(2)}) copy-start(f32[6,2,4,64]{3,2,1,0:T(4,128)} %param.10) | copy-start | bytes 36868

commit v6 on v5

--- a/solution.py
+++ b/solution.py
@@ -48,8 +48,7 @@
     return lax.dot_general(a, b, (((1,), (0,)), ((), ())), preferred_element_type=jnp.float32)
 
 
-def grads_kernel(x_ref, c_ref, first_ref, second_ref, h_ref, gl_ref, gr_ref, noise_ref, spread_ref,
-                 out_ref, acc_ref, *, scale):
+def grads_kernel(minor_ref, major_ref, noise_ref, spread_ref, out_ref, acc_ref, *, scale, pairs, flips):
     step = pl.program_id(0)
     nb, width = acc_ref.shape[1], acc_ref.shape[2]
 
@@ -59,45 +58,41 @@
 
     for b in range(nb):
         cols = slice(b * width, (b + 1) * width)
-        pairs = (
-            (second_ref[1, b], x_ref[:, cols]),
-            (first_ref[0, b], gl_ref[:, cols]),
-            (second_ref[2, b], x_ref[:, cols]),
-            (first_ref[1, b], gr_ref[:, cols]),
-            (first_ref[2, b], h_ref[:, cols]),
-            (second_ref[0, b], c_ref[:, cols]),
-        )
         for f, (lhs, rhs) in enumerate(pairs):
-            acc_ref[f, b] += nn_dot(lhs, rhs)
+            acc_ref[f, b] += nn_dot(minor_ref[lhs, b], major_ref[rhs, :, cols])
 
     @pl.when(step == pl.num_programs(0) - 1)
     def _():
         for f in range(acc_ref.shape[0]):
             for b in range(nb):
                 grad = acc_ref[f, b]
-                if f in (0, 2, 4):
+                if flips[f]:
                     grad = grad.T
                 grad = grad * scale
                 out_ref[0, f, b] = grad
                 out_ref[1, f, b] = grad * noise_ref[f, b] * spread_ref[f, b]
 
 
-def grads_and_curvature(x, c, first_t, second_t, h, gl, gr, noise, spread, scale):
-    tokens, feats = x.shape
-    nb, width = first_t.shape[1], first_t.shape[2]
+def grads_and_curvature(minor, major, noise, spread, scale, pairs, flips):
+    n_minor, nb, width, tokens = minor.shape
+    n_major, feats = major.shape[0], major.shape[2]
     tb = min(TOKEN_BLOCK, tokens)
-    act = pl.BlockSpec((tb, feats), lambda i: (i, 0))
-    trio = pl.BlockSpec((3, nb, width, tb), lambda i: (0, 0, 0, i))
-    whole = pl.BlockSpec(noise.shape, lambda i: (0, 0, 0, 0))
+    shape = (len(pairs), nb, width, width)
+    whole = pl.BlockSpec(shape, lambda i: (0, 0, 0, 0))
     return pl.pallas_call(
-        lambda *refs: grads_kernel(*refs, scale=scale),
+        lambda *refs: grads_kernel(*refs, scale=scale, pairs=pairs, flips=flips),
         grid=(tokens // tb,),
-        in_specs=[act, act, trio, trio, act, act, act, whole, whole],
-        out_specs=pl.BlockSpec((2,) + noise.shape, lambda i: (0, 0, 0, 0, 0)),
-        out_shape=jax.ShapeDtypeStruct((2,) + noise.shape, jnp.float32),
-        scratch_shapes=[pltpu.VMEM(noise.shape, jnp.float32)],
+        in_specs=[
+            pl.BlockSpec((n_minor, nb, width, tb), lambda i: (0, 0, 0, i)),
+            pl.BlockSpec((n_major, tb, feats), lambda i: (0, i, 0)),
+            whole,
+            whole,
+        ],
+        out_specs=pl.BlockSpec((2,) + shape, lambda i: (0, 0, 0, 0, 0)),
+        out_shape=jax.ShapeDtypeStruct((2,) + shape, jnp.float32),
+        scratch_shapes=[pltpu.VMEM(shape, jnp.float32)],
         compiler_params=pltpu.CompilerParams(dimension_semantics=("arbitrary",)),
-    )(x, c, first_t, second_t, h, gl, gr, noise, spread)
+    )(minor, major, noise, spread)
 
 
 def per_device(inputs, out_grad, mean_state, hess_state, grad_state, noise_draw):
@@ -129,16 +124,25 @@
     value_grad = (d_hidden * jax.nn.silu(u_left)).astype(jnp.bfloat16)
     back_left = bdot("tjc,jic->tij", gate_grad, sampled[1]).astype(jnp.bfloat16)
     back_right = bdot("tjc,jic->tij", value_grad, sampled[3]).astype(jnp.bfloat16)
+    token_minor = lambda a: jnp.moveaxis(a, 0, -1)
+    flat = lambda a: a.reshape(tokens, -1)
+    early = grads_and_curvature(
+        token_minor(first), jnp.stack([flat(gate_grad), flat(value_grad), flat(hidden)]),
+        noise[jnp.array([1, 3, 4])], spread[jnp.array([1, 3, 4])], scale,
+        pairs=((0, 0), (1, 1), (2, 2)), flips=(False, False, True),
+    )
+    early_sums = scatter_rows(early, groups)
     second = lax.all_to_all(
         jnp.stack([outer, back_left, back_right], axis=1), "mp", split_axis=2, concat_axis=3, tiled=True
     )
-    token_minor = lambda a: jnp.moveaxis(a, 0, -1)
-    flat = lambda a: a.reshape(tokens, -1)
-    stacked = grads_and_curvature(
-        inputs, out_grad, token_minor(first), token_minor(second),
-        flat(hidden), flat(gate_grad), flat(value_grad), noise, spread, scale,
+    late = grads_and_curvature(
+        token_minor(second), jnp.stack([inputs, out_grad]),
+        noise[jnp.array([0, 2, 5])], spread[jnp.array([0, 2, 5])], scale,
+        pairs=((1, 0), (2, 0), (0, 1)), flips=(True, True, False),
     )
-    sums = scatter_rows(stacked, groups)
+    late_sums = scatter_rows(late, groups)
+    order = jnp.array([0, 3, 1, 4, 5, 2])
+    sums = jnp.concatenate([late_sums, early_sums], axis=1)[:, order]
     grad_avg = sums[0] / groups
     hess_avg = sums[1] / groups
     new_grad = BETA_GRAD * grad_state + (1.0 - BETA_GRAD) * grad_avg

time: 167 us -> 171 us (1.024)
  blocking collectives: 96 us -> 75.6 us
  starting transfers between devices: 5.08 us -> 19.7 us
  local copies, waits for them, and re-layouts: 20.7 us -> 28.7 us
  other arithmetic: 3.83 us -> 9.68 us
  waiting for transfers between devices: 30.9 us -> 25.5 us
  Pallas kernels: 4.75 us -> 6.54 us
    all_to_all x1 -> x0, blocking collectives: 20.5 us -> none  [scatter_rows(): got = lax.all_to_all(split, 'dp', split_axis=0, concat_axis=0, tiled=True)]
    all_to_all x0 -> x2, starting transfers between devices: none -> 14.7 us  [scatter_rows(): got = lax.all_to_all(split, 'dp', split_axis=0, concat_axis=0, tiled=True)]
    all_to_all x1, waiting for transfers between devices: 30.9 us -> 18.3 us  [per_device(): lax.all_to_all(jnp.stack([outer, back_left, back_right], axis=1), 'mp', s...]
    all_to_all x0 -> x2, waiting for transfers between devices: none -> 7.24 us  [scatter_rows(): got = lax.all_to_all(split, 'dp', split_axis=0, concat_axis=0, tiled=True)]
    gather x0 -> x5, local copies, waits for them, and re-layouts: none -> 6.54 us  [the longest x1 2.25 us: per_device(): noise[jnp.array([1, 3, 4])]]
    another operation x0 -> x3, other arithmetic: none -> 4.25 us  [the longest x1 2.37 us: per_device(): jnp.stack([flat(gate_grad), flat(value_grad), flat(hidden)])]
    reshape x3 -> x0, local copies, waits for them, and re-layouts: 4.04 us -> none  [per_device(): flat = lambda a: a.reshape(tokens, -1)]
    another operation x0 -> x3, local copies, waits for them, and re-layouts: none -> 2.28 us  [per_device(): jnp.stack([flat(gate_grad), flat(value_grad), flat(hidden)])]
  transfers between devices with their start and end apart: 1 -> 3, of which waited for: 1 -> 2; matrix products, arithmetic and copies ran while one was open for 3% -> 14% of each run, Pallas kernels for 0% -> 4%
where the time goes in v6:
time: 171 us; the launch traced here: 170 us
  blocking collectives  75.6 us (44%)
  local copies, waits for them, and re-layouts  28.7 us (17%)
  waiting for transfers between devices  25.5 us (15%)
  starting transfers between devices  19.7 us (12%)
  other arithmetic  9.68 us (6%)
  Pallas kernels  6.54 us (4%)
  matrix products  3.17 us (2%)
    all_to_all x1, blocking collectives, per_device(): lax.all_to_all(jnp.stack([y_left, y_right, back_outer], axis=1), 'mp', sp...  48.9 us
    all_gather x1, blocking collectives, gather_rows(): full = lax.all_gather(moved, 'dp', axis=0, tiled=True)  26.8 us
    all_to_all x1, waiting for transfers between devices, per_device(): lax.all_to_all(jnp.stack([outer, back_left, back_right], axis=1), 'mp', s...  18.3 us
    all_to_all x2, starting transfers between devices, scatter_rows(): got = lax.all_to_all(split, 'dp', split_axis=0, concat_axis=0, tiled=True)  14.7 us
    all_to_all x2, waiting for transfers between devices, scatter_rows(): got = lax.all_to_all(split, 'dp', split_axis=0, concat_axis=0, tiled=True)  7.24 us
    pallas_call x2, Pallas kernels, grads_and_curvature(): pl.pallas_call(lambda *refs: grads_kernel(*refs, scale=scale, pairs=pairs...  6.54 us
    all_to_all x1, starting transfers between devices, per_device(): lax.all_to_all(jnp.stack([outer, back_left, back_right], axis=1), 'mp', s...  5.08 us
    unnamed x43, local copies, waits for them, and re-layouts  5.07 us
  transfers between devices with their start and end apart: 3, of which 2 were waited for; matrix products, arithmetic and copies ran while one was open for 14% of the time, Pallas kernels for 4%

profile of v6, /device:TPU:1, one launch (start us, length us, event | category | flops | bytes accessed | tf_op | source)
XLA Modules:
  0.0 170.1 jit_solution(2000393988306884358)
XLA Ops:
  0.6 0.0 copy-start.10
  0.6 0.8 pad_maximum_fusion.4
  1.5 0.0 copy-start.7
  1.5 26.8 %all_gather.3 = f32[64,2,6,2,64]{4,3,2,1,0:T(2,128)S(1)} all-gather(f32[4,2,6,2,64]{4,3,2,1,0:T(2,128)S(1)} %bitcast.173), channel_id=1, replica_groups=mesh['dp'=16,'mp'=32] {'dp'}, dimensions={0}, use_global_device_ids=true | all-gather | bytes 417792 | tf_op jit(solution)/shard_map/all_gather | solution.py:28
  28.3 0.4 copy.50
  28.8 0.2 copy.51
  28.9 0.2 copy.52
  29.1 0.0 copy-start.5
  29.2 0.2 fusion.11
  29.3 0.3 copy-done.1
  29.6 0.3 fusion
  29.9 0.3 fusion.1
  30.2 0.2 copy.53
  30.4 0.3 fusion.2
  30.8 0.2 pad_maximum_fusion
  31.0 1.6 copy.55
  32.6 48.9 %all_to_all.46 = bf16[2048,3,64,2]{0,3,1,2:T(2,128)(2,1)S(1)} all-to-all(bf16[2048,3,64,2]{0,3,1,2:T(2,128)(2,1)S(1)} %copy.55), channel_id=1, replica_groups=mesh['dp'=16,'mp'=32] {'mp'}, dimensions={2} | all-to-all | bytes 3145728 | tf_op jit(solution)/shard_map/all_to_all | solution.py:114
  81.5 1.3 copy.86
  82.7 0.6 all_to_all.35
  83.4 0.3 convolution_bitcast_fusion.1
  83.7 0.3 convolution_bitcast_fusion
  84.0 0.5 copy-done
  84.5 0.7 multiply_convert_fusion.1
  85.2 0.3 fusion.3
  85.5 0.3 fusion.4
  85.9 0.3 fusion.5
  86.2 0.2 pad_maximum_fusion.1
  86.4 2.8 %copy.60 = bf16[2048,3,64,2]{0,3,1,2:T(2,128)(2,1)} copy(bf16[2048,3,64,2]{0,2,3,1:T(8,128)(2,1)S(1)} %pad_maximum_fusion.1) | data formatting | bytes 3145728 | tf_op jit(solution)/shard_map/stack | solution.py:136
  89.2 5.1 %all-to-all-start.1 = ((bf16[2048,3,64,2]{0,3,1,2:T(2,128)(2,1)}), bf16[2048,3,64,2]{0,3,1,2:T(2,128)(2,1)S(1)}, u32[]{:S(2)}, u32[]{:S(2)}) async-start(bf16[2048,3,64,2]{0,3,1,2:T(2,128)(2,1)} %copy.60), calls=%async_computation.1 | async-start | bytes 3145728 | tf_op jit(solution)/shard_map/all_to_all | solution.py:135
  94.3 0.0 copy-start.17
  94.3 0.9 fusion.9
  95.2 1.2 copy.63
  96.4 1.2 gather_fusion.3
  97.7 2.2 %gather_fusion.2 = f32[3,2,64,64]{3,2,1,0:T(8,128)} fusion(f32[6,2,64,64]{3,2,1,0:T(8,128)} %bitcast.167, s32[1024]{0:T(1024)S(1)} %pad_clamp_fusion.1), kind=kCustom, calls=%fused_computation.2 | custom fusion | bytes 196620 | tf_op jit(solution)/shard_map/gather | solution.py:131
  99.9 1.0 copy.65
  100.9 1.0 copy.66
  101.9 0.3 copy.67
  102.2 2.4 %pad_maximum_fusion.2.refs_1_ = bf16[3,2048,128]{2,1,0:T(8,128)(2,1)} fusion(bf16[1,2048,128]{2,1,0:T(8,128)(2,1)S(1)} %copy.67, bf16[1,2048,128]{2,1,0:T(8,128)(2,1)} %copy.66, bf16[1,2048,128]{2,1,0:T(8,128)(2,1)S(1)} %copy-done.9), kind=kLoop, calls=%fused_computation.22 | loop fusion | flops 1572864 | bytes 3145728 | tf_op jit(solution)/shard_map/stack | solution.py:130
  104.6 3.3 %shard_map.131 = f32[2,3,2,64,64]{4,3,2,1,0:T(8,128)} custom-call(bf16[3,2,64,2048]{3,2,1,0:T(8,128)(2,1)} %bitcast.151, bf16[3,2048,128]{2,1,0:T(8,128)(2,1)} %pad_maximum_fusion.2.refs_1_, f32[3,2,64,64]{3,2,1,0:T(8,128)} %gather_fusion.2, f32[3,2,64,64]{3,2,1,0:T(8,128)} %gather_fusion.3), custom_call_target="tpu_custom_call" | custom-call | tf_op jit(solution)/shard_map/pallas_call | solution.py:82
  107.9 1.9 %copy.87 = f32[2,3,2,16,4,64]{5,4,2,1,0,3:T(4,128)} copy(f32[2,3,2,16,4,64]{5,4,3,2,1,0:T(4,128)} %bitcast.172) | data formatting | bytes 393216 | tf_op jit(solution)/shard_map/reshape | solution.py:34
  109.8 2.0 %reshape.73 = f32[16,1,3072]{2,1,0:T(1,128)} reshape(f32[16,2,3,2,4,64]{5,4,3,2,1,0:T(4,128)} %bitcast.169) | data formatting | bytes 393216
  111.8 18.3 %all-to-all-done.1 = bf16[2048,3,64,2]{0,3,1,2:T(2,128)(2,1)S(1)} async-done(((bf16[2048,3,64,2]{0,3,1,2:T(2,128)(2,1)}), bf16[2048,3,64,2]{0,3,1,2:T(2,128)(2,1)S(1)}, u32[]{:S(2)}, u32[]{:S(2)}) %all-to-all-start.1) | async-done | bytes 1572896 | tf_op jit(solution)/shard_map/all_to_all | solution.py:135
  130.1 7.4 %all-to-all-start.3 = ((f32[16,1,3072]{2,1,0:T(1,128)}), f32[16,1,3072]{2,1,0:T(1,128)}, u32[]{:S(2)}, u32[]{:S(2)}) async-start(f32[16,1,3072]{2,1,0:T(1,128)} %reshape.73), calls=%async_computation.3 | async-start | bytes 393216 | tf_op jit(solution)/shard_map/all_to_all | solution.py:37
  137.6 1.2 gather_fusion.1
  138.8 1.2 gather_fusion
  140.0 1.1 pad_maximum_fusion.3.refs_1_
  141.1 1.3 copy.85
  142.4 2.0 %all_to_all.39 = bf16[2048,3,2,64]{0,3,2,1:T(8,128)(2,1)} reshape(bf16[2048,3,2,32,2]{0,4,3,2,1:T(2,128)(2,1)S(1)} %bitcast.155) | data formatting | bytes 3145728 | tf_op jit(solution)/shard_map/all_to_all | solution.py:135
  144.4 3.3 %shard_map.130 = f32[2,3,2,64,64]{4,3,2,1,0:T(8,128)} custom-call(bf16[3,2,64,2048]{3,2,1,0:T(8,128)(2,1)} %bitcast.156, bf16[2,2048,128]{2,1,0:T(8,128)(2,1)} %pad_maximum_fusion.3.refs_1_, f32[3,2,64,64]{3,2,1,0:T(8,128)} %gather_fusion, f32[3,2,64,64]{3,2,1,0:T(8,128)} %gather_fusion.1), custom_call_target="tpu_custom_call" | custom-call | tf_op jit(solution)/shard_map/pallas_call | solution.py:82
  147.7 1.1 copy.88
  148.8 1.1 reshape.75
  149.8 7.3 %all-to-all-start.2 = ((f32[16,1,3072]{2,1,0:T(1,128)}), f32[16,1,3072]{2,1,0:T(1,128)S(1)}, u32[]{:S(2)}, u32[]{:S(2)}) async-start(f32[16,1,3072]{2,1,0:T(1,128)} %reshape.75), calls=%async_computation.2 | async-start | bytes 393216 | tf_op jit(solution)/shard_map/all_to_all | solution.py:37
  157.1 0.0 copy-start.13
  157.1 0.0 copy-start.14
  157.1 0.5 broadcast.71
  157.7 2.0 %reduce = f32[16,3072]{1,0:T(8,128)S(1)} reduce(f32[16,1,3072]{2,1,0:T(1,128)} %all-to-all-done.3, f32[]{:T(128)} %broadcast.71), dimensions={1}, to_apply=%all_to_all.41.reduce_sub_computation | reduce | bytes 393220 | tf_op jit(solution)/shard_map/all_to_all | solution.py:37
  159.7 0.3 reshape.74
  160.0 0.1 reduce_sum.19
  160.1 7.2 %all-to-all-done.2 = f32[16,1,3072]{2,1,0:T(1,128)S(1)} async-done(((f32[16,1,3072]{2,1,0:T(1,128)}), f32[16,1,3072]{2,1,0:T(1,128)S(1)}, u32[]{:S(2)}, u32[]{:S(2)}) %all-to-all-start.2) | async-done | bytes 196640 | tf_op jit(solution)/shard_map/all_to_all | solution.py:37
  167.3 1.1 reduce.1
  168.4 0.3 reshape.76
  168.7 0.1 reduce_sum.18
  168.8 0.6 gather_fusion.4
  169.4 0.7 divide_subtract_fusion
  (34 shorter events, 0.1 us)
Async XLA Ops:
  0.6 28.1 %copy-start.10 = (f32[1,6,2,64,64]{4,3,2,1,0:T(8,128)S(1)}, f32[1,6,2,64,64]{4,3,2,1,0:T(8,128)}, u32[]{:S(2)}) copy-start(f32[1,6,2,64,64]{4,3,2,1,0:T(8,128)} %param.16) | copy-start | bytes 589828
  1.5 27.4 %copy-start.7 = (bf16[2048,128]{1,0:T(8,128)(2,1)S(1)}, bf16[2048,128]{1,0:T(8,128)(2,1)}, u32[]{:S(2)}) copy-start(bf16[2048,128]{1,0:T(8,128)(2,1)} %param.11) | copy-start | bytes 1572868
  28.7 0.9 copy-start.1
  29.1 1.1 copy-start.5
  83.4 1.1 copy-start
  85.2 1.0 copy-start.3
  89.2 5.1 %copy-start.2 = (f32[64,2,6,2,64]{0,4,3,2,1:T(8,128)S(1)}, f32[64,2,6,2,64]{0,4,3,2,1:T(8,128)}, u32[]{:S(2)}) copy-start(f32[64,2,6,2,64]{0,4,3,2,1:T(8,128)} %copy-done.1) | copy-start | bytes 1179652
  89.2 40.9 %all-to-all-start.1 = ((bf16[2048,3,64,2]{0,3,1,2:T(2,128)(2,1)}), bf16[2048,3,64,2]{0,3,1,2:T(2,128)(2,1)S(1)}, u32[]{:S(2)}, u32[]{:S(2)}) async-start(bf16[2048,3,64,2]{0,3,1,2:T(2,128)(2,1)} %copy.60), calls=%async_computation.1 | async-start | bytes 3145728 | tf_op jit(solution)/shard_map/all_to_all | solution.py:135
  94.3 2.1 %copy-start.17 = (s32[3]{0:T(128)S(1)}, s32[3]{0:T(128)}, u32[]{:S(2)}) copy-start(s32[3]{0:T(128)} %constant.57) | copy-start | bytes 40
  95.2 4.7 %copy-start.4 = (bf16[2048,2,64]{0,2,1:T(8,128)(2,1)S(1)}, bf16[2048,2,64]{0,2,1:T(8,128)(2,1)}, u32[]{:S(2)}) copy-start(bf16[2048,2,64]{0,2,1:T(8,128)(2,1)} %copy-done.3) | copy-start | bytes 1572868
  100.9 1.3 copy-start.9
  107.9 29.7 %copy-start.16 = (s32[3]{0:T(128)S(1)}, s32[3]{0:T(128)}, u32[]{:S(2)}) copy-start(s32[3]{0:T(128)} %constant.55) | copy-start | bytes 40
  107.9 30.9 %copy-start.11 = (f32[1,6,2,64,64]{4,3,2,1,0:T(8,128)S(1)}, f32[1,6,2,64,64]{4,3,2,1,0:T(8,128)}, u32[]{:S(2)}) copy-start(f32[1,6,2,64,64]{4,3,2,1,0:T(8,128)} %param.16) | copy-start | bytes 589828
  107.9 32.2 %copy-start.6 = (bf16[2048,128]{1,0:T(8,128)(2,1)S(1)}, bf16[2048,128]{1,0:T(8,128)(2,1)}, u32[]{:S(2)}) copy-start(bf16[2048,128]{1,0:T(8,128)(2,1)} %param.12) | copy-start | bytes 1572868
  107.9 32.2 %copy-start.8 = (bf16[2048,128]{1,0:T(8,128)(2,1)S(1)}, bf16[2048,128]{1,0:T(8,128)(2,1)}, u32[]{:S(2)}) copy-start(bf16[2048,128]{1,0:T(8,128)(2,1)} %param.11) | copy-start | bytes 1572868
  130.1 19.7 %all-to-all-start.3 = ((f32[16,1,3072]{2,1,0:T(1,128)}), f32[16,1,3072]{2,1,0:T(1,128)}, u32[]{:S(2)}, u32[]{:S(2)}) async-start(f32[16,1,3072]{2,1,0:T(1,128)} %reshape.73), calls=%async_computation.3 | async-start | bytes 393216 | tf_op jit(solution)/shard_map/all_to_all | solution.py:37
  147.7 9.4 %copy-start.15 = (s32[6]{0:T(128)S(1)}, s32[6]{0:T(128)}, u32[]{:S(2)}) copy-start(s32[6]{0:T(128)} %constant.59) | copy-start | bytes 76
  149.8 17.5 %all-to-all-start.2 = ((f32[16,1,3072]{2,1,0:T(1,128)}), f32[16,1,3072]{2,1,0:T(1,128)S(1)}, u32[]{:S(2)}, u32[]{:S(2)}) async-start(f32[16,1,3072]{2,1,0:T(1,128)} %reshape.75), calls=%async_computation.2 | async-start | bytes 393216 | tf_op jit(solution)/shard_map/all_to_all | solution.py:37
  157.1 12.3 %copy-start.12 = (f32[6,2,4,64]{3,2,1,0:T(4,128)S(1)}, f32[6,2,4,64]{3,2,1,0:T(4,128)}, u32[]{:S(2)}) copy-start(f32[6,2,4,64]{3,2,1,0:T(4,128)} %param.13) | copy-start | bytes 36868
  157.1 12.3 %copy-start.13 = (f32[6,2,4,64]{3,2,1,0:T(4,128)S(1)}, f32[6,2,4,64]{3,2,1,0:T(4,128)}, u32[]{:S(2)}) copy-start(f32[6,2,4,64]{3,2,1,0:T(4,128)} %param.14) | copy-start | bytes 36868
  157.1 12.3 %copy-start.14 = (f32[6,2,4,64]{3,2,1,0:T(4,128)S(1)}, f32[6,2,4,64]{3,2,1,0:T(4,128)}, u32[]{:S(2)}) copy-start(f32[6,2,4,64]{3,2,1,0:T(4,128)} %param.15) | copy-start | bytes 36868

commit v7 on v5

--- a/solution.py
+++ b/solution.py
@@ -1,3 +1,5 @@
+import functools
+
 import jax
 import jax.numpy as jnp
 from jax import lax
@@ -48,8 +50,13 @@
     return lax.dot_general(a, b, (((1,), (0,)), ((), ())), preferred_element_type=jnp.float32)
 
 
-def grads_kernel(x_ref, c_ref, first_ref, second_ref, h_ref, gl_ref, gr_ref, noise_ref, spread_ref,
-                 out_ref, acc_ref, *, scale):
+def grads_kernel(*refs, scale, pairs, n_minor, n_major, carry):
+    minor = refs[:n_minor]
+    major = refs[n_minor:n_minor + n_major]
+    noise_ref, spread_ref = refs[n_minor + n_major:n_minor + n_major + 2]
+    rest = refs[n_minor + n_major + 2:]
+    prev_ref = rest[0] if carry else None
+    out_ref, acc_ref = rest[-2], rest[-1]
     step = pl.program_id(0)
     nb, width = acc_ref.shape[1], acc_ref.shape[2]
 
@@ -59,45 +66,58 @@
 
     for b in range(nb):
         cols = slice(b * width, (b + 1) * width)
-        pairs = (
-            (second_ref[1, b], x_ref[:, cols]),
-            (first_ref[0, b], gl_ref[:, cols]),
-            (second_ref[2, b], x_ref[:, cols]),
-            (first_ref[1, b], gr_ref[:, cols]),
-            (first_ref[2, b], h_ref[:, cols]),
-            (second_ref[0, b], c_ref[:, cols]),
-        )
-        for f, (lhs, rhs) in enumerate(pairs):
-            acc_ref[f, b] += nn_dot(lhs, rhs)
+        for k, (f, lhs, rhs, flip) in enumerate(pairs):
+            acc_ref[k, b] += nn_dot(minor[lhs][b], major[rhs][:, cols])
 
     @pl.when(step == pl.num_programs(0) - 1)
     def _():
-        for f in range(acc_ref.shape[0]):
+        done = set()
+        for k, (f, lhs, rhs, flip) in enumerate(pairs):
+            done.add(f)
             for b in range(nb):
-                grad = acc_ref[f, b]
-                if f in (0, 2, 4):
+                grad = acc_ref[k, b]
+                if flip:
                     grad = grad.T
                 grad = grad * scale
                 out_ref[0, f, b] = grad
                 out_ref[1, f, b] = grad * noise_ref[f, b] * spread_ref[f, b]
+        if carry:
+            for f in range(noise_ref.shape[0]):
+                if f not in done:
+                    out_ref[:, f] = prev_ref[:, f]
 
 
-def grads_and_curvature(x, c, first_t, second_t, h, gl, gr, noise, spread, scale):
-    tokens, feats = x.shape
-    nb, width = first_t.shape[1], first_t.shape[2]
+def grads_and_curvature(minor, major, noise, spread, scale, pairs, prev=None):
+    nb, width, tokens = minor[0].shape
+    feats = major[0].shape[1]
     tb = min(TOKEN_BLOCK, tokens)
-    act = pl.BlockSpec((tb, feats), lambda i: (i, 0))
-    trio = pl.BlockSpec((3, nb, width, tb), lambda i: (0, 0, 0, i))
-    whole = pl.BlockSpec(noise.shape, lambda i: (0, 0, 0, 0))
+    whole4 = pl.BlockSpec(noise.shape, lambda i: (0, 0, 0, 0))
+    whole5 = pl.BlockSpec((2,) + noise.shape, lambda i: (0, 0, 0, 0, 0))
+    in_specs = (
+        [pl.BlockSpec((nb, width, tb), lambda i: (0, 0, i))] * len(minor)
+        + [pl.BlockSpec((tb, feats), lambda i: (i, 0))] * len(major)
+        + [whole4, whole4]
+    )
+    operands = list(minor) + list(major) + [noise, spread]
+    aliases = {}
+    if prev is not None:
+        in_specs.append(whole5)
+        aliases = {len(operands): 0}
+        operands.append(prev)
+    kernel = functools.partial(
+        grads_kernel, scale=scale, pairs=pairs, n_minor=len(minor), n_major=len(major),
+        carry=prev is not None,
+    )
     return pl.pallas_call(
-        lambda *refs: grads_kernel(*refs, scale=scale),
+        kernel,
         grid=(tokens // tb,),
-        in_specs=[act, act, trio, trio, act, act, act, whole, whole],
-        out_specs=pl.BlockSpec((2,) + noise.shape, lambda i: (0, 0, 0, 0, 0)),
+        in_specs=in_specs,
+        out_specs=whole5,
         out_shape=jax.ShapeDtypeStruct((2,) + noise.shape, jnp.float32),
-        scratch_shapes=[pltpu.VMEM(noise.shape, jnp.float32)],
+        scratch_shapes=[pltpu.VMEM((len(pairs), nb, width, width), jnp.float32)],
+        input_output_aliases=aliases,
         compiler_params=pltpu.CompilerParams(dimension_semantics=("arbitrary",)),
-    )(x, c, first_t, second_t, h, gl, gr, noise, spread)
+    )(*operands)
 
 
 def per_device(inputs, out_grad, mean_state, hess_state, grad_state, noise_draw):
@@ -129,14 +149,20 @@
     value_grad = (d_hidden * jax.nn.silu(u_left)).astype(jnp.bfloat16)
     back_left = bdot("tjc,jic->tij", gate_grad, sampled[1]).astype(jnp.bfloat16)
     back_right = bdot("tjc,jic->tij", value_grad, sampled[3]).astype(jnp.bfloat16)
+    token_minor = lambda a: jnp.moveaxis(a, 0, -1)
+    flat = lambda a: a.reshape(tokens, -1)
+    first_t = token_minor(first)
+    early = grads_and_curvature(
+        [first_t[0], first_t[1], first_t[2]], [flat(gate_grad), flat(value_grad), flat(hidden)],
+        noise, spread, scale, pairs=((1, 0, 0, False), (3, 1, 1, False), (4, 2, 2, True)),
+    )
     second = lax.all_to_all(
         jnp.stack([outer, back_left, back_right], axis=1), "mp", split_axis=2, concat_axis=3, tiled=True
     )
-    token_minor = lambda a: jnp.moveaxis(a, 0, -1)
-    flat = lambda a: a.reshape(tokens, -1)
+    second_t = token_minor(second)
     stacked = grads_and_curvature(
-        inputs, out_grad, token_minor(first), token_minor(second),
-        flat(hidden), flat(gate_grad), flat(value_grad), noise, spread, scale,
+        [second_t[0], second_t[1], second_t[2]], [inputs, out_grad],
+        noise, spread, scale, pairs=((0, 1, 0, True), (2, 2, 0, True), (5, 0, 1, False)), prev=early,
     )
     sums = scatter_rows(stacked, groups)
     grad_avg = sums[0] / groups

time: 167 us -> 168 us (level)
  waiting for transfers between devices: 30.9 us -> 23 us
  local copies, waits for them, and re-layouts: 20.7 us -> 26.7 us
  Pallas kernels: 4.75 us -> 7.64 us
    all_to_all x1, waiting for transfers between devices: 30.9 us -> 23 us  [per_device(): lax.all_to_all(jnp.stack([outer, back_left, back_right], axis=1), 'mp', s...]
    pallas_call x1 -> x2, Pallas kernels: 4.75 us -> 7.64 us  [grads_and_curvature(): pl.pallas_call(kernel, grid=(tokens // tb,), in_specs=in_specs, out_specs...]
    squeeze x0 -> x2, local copies, waits for them, and re-layouts: none -> 2.38 us  [the longest x1 1.19 us: per_device(): second_t[2]]
    reshape x3, local copies, waits for them, and re-layouts: 4.04 us -> 6.11 us  [per_device(): flat = lambda a: a.reshape(tokens, -1)]
    unnamed x26 -> x22, local copies, waits for them, and re-layouts: 4.32 us -> 4.29 us
  transfers between devices with their start and end apart: 1 -> 1, of which waited for: 1 -> 1; matrix products, arithmetic and copies ran while one was open for 3% -> 5% of each run, Pallas kernels for 0% -> 2%
where the time goes in v7:
time: 168 us; the launch traced here: 167 us
  blocking collectives  96 us (57%)
  local copies, waits for them, and re-layouts  26.7 us (16%)
  waiting for transfers between devices  23 us (14%)
  Pallas kernels  7.64 us (5%)
  starting transfers between devices  4.94 us (3%)
  other arithmetic  4.82 us (3%)
  matrix products  3.16 us (2%)
    all_to_all x1, blocking collectives, per_device(): lax.all_to_all(jnp.stack([y_left, y_right, back_outer], axis=1), 'mp', sp...  48.9 us
    all_gather x1, blocking collectives, gather_rows(): full = lax.all_gather(moved, 'dp', axis=0, tiled=True)  26.6 us
    all_to_all x1, waiting for transfers between devices, per_device(): lax.all_to_all(jnp.stack([outer, back_left, back_right], axis=1), 'mp', s...  23 us
    all_to_all x1, blocking collectives, scatter_rows(): got = lax.all_to_all(split, 'dp', split_axis=0, concat_axis=0, tiled=True)  20.5 us
    pallas_call x2, Pallas kernels, grads_and_curvature(): pl.pallas_call(kernel, grid=(tokens // tb,), in_specs=in_specs, out_specs...  7.64 us
    reshape x3, local copies, waits for them, and re-layouts, per_device(): flat = lambda a: a.reshape(tokens, -1)  6.11 us
    all_to_all x1, starting transfers between devices, per_device(): lax.all_to_all(jnp.stack([outer, back_left, back_right], axis=1), 'mp', s...  4.94 us
    all_to_all x2, local copies, waits for them, and re-layouts, per_device(): lax.all_to_all(jnp.stack([outer, back_left, back_right], axis=1), 'mp', s...  4.88 us
  transfers between devices with their start and end apart: 1, of which 1 were waited for; matrix products, arithmetic and copies ran while one was open for 5% of the time, Pallas kernels for 2%

profile of v7, /device:TPU:1, one launch (start us, length us, event | category | flops | bytes accessed | tf_op | source)
XLA Modules:
  0.0 167.2 jit_solution(17145084093719185951)
XLA Ops:
  0.6 0.0 copy-start.1
  0.6 1.3 copy.38
  1.9 0.8 copy_bitcast_fusion.4
  2.8 26.6 %all_gather.3 = f32[64,2,6,2,64]{4,3,2,1,0:T(2,128)S(1)} all-gather(f32[4,2,6,2,64]{4,3,2,1,0:T(2,128)S(1)} %maximum_bitcast_fusion), channel_id=1, replica_groups=mesh['dp'=16,'mp'=32] {'dp'}, dimensions={0}, use_global_device_ids=true | all-gather | bytes 417792 | tf_op jit(solution)/shard_map/all_gather | solution.py:30
  29.4 0.2 copy.67
  29.6 0.0 copy-start
  29.6 0.9 copy-done
  30.4 0.0 copy-done.1
  30.4 0.0 copy-start.2
  30.5 0.2 fusion.11
  30.6 0.3 fusion.1
  31.0 0.3 fusion
  31.3 0.2 copy-done.2
  31.5 0.2 copy.41
  31.7 0.3 fusion.2
  32.0 0.2 pad_maximum_fusion
  32.2 1.6 copy.42
  33.8 48.9 %all_to_all.41 = bf16[2048,3,64,2]{0,3,1,2:T(2,128)(2,1)S(1)} all-to-all(bf16[2048,3,64,2]{0,3,1,2:T(2,128)(2,1)S(1)} %copy.42), channel_id=1, replica_groups=mesh['dp'=16,'mp'=32] {'mp'}, dimensions={2} | all-to-all | bytes 3145728 | tf_op jit(solution)/shard_map/all_to_all | solution.py:139
  82.7 1.3 copy.65
  83.9 0.6 all_to_all.32
  84.6 0.3 convolution_bitcast_fusion
  84.9 0.3 convolution_bitcast_fusion.2
  85.2 0.7 multiply_convert_fusion.2
  85.9 0.0 copy-start.3
  85.9 0.0 copy-start.4
  85.9 0.0 copy-start.5
  85.9 0.3 fusion.3
  86.3 0.3 fusion.4
  86.6 0.1 copy-done.3
  86.7 0.2 copy-done.4
  86.9 0.2 copy-done.5
  87.1 0.3 fusion.5
  87.3 0.2 pad_maximum_fusion.1
  87.5 2.8 %copy.47 = bf16[2048,3,64,2]{0,3,1,2:T(2,128)(2,1)} copy(bf16[2048,3,64,2]{0,2,3,1:T(8,128)(2,1)S(1)} %pad_maximum_fusion.1) | data formatting | bytes 3145728 | tf_op jit(solution)/shard_map/stack | solution.py:160
  90.3 4.9 %all-to-all-start.1 = ((bf16[2048,3,64,2]{0,3,1,2:T(2,128)(2,1)}), bf16[2048,3,64,2]{0,3,1,2:T(2,128)(2,1)S(1)}, u32[]{:S(2)}, u32[]{:S(2)}) async-start(bf16[2048,3,64,2]{0,3,1,2:T(2,128)(2,1)} %copy.47), calls=%async_computation.1 | async-start | bytes 3145728 | tf_op jit(solution)/shard_map/all_to_all | solution.py:159
  95.2 1.9 %fusion.9.refs_7_.refs_6_ = f32[6,2,64,64]{3,2,1,0:T(8,128)} fusion(f32[2,6,2,64,64]{4,3,2,1,0:T(8,128)} %bitcast.155), kind=kLoop, calls=%fused_computation.38 | loop fusion | flops 98304 | bytes 393216 | tf_op jit(solution)/shard_map/sqrt | solution.py:131
  97.1 2.0 %copy.50.refs_4_ = bf16[2048,128]{1,0:T(8,128)(2,1)} copy(bf16[2048,128]{0,1:T(8,128)(2,1)} %bitcast.163) | data formatting | bytes 1048576 | tf_op jit(solution)/shard_map/reshape | solution.py:153
  99.2 2.0 %copy.49.refs_3_ = bf16[2048,128]{1,0:T(8,128)(2,1)} copy(bf16[2048,128]{0,1:T(8,128)(2,1)} %bitcast.162) | data formatting | bytes 1048576 | tf_op jit(solution)/shard_map/reshape | solution.py:153
  101.2 2.0 %copy.51.refs_5_ = bf16[2048,128]{1,0:T(8,128)(2,1)} copy(bf16[2048,128]{0,1:T(8,128)(2,1)} %bitcast.161) | data formatting | bytes 1048576 | tf_op jit(solution)/shard_map/reshape | solution.py:153
  103.2 1.2 slice_bitcast_fusion
  104.4 3.7 %shard_map.85.refs_7_ = f32[2,6,2,64,64]{4,3,2,1,0:T(8,128)} custom-call(bf16[2,64,2048]{2,1,0:T(8,128)(2,1)} %get-tuple-element.11.refs_0_, bf16[2,64,2048]{2,1,0:T(8,128)(2,1)} %get-tuple-element.10.refs_1_, bf16[2,64,2048]{2,1,0:T(8,128)(2,1)} %get-tuple-element.9.refs_2_, bf16[2048,128]{1,0:T(8,128)(2,1)} %copy.49.refs_3_, ...), custom_call_target="tpu_custom_call" | custom-call | tf_op jit(solution)/shard_map/pallas_call | solution.py:111
  108.1 23.0 %all-to-all-done.1 = bf16[2048,3,64,2]{0,3,1,2:T(2,128)(2,1)S(1)} async-done(((bf16[2048,3,64,2]{0,3,1,2:T(2,128)(2,1)}), bf16[2048,3,64,2]{0,3,1,2:T(2,128)(2,1)S(1)}, u32[]{:S(2)}, u32[]{:S(2)}) %all-to-all-start.1) | async-done | bytes 1572896 | tf_op jit(solution)/shard_map/all_to_all | solution.py:159
  131.1 2.4 %copy.64 = bf16[2048,3,32,2,2]{0,4,2,3,1:T(2,128)(2,1)} copy(bf16[2048,3,32,2,2]{0,4,1,3,2:T(2,128)(2,1)S(1)} %bitcast.149) | data formatting | bytes 3145728 | tf_op jit(solution)/shard_map/all_to_all | solution.py:159
  133.5 2.5 %all_to_all.36 = bf16[2048,3,2,64]{0,3,2,1:T(8,128)(2,1)S(1)} reshape(bf16[2048,3,2,32,2]{0,4,3,2,1:T(2,128)(2,1)} %bitcast.153) | data formatting | bytes 3145728 | tf_op jit(solution)/shard_map/all_to_all | solution.py:159
  136.0 1.2 slice_bitcast_fusion.3
  137.2 3.9 %shard_map.86 = f32[2,6,2,64,64]{4,3,2,1,0:T(8,128)} custom-call(bf16[2,64,2048]{2,1,0:T(8,128)(2,1)} %get-tuple-element.14.refs_0_, bf16[2,64,2048]{2,1,0:T(8,128)(2,1)} %get-tuple-element.13.refs_1_, bf16[2,64,2048]{2,1,0:T(8,128)(2,1)} %get-tuple-element.12.refs_2_, bf16[2048,128]{1,0:T(8,128)(2,1)} %refs_3_.1, ...), custom_call_target="tpu_custom_call", output_to_operand_aliasing={{}: (7, {})} | custom-call | tf_op jit(solution)/shard_map/pallas_call | solution.py:111
  141.1 1.3 copy.66
  142.5 0.7 reshape.41
  143.2 20.5 %all_to_all.42 = f32[16,1,6144]{2,1,0:T(1,128)S(1)} all-to-all(f32[16,1,6144]{2,1,0:T(1,128)S(1)} %reshape.41), channel_id=1, replica_groups=mesh['dp'=16,'mp'=32] {'dp'}, dimensions={0} | all-to-all | bytes 786432 | tf_op jit(solution)/shard_map/all_to_all | solution.py:39
  163.7 0.0 copy-start.6
  163.7 0.0 copy-start.7
  163.7 0.0 copy-start.8
  163.7 0.5 broadcast.39
  164.2 1.6 reduce
  165.8 0.5 reshape.42
  166.3 0.2 reduce_sum.9
  166.5 0.0 copy-done.6
  166.5 0.0 copy-done.7
  166.5 0.0 copy-done.8
  166.5 0.7 divide_subtract_fusion
  (1 shorter events, 0.0 us)
Async XLA Ops:
  0.6 29.8 %copy-start.1 = (f32[1,6,2,64,64]{4,3,2,1,0:T(8,128)S(1)}, f32[1,6,2,64,64]{4,3,2,1,0:T(8,128)}, u32[]{:S(2)}) copy-start(f32[1,6,2,64,64]{4,3,2,1,0:T(8,128)} %param.11) | copy-start | bytes 589828
  29.6 0.9 copy-start
  30.4 1.0 copy-start.2
  85.9 0.8 copy-start.3
  85.9 1.0 copy-start.4
  85.9 1.1 copy-start.5
  90.3 40.8 %all-to-all-start.1 = ((bf16[2048,3,64,2]{0,3,1,2:T(2,128)(2,1)}), bf16[2048,3,64,2]{0,3,1,2:T(2,128)(2,1)S(1)}, u32[]{:S(2)}, u32[]{:S(2)}) async-start(bf16[2048,3,64,2]{0,3,1,2:T(2,128)(2,1)} %copy.47), calls=%async_computation.1 | async-start | bytes 3145728 | tf_op jit(solution)/shard_map/all_to_all | solution.py:159
  163.7 2.8 %copy-start.6 = (f32[6,2,4,64]{3,2,1,0:T(4,128)S(1)}, f32[6,2,4,64]{3,2,1,0:T(4,128)}, u32[]{:S(2)}) copy-start(f32[6,2,4,64]{3,2,1,0:T(4,128)} %param.8) | copy-start | bytes 36868
  163.7 2.8 %copy-start.7 = (f32[6,2,4,64]{3,2,1,0:T(4,128)S(1)}, f32[6,2,4,64]{3,2,1,0:T(4,128)}, u32[]{:S(2)}) copy-start(f32[6,2,4,64]{3,2,1,0:T(4,128)} %param.9) | copy-start | bytes 36868
  163.7 2.8 %copy-start.8 = (f32[6,2,4,64]{3,2,1,0:T(4,128)S(1)}, f32[6,2,4,64]{3,2,1,0:T(4,128)}, u32[]{:S(2)}) copy-start(f32[6,2,4,64]{3,2,1,0:T(4,128)} %param.10) | copy-start | bytes 36868

commit v8 on v7

--- a/solution.py
+++ b/solution.py
@@ -67,7 +67,7 @@
     for b in range(nb):
         cols = slice(b * width, (b + 1) * width)
         for k, (f, lhs, rhs, flip) in enumerate(pairs):
-            acc_ref[k, b] += nn_dot(minor[lhs][b], major[rhs][:, cols])
+            acc_ref[k, b] += nn_dot(minor[0][lhs, b], major[rhs][:, cols])
 
     @pl.when(step == pl.num_programs(0) - 1)
     def _():
@@ -88,24 +88,24 @@
 
 
 def grads_and_curvature(minor, major, noise, spread, scale, pairs, prev=None):
-    nb, width, tokens = minor[0].shape
+    n_minor, nb, width, tokens = minor.shape
     feats = major[0].shape[1]
     tb = min(TOKEN_BLOCK, tokens)
     whole4 = pl.BlockSpec(noise.shape, lambda i: (0, 0, 0, 0))
     whole5 = pl.BlockSpec((2,) + noise.shape, lambda i: (0, 0, 0, 0, 0))
     in_specs = (
-        [pl.BlockSpec((nb, width, tb), lambda i: (0, 0, i))] * len(minor)
+        [pl.BlockSpec((n_minor, nb, width, tb), lambda i: (0, 0, 0, i))]
         + [pl.BlockSpec((tb, feats), lambda i: (i, 0))] * len(major)
         + [whole4, whole4]
     )
-    operands = list(minor) + list(major) + [noise, spread]
+    operands = [minor] + list(major) + [noise, spread]
     aliases = {}
     if prev is not None:
         in_specs.append(whole5)
         aliases = {len(operands): 0}
         operands.append(prev)
     kernel = functools.partial(
-        grads_kernel, scale=scale, pairs=pairs, n_minor=len(minor), n_major=len(major),
+        grads_kernel, scale=scale, pairs=pairs, n_minor=1, n_major=len(major),
         carry=prev is not None,
     )
     return pl.pallas_call(
@@ -153,7 +153,7 @@
     flat = lambda a: a.reshape(tokens, -1)
     first_t = token_minor(first)
     early = grads_and_curvature(
-        [first_t[0], first_t[1], first_t[2]], [flat(gate_grad), flat(value_grad), flat(hidden)],
+        first_t, [flat(gate_grad), flat(value_grad), flat(hidden)],
         noise, spread, scale, pairs=((1, 0, 0, False), (3, 1, 1, False), (4, 2, 2, True)),
     )
     second = lax.all_to_all(
@@ -161,7 +161,7 @@
     )
     second_t = token_minor(second)
     stacked = grads_and_curvature(
-        [second_t[0], second_t[1], second_t[2]], [inputs, out_grad],
+        second_t, [inputs, out_grad],
         noise, spread, scale, pairs=((0, 1, 0, True), (2, 2, 0, True), (5, 0, 1, False)), prev=early,
     )
     sums = scatter_rows(stacked, groups)

time: 168 us -> 167 us (level)
  local copies, waits for them, and re-layouts: 26.7 us -> 20.2 us
  waiting for transfers between devices: 23 us -> 27.3 us
    all_to_all x1, waiting for transfers between devices: 23 us -> 27.3 us  [per_device(): lax.all_to_all(jnp.stack([outer, back_left, back_right], axis=1), 'mp', s...]
    squeeze x2 -> x0, local copies, waits for them, and re-layouts: 2.38 us -> none  [the longest x1 1.19 us: per_device(): second_t[2]]
    reshape x3, local copies, waits for them, and re-layouts: 6.11 us -> 4.04 us  [per_device(): flat = lambda a: a.reshape(tokens, -1)]
    unnamed x22 -> x26, local copies, waits for them, and re-layouts: 4.29 us -> 3.82 us
  transfers between devices with their start and end apart: 1 -> 1, of which waited for: 1 -> 1; matrix products, arithmetic and copies ran while one was open for 5% -> 3% of each run, Pallas kernels for 2% -> 2%
where the time goes in v8:
time: 167 us; the launch traced here: 166 us
  blocking collectives  96 us (57%)
  waiting for transfers between devices  27.3 us (16%)
  local copies, waits for them, and re-layouts  20.2 us (12%)
  Pallas kernels  7.49 us (4%)
  starting transfers between devices  5.08 us (3%)
  matrix products  4.8 us (3%)
  other arithmetic  3.83 us (2%)
    all_to_all x1, blocking collectives, per_device(): lax.all_to_all(jnp.stack([y_left, y_right, back_outer], axis=1), 'mp', sp...  48.9 us
    all_to_all x1, waiting for transfers between devices, per_device(): lax.all_to_all(jnp.stack([outer, back_left, back_right], axis=1), 'mp', s...  27.3 us
    all_gather x1, blocking collectives, gather_rows(): full = lax.all_gather(moved, 'dp', axis=0, tiled=True)  26.6 us
    all_to_all x1, blocking collectives, scatter_rows(): got = lax.all_to_all(split, 'dp', split_axis=0, concat_axis=0, tiled=True)  20.5 us
    pallas_call x2, Pallas kernels, grads_and_curvature(): pl.pallas_call(kernel, grid=(tokens // tb,), in_specs=in_specs, out_specs...  7.49 us
    all_to_all x1, starting transfers between devices, per_device(): lax.all_to_all(jnp.stack([outer, back_left, back_right], axis=1), 'mp', s...  5.08 us
    dot_general x9, matrix products, bdot(): return jnp.einsum(form, left, right, preferred_element_type=jnp.float32)  4.8 us
    reshape x3, local copies, waits for them, and re-layouts, per_device(): flat = lambda a: a.reshape(tokens, -1)  4.04 us
  transfers between devices with their start and end apart: 1, of which 1 were waited for; matrix products, arithmetic and copies ran while one was open for 3% of the time, Pallas kernels for 2%

profile of v8, /device:TPU:1, one launch (start us, length us, event | category | flops | bytes accessed | tf_op | source)
XLA Modules:
  0.0 165.7 jit_solution(3903749910798111203)
XLA Ops:
  0.6 0.0 copy-start.3
  0.6 1.3 copy.38
  1.9 0.8 copy_bitcast_fusion.4
  2.8 26.6 %all_gather.3 = f32[64,2,6,2,64]{4,3,2,1,0:T(2,128)S(1)} all-gather(f32[4,2,6,2,64]{4,3,2,1,0:T(2,128)S(1)} %maximum_bitcast_fusion), channel_id=1, replica_groups=mesh['dp'=16,'mp'=32] {'dp'}, dimensions={0}, use_global_device_ids=true | all-gather | bytes 417792 | tf_op jit(solution)/shard_map/all_gather | solution.py:30
  29.4 0.2 copy.67
  29.6 0.0 copy-start.1
  29.6 0.9 copy-done.1
  30.5 0.0 copy-done.3
  30.5 0.0 copy-start.4
  30.5 0.2 fusion.11
  30.6 0.0 copy-start.6
  30.7 0.3 fusion.1
  31.0 0.3 fusion
  31.4 0.1 copy-done.4
  31.5 0.2 copy.41
  31.7 0.0 copy-done.6
  31.7 0.3 fusion.2
  32.0 0.2 pad_maximum_fusion
  32.2 1.6 copy.42
  33.8 48.9 %all_to_all.41 = bf16[2048,3,64,2]{0,3,1,2:T(2,128)(2,1)S(1)} all-to-all(bf16[2048,3,64,2]{0,3,1,2:T(2,128)(2,1)S(1)} %copy.42), channel_id=1, replica_groups=mesh['dp'=16,'mp'=32] {'mp'}, dimensions={2} | all-to-all | bytes 3145728 | tf_op jit(solution)/shard_map/all_to_all | solution.py:139
  82.7 1.3 copy.65
  84.0 0.6 all_to_all.32
  84.6 0.0 copy-start
  84.6 0.0 copy-start.7
  84.6 1.1 convolution_bitcast_fusion
  85.8 1.1 convolution_bitcast_fusion.2
  86.9 0.0 copy-done
  86.9 0.0 copy-done.7
  86.9 0.7 multiply_convert_fusion.2
  87.6 0.0 copy-start.5
  87.6 0.3 fusion.3
  88.0 0.3 fusion.4
  88.3 0.3 fusion.5
  88.5 0.2 pad_maximum_fusion.1
  88.7 0.0 copy-done.5
  88.7 2.8 %copy.47 = bf16[2048,3,64,2]{0,3,1,2:T(2,128)(2,1)} copy(bf16[2048,3,64,2]{0,2,3,1:T(8,128)(2,1)S(1)} %pad_maximum_fusion.1) | data formatting | bytes 3145728 | tf_op jit(solution)/shard_map/stack | solution.py:160
  91.5 0.0 copy-start.2
  91.5 5.1 %all-to-all-start.1 = ((bf16[2048,3,64,2]{0,3,1,2:T(2,128)(2,1)}), bf16[2048,3,64,2]{0,3,1,2:T(2,128)(2,1)S(1)}, u32[]{:S(2)}, u32[]{:S(2)}) async-start(bf16[2048,3,64,2]{0,3,1,2:T(2,128)(2,1)} %copy.47), calls=%async_computation.1 | async-start | bytes 3145728 | tf_op jit(solution)/shard_map/all_to_all | solution.py:159
  96.6 0.0 copy-done.2
  96.6 0.9 fusion.9.refs_5_.refs_4_
  97.5 2.0 %copy.50.refs_2_ = bf16[2048,128]{1,0:T(8,128)(2,1)} copy(bf16[2048,128]{0,1:T(8,128)(2,1)} %bitcast.151) | data formatting | bytes 1048576 | tf_op jit(solution)/shard_map/reshape | solution.py:153
  99.5 1.0 copy.49.refs_1_
  100.5 1.0 copy.51.refs_3_
  101.5 3.6 %shard_map.85.refs_5_ = f32[2,6,2,64,64]{4,3,2,1,0:T(8,128)} custom-call(bf16[3,2,64,2048]{3,2,1,0:T(8,128)(2,1)} %bitcast.135, bf16[2048,128]{1,0:T(8,128)(2,1)} %copy.49.refs_1_, bf16[2048,128]{1,0:T(8,128)(2,1)} %copy.50.refs_2_, bf16[2048,128]{1,0:T(8,128)(2,1)} %copy.51.refs_3_, f32[6,2,64,64]{3,2,1,0:T(8,128)} %bitcast.146, ...), custom_call_target="tpu_custom_call" | custom-call | tf_op jit(solution)/shard_map/pallas_call | solution.py:111
  105.2 27.3 %all-to-all-done.1 = bf16[2048,3,64,2]{0,3,1,2:T(2,128)(2,1)S(1)} async-done(((bf16[2048,3,64,2]{0,3,1,2:T(2,128)(2,1)}), bf16[2048,3,64,2]{0,3,1,2:T(2,128)(2,1)S(1)}, u32[]{:S(2)}, u32[]{:S(2)}) %all-to-all-start.1) | async-done | bytes 1572896 | tf_op jit(solution)/shard_map/all_to_all | solution.py:159
  132.5 1.3 copy.64
  133.7 2.0 %all_to_all.36 = bf16[2048,3,2,64]{0,3,2,1:T(8,128)(2,1)} reshape(bf16[2048,3,2,32,2]{0,4,3,2,1:T(2,128)(2,1)S(1)} %bitcast.141) | data formatting | bytes 3145728 | tf_op jit(solution)/shard_map/all_to_all | solution.py:159
  135.8 3.9 %shard_map.86 = f32[2,6,2,64,64]{4,3,2,1,0:T(8,128)} custom-call(bf16[3,2,64,2048]{3,2,1,0:T(8,128)(2,1)} %bitcast.138, bf16[2048,128]{1,0:T(8,128)(2,1)} %refs_1_.1, bf16[2048,128]{1,0:T(8,128)(2,1)} %refs_2_.1, f32[6,2,64,64]{3,2,1,0:T(8,128)} %bitcast.147, f32[6,2,64,64]{3,2,1,0:T(8,128)} %fusion.9.refs_5_.refs_4_, ...), custom_call_target="tpu_custom_call", output_to_operand_aliasing={{}: (5, {})} | custom-call | tf_op jit(solution)/shard_map/pallas_call | solution.py:111
  139.6 1.3 copy.66
  141.0 0.7 reshape.41
  141.7 20.5 %all_to_all.42 = f32[16,1,6144]{2,1,0:T(1,128)S(1)} all-to-all(f32[16,1,6144]{2,1,0:T(1,128)S(1)} %reshape.41), channel_id=1, replica_groups=mesh['dp'=16,'mp'=32] {'dp'}, dimensions={0} | all-to-all | bytes 786432 | tf_op jit(solution)/shard_map/all_to_all | solution.py:39
  162.2 0.0 copy-start.8
  162.2 0.0 copy-start.9
  162.2 0.0 copy-start.10
  162.2 0.5 broadcast.39
  162.7 1.6 reduce
  164.3 0.5 reshape.42
  164.8 0.2 reduce_sum.9
  165.0 0.0 copy-done.8
  165.0 0.0 copy-done.9
  165.0 0.0 copy-done.10
  165.0 0.7 divide_subtract_fusion
  (1 shorter events, 0.0 us)
Async XLA Ops:
  0.6 29.8 %copy-start.3 = (f32[1,6,2,64,64]{4,3,2,1,0:T(8,128)S(1)}, f32[1,6,2,64,64]{4,3,2,1,0:T(8,128)}, u32[]{:S(2)}) copy-start(f32[1,6,2,64,64]{4,3,2,1,0:T(8,128)} %param.11) | copy-start | bytes 589828
  29.6 0.9 copy-start.1
  30.5 1.0 copy-start.4
  30.6 1.1 copy-start.6
  84.6 2.3 %copy-start = (bf16[2048,3,2,64]{0,3,2,1:T(8,128)(2,1)}, bf16[2048,3,2,64]{0,3,2,1:T(8,128)(2,1)S(1)}, u32[]{:S(2)}) copy-start(bf16[2048,3,2,64]{0,3,2,1:T(8,128)(2,1)S(1)} %all_to_all.32) | copy-start | bytes 4718596
  84.6 2.3 %copy-start.7 = (bf16[6,2,64,64]{3,2,1,0:T(8,128)(2,1)S(1)}, bf16[6,2,64,64]{3,2,1,0:T(8,128)(2,1)}, u32[]{:S(2)}) copy-start(bf16[6,2,64,64]{3,2,1,0:T(8,128)(2,1)} %copy-done.6) | copy-start | bytes 294916
  87.6 1.1 copy-start.5
  91.5 5.1 %copy-start.2 = (f32[64,2,6,2,64]{4,0,3,2,1:T(8,128)S(1)}, f32[64,2,6,2,64]{4,0,3,2,1:T(8,128)}, u32[]{:S(2)}) copy-start(f32[64,2,6,2,64]{4,0,3,2,1:T(8,128)} %copy-done.1) | copy-start | bytes 1179652
  91.5 41.0 %all-to-all-start.1 = ((bf16[2048,3,64,2]{0,3,1,2:T(2,128)(2,1)}), bf16[2048,3,64,2]{0,3,1,2:T(2,128)(2,1)S(1)}, u32[]{:S(2)}, u32[]{:S(2)}) async-start(bf16[2048,3,64,2]{0,3,1,2:T(2,128)(2,1)} %copy.47), calls=%async_computation.1 | async-start | bytes 3145728 | tf_op jit(solution)/shard_map/all_to_all | solution.py:159
  162.2 2.8 %copy-start.8 = (f32[6,2,4,64]{3,2,1,0:T(4,128)S(1)}, f32[6,2,4,64]{3,2,1,0:T(4,128)}, u32[]{:S(2)}) copy-start(f32[6,2,4,64]{3,2,1,0:T(4,128)} %param.8) | copy-start | bytes 36868
  162.2 2.8 %copy-start.9 = (f32[6,2,4,64]{3,2,1,0:T(4,128)S(1)}, f32[6,2,4,64]{3,2,1,0:T(4,128)}, u32[]{:S(2)}) copy-start(f32[6,2,4,64]{3,2,1,0:T(4,128)} %param.9) | copy-start | bytes 36868
  162.2 2.8 %copy-start.10 = (f32[6,2,4,64]{3,2,1,0:T(4,128)S(1)}, f32[6,2,4,64]{3,2,1,0:T(4,128)}, u32[]{:S(2)}) copy-start(f32[6,2,4,64]{3,2,1,0:T(4,128)} %param.10) | copy-start | bytes 36868

commit v9 on v8

--- a/solution.py
+++ b/solution.py
@@ -50,32 +50,33 @@
     return lax.dot_general(a, b, (((1,), (0,)), ((), ())), preferred_element_type=jnp.float32)
 
 
-def grads_kernel(*refs, scale, pairs, n_minor, n_major, carry):
-    minor = refs[:n_minor]
-    major = refs[n_minor:n_minor + n_major]
-    noise_ref, spread_ref = refs[n_minor + n_major:n_minor + n_major + 2]
-    rest = refs[n_minor + n_major + 2:]
+def grads_kernel(minor_ref, *refs, scale, prods, outs, n_major, carry):
+    major = refs[:n_major]
+    noise_ref, spread_ref = refs[n_major:n_major + 2]
+    rest = refs[n_major + 2:]
     prev_ref = rest[0] if carry else None
-    out_ref, acc_ref = rest[-2], rest[-1]
+    out_ref = rest[-1 - len(prods)]
+    accs = rest[-len(prods):]
     step = pl.program_id(0)
-    nb, width = acc_ref.shape[1], acc_ref.shape[2]
+    n_s, nb, width, tb = minor_ref.shape
 
     @pl.when(step == 0)
     def _():
-        acc_ref[...] = jnp.zeros_like(acc_ref)
+        for acc in accs:
+            acc[...] = jnp.zeros_like(acc)
 
-    for b in range(nb):
-        cols = slice(b * width, (b + 1) * width)
-        for k, (f, lhs, rhs, flip) in enumerate(pairs):
-            acc_ref[k, b] += nn_dot(minor[0][lhs, b], major[rhs][:, cols])
+    lhs = minor_ref[...].reshape(n_s * nb * width, tb)
+    for k, (r0, rows, m) in enumerate(prods):
+        accs[k][...] += nn_dot(lhs[r0:r0 + rows], major[m][...])
 
     @pl.when(step == pl.num_programs(0) - 1)
     def _():
         done = set()
-        for k, (f, lhs, rhs, flip) in enumerate(pairs):
+        for f, k, r0, flip in outs:
             done.add(f)
+            full = accs[k][...]
             for b in range(nb):
-                grad = acc_ref[k, b]
+                grad = full[r0 + b * width:r0 + (b + 1) * width, b * width:(b + 1) * width]
                 if flip:
                     grad = grad.T
                 grad = grad * scale
@@ -87,14 +88,14 @@
                     out_ref[:, f] = prev_ref[:, f]
 
 
-def grads_and_curvature(minor, major, noise, spread, scale, pairs, prev=None):
-    n_minor, nb, width, tokens = minor.shape
+def grads_and_curvature(minor, major, noise, spread, scale, prods, outs, prev=None):
+    n_s, nb, width, tokens = minor.shape
     feats = major[0].shape[1]
     tb = min(TOKEN_BLOCK, tokens)
     whole4 = pl.BlockSpec(noise.shape, lambda i: (0, 0, 0, 0))
     whole5 = pl.BlockSpec((2,) + noise.shape, lambda i: (0, 0, 0, 0, 0))
     in_specs = (
-        [pl.BlockSpec((n_minor, nb, width, tb), lambda i: (0, 0, 0, i))]
+        [pl.BlockSpec((n_s, nb, width, tb), lambda i: (0, 0, 0, i))]
         + [pl.BlockSpec((tb, feats), lambda i: (i, 0))] * len(major)
         + [whole4, whole4]
     )
@@ -105,8 +106,7 @@
         aliases = {len(operands): 0}
         operands.append(prev)
     kernel = functools.partial(
-        grads_kernel, scale=scale, pairs=pairs, n_minor=1, n_major=len(major),
-        carry=prev is not None,
+        grads_kernel, scale=scale, prods=prods, outs=outs, n_major=len(major), carry=prev is not None,
     )
     return pl.pallas_call(
         kernel,
@@ -114,7 +114,7 @@
         in_specs=in_specs,
         out_specs=whole5,
         out_shape=jax.ShapeDtypeStruct((2,) + noise.shape, jnp.float32),
-        scratch_shapes=[pltpu.VMEM((len(pairs), nb, width, width), jnp.float32)],
+        scratch_shapes=[pltpu.VMEM((rows, feats), jnp.float32) for _, rows, _ in prods],
         input_output_aliases=aliases,
         compiler_params=pltpu.CompilerParams(dimension_semantics=("arbitrary",)),
     )(*operands)
@@ -153,16 +153,18 @@
     flat = lambda a: a.reshape(tokens, -1)
     first_t = token_minor(first)
     early = grads_and_curvature(
-        first_t, [flat(gate_grad), flat(value_grad), flat(hidden)],
-        noise, spread, scale, pairs=((1, 0, 0, False), (3, 1, 1, False), (4, 2, 2, True)),
+        first_t, [flat(gate_grad), flat(value_grad), flat(hidden)], noise, spread, scale,
+        prods=((0, 128, 0), (128, 128, 1), (256, 128, 2)),
+        outs=((1, 0, 0, False), (3, 1, 0, False), (4, 2, 0, True)),
     )
     second = lax.all_to_all(
         jnp.stack([outer, back_left, back_right], axis=1), "mp", split_axis=2, concat_axis=3, tiled=True
     )
     second_t = token_minor(second)
     stacked = grads_and_curvature(
-        second_t, [inputs, out_grad],
-        noise, spread, scale, pairs=((0, 1, 0, True), (2, 2, 0, True), (5, 0, 1, False)), prev=early,
+        second_t, [inputs, out_grad], noise, spread, scale,
+        prods=((128, 256, 0), (0, 128, 1)),
+        outs=((0, 0, 0, True), (2, 0, 128, True), (5, 1, 0, False)), prev=early,
     )
     sums = scatter_rows(stacked, groups)
     grad_avg = sums[0] / groups

time: 167 us -> 166 us (level)
  no operation moved by 1% of the time
where the time goes in v9:
time: 166 us
  blocking collectives  96 us (58%)
  waiting for transfers between devices  27.4 us (17%)
  local copies, waits for them, and re-layouts  20.2 us (12%)
  Pallas kernels  7.27 us (4%)
  starting transfers between devices  5.08 us (3%)
  matrix products  4.8 us (3%)
  other arithmetic  3.83 us (2%)
    all_to_all x1, blocking collectives, per_device(): lax.all_to_all(jnp.stack([y_left, y_right, back_outer], axis=1), 'mp', sp...  48.9 us
    all_to_all x1, waiting for transfers between devices, per_device(): lax.all_to_all(jnp.stack([outer, back_left, back_right], axis=1), 'mp', s...  27.4 us
    all_gather x1, blocking collectives, gather_rows(): full = lax.all_gather(moved, 'dp', axis=0, tiled=True)  26.6 us
    all_to_all x1, blocking collectives, scatter_rows(): got = lax.all_to_all(split, 'dp', split_axis=0, concat_axis=0, tiled=True)  20.5 us
    pallas_call x2, Pallas kernels, grads_and_curvature(): pl.pallas_call(kernel, grid=(tokens // tb,), in_specs=in_specs, out_specs...  7.27 us
    all_to_all x1, starting transfers between devices, per_device(): lax.all_to_all(jnp.stack([outer, back_left, back_right], axis=1), 'mp', s...  5.08 us
    dot_general x9, matrix products, bdot(): return jnp.einsum(form, left, right, preferred_element_type=jnp.float32)  4.8 us
    reshape x3, local copies, waits for them, and re-layouts, per_device(): flat = lambda a: a.reshape(tokens, -1)  4.04 us
  transfers between devices with their start and end apart: 1, of which 1 were waited for; matrix products, arithmetic and copies ran while one was open for 3% of the time, Pallas kernels for 2%

profile of v9, /device:TPU:1, one launch (start us, length us, event | category | flops | bytes accessed | tf_op | source)
XLA Modules:
  0.0 165.6 jit_solution(1821743571781116820)
XLA Ops:
  0.6 0.0 copy-start.3
  0.6 1.3 copy.38
  1.9 0.8 copy_bitcast_fusion.4
  2.8 26.6 %all_gather.3 = f32[64,2,6,2,64]{4,3,2,1,0:T(2,128)S(1)} all-gather(f32[4,2,6,2,64]{4,3,2,1,0:T(2,128)S(1)} %maximum_bitcast_fusion), channel_id=1, replica_groups=mesh['dp'=16,'mp'=32] {'dp'}, dimensions={0}, use_global_device_ids=true | all-gather | bytes 417792 | tf_op jit(solution)/shard_map/all_gather | solution.py:30
  29.4 0.2 copy.67
  29.6 0.0 copy-start.1
  29.6 0.9 copy-done.1
  30.5 0.0 copy-done.3
  30.5 0.0 copy-start.4
  30.5 0.2 fusion.11
  30.6 0.0 copy-start.6
  30.7 0.3 fusion.1
  31.0 0.3 fusion
  31.4 0.1 copy-done.4
  31.5 0.2 copy.41
  31.7 0.0 copy-done.6
  31.7 0.3 fusion.2
  32.0 0.2 pad_maximum_fusion
  32.2 1.6 copy.42
  33.8 48.9 %all_to_all.41 = bf16[2048,3,64,2]{0,3,1,2:T(2,128)(2,1)S(1)} all-to-all(bf16[2048,3,64,2]{0,3,1,2:T(2,128)(2,1)S(1)} %copy.42), channel_id=1, replica_groups=mesh['dp'=16,'mp'=32] {'mp'}, dimensions={2} | all-to-all | bytes 3145728 | tf_op jit(solution)/shard_map/all_to_all | solution.py:139
  82.7 1.3 copy.65
  84.0 0.6 all_to_all.32
  84.6 0.0 copy-start
  84.6 0.0 copy-start.7
  84.6 1.1 convolution_bitcast_fusion
  85.8 1.1 convolution_bitcast_fusion.2
  86.9 0.0 copy-done
  86.9 0.0 copy-done.7
  86.9 0.7 multiply_convert_fusion.2
  87.6 0.0 copy-start.5
  87.6 0.3 fusion.3
  88.0 0.3 fusion.4
  88.3 0.3 fusion.5
  88.5 0.2 pad_maximum_fusion.1
  88.7 0.0 copy-done.5
  88.7 2.8 %copy.47 = bf16[2048,3,64,2]{0,3,1,2:T(2,128)(2,1)} copy(bf16[2048,3,64,2]{0,2,3,1:T(8,128)(2,1)S(1)} %pad_maximum_fusion.1) | data formatting | bytes 3145728 | tf_op jit(solution)/shard_map/stack | solution.py:161
  91.5 0.0 copy-start.2
  91.5 5.1 %all-to-all-start.1 = ((bf16[2048,3,64,2]{0,3,1,2:T(2,128)(2,1)}), bf16[2048,3,64,2]{0,3,1,2:T(2,128)(2,1)S(1)}, u32[]{:S(2)}, u32[]{:S(2)}) async-start(bf16[2048,3,64,2]{0,3,1,2:T(2,128)(2,1)} %copy.47), calls=%async_computation.1 | async-start | bytes 3145728 | tf_op jit(solution)/shard_map/all_to_all | solution.py:160
  96.6 0.0 copy-done.2
  96.6 0.9 fusion.9.refs_4_.refs_3_
  97.5 2.0 %copy.50.refs_1_ = bf16[2048,128]{1,0:T(8,128)(2,1)} copy(bf16[2048,128]{0,1:T(8,128)(2,1)} %bitcast.151) | data formatting | bytes 1048576 | tf_op jit(solution)/shard_map/reshape | solution.py:153
  99.5 1.0 copy.49.refs_0_
  100.5 1.0 copy.51.refs_2_
  101.5 3.5 %shard_map.85.refs_4_ = f32[2,6,2,64,64]{4,3,2,1,0:T(8,128)} custom-call(bf16[3,2,64,2048]{3,2,1,0:T(8,128)(2,1)} %bitcast.135, bf16[2048,128]{1,0:T(8,128)(2,1)} %copy.49.refs_0_, bf16[2048,128]{1,0:T(8,128)(2,1)} %copy.50.refs_1_, bf16[2048,128]{1,0:T(8,128)(2,1)} %copy.51.refs_2_, f32[6,2,64,64]{3,2,1,0:T(8,128)} %bitcast.146, ...), custom_call_target="tpu_custom_call" | custom-call | tf_op jit(solution)/shard_map/pallas_call | solution.py:111
  105.1 27.4 %all-to-all-done.1 = bf16[2048,3,64,2]{0,3,1,2:T(2,128)(2,1)S(1)} async-done(((bf16[2048,3,64,2]{0,3,1,2:T(2,128)(2,1)}), bf16[2048,3,64,2]{0,3,1,2:T(2,128)(2,1)S(1)}, u32[]{:S(2)}, u32[]{:S(2)}) %all-to-all-start.1) | async-done | bytes 1572896 | tf_op jit(solution)/shard_map/all_to_all | solution.py:160
  132.5 1.3 copy.64
  133.7 2.0 %all_to_all.36 = bf16[2048,3,2,64]{0,3,2,1:T(8,128)(2,1)} reshape(bf16[2048,3,2,32,2]{0,4,3,2,1:T(2,128)(2,1)S(1)} %bitcast.141) | data formatting | bytes 3145728 | tf_op jit(solution)/shard_map/all_to_all | solution.py:160
  135.8 3.7 %shard_map.86 = f32[2,6,2,64,64]{4,3,2,1,0:T(8,128)} custom-call(bf16[3,2,64,2048]{3,2,1,0:T(8,128)(2,1)} %bitcast.138, bf16[2048,128]{1,0:T(8,128)(2,1)} %refs_0_.1, bf16[2048,128]{1,0:T(8,128)(2,1)} %refs_1_.1, f32[6,2,64,64]{3,2,1,0:T(8,128)} %bitcast.147, f32[6,2,64,64]{3,2,1,0:T(8,128)} %fusion.9.refs_4_.refs_3_, ...), custom_call_target="tpu_custom_call", output_to_operand_aliasing={{}: (5, {})} | custom-call | tf_op jit(solution)/shard_map/pallas_call | solution.py:111
  139.5 1.3 copy.66
  140.8 0.7 reshape.41
  141.6 20.5 %all_to_all.42 = f32[16,1,6144]{2,1,0:T(1,128)S(1)} all-to-all(f32[16,1,6144]{2,1,0:T(1,128)S(1)} %reshape.41), channel_id=1, replica_groups=mesh['dp'=16,'mp'=32] {'dp'}, dimensions={0} | all-to-all | bytes 786432 | tf_op jit(solution)/shard_map/all_to_all | solution.py:39
  162.1 0.0 copy-start.8
  162.1 0.0 copy-start.9
  162.1 0.0 copy-start.10
  162.1 0.5 broadcast.39
  162.6 1.6 reduce
  164.2 0.5 reshape.42
  164.7 0.2 reduce_sum.9
  164.9 0.0 copy-done.8
  164.9 0.0 copy-done.9
  164.9 0.0 copy-done.10
  164.9 0.7 divide_subtract_fusion
  (1 shorter events, 0.0 us)
Async XLA Ops:
  0.6 29.8 %copy-start.3 = (f32[1,6,2,64,64]{4,3,2,1,0:T(8,128)S(1)}, f32[1,6,2,64,64]{4,3,2,1,0:T(8,128)}, u32[]{:S(2)}) copy-start(f32[1,6,2,64,64]{4,3,2,1,0:T(8,128)} %param.11) | copy-start | bytes 589828
  29.6 0.9 copy-start.1
  30.5 1.0 copy-start.4
  30.6 1.1 copy-start.6
  84.6 2.3 %copy-start = (bf16[2048,3,2,64]{0,3,2,1:T(8,128)(2,1)}, bf16[2048,3,2,64]{0,3,2,1:T(8,128)(2,1)S(1)}, u32[]{:S(2)}) copy-start(bf16[2048,3,2,64]{0,3,2,1:T(8,128)(2,1)S(1)} %all_to_all.32) | copy-start | bytes 4718596
  84.6 2.3 %copy-start.7 = (bf16[6,2,64,64]{3,2,1,0:T(8,128)(2,1)S(1)}, bf16[6,2,64,64]{3,2,1,0:T(8,128)(2,1)}, u32[]{:S(2)}) copy-start(bf16[6,2,64,64]{3,2,1,0:T(8,128)(2,1)} %copy-done.6) | copy-start | bytes 294916
  87.6 1.1 copy-start.5
  91.5 5.1 %copy-start.2 = (f32[64,2,6,2,64]{4,0,3,2,1:T(8,128)S(1)}, f32[64,2,6,2,64]{4,0,3,2,1:T(8,128)}, u32[]{:S(2)}) copy-start(f32[64,2,6,2,64]{4,0,3,2,1:T(8,128)} %copy-done.1) | copy-start | bytes 1179652
  91.5 41.0 %all-to-all-start.1 = ((bf16[2048,3,64,2]{0,3,1,2:T(2,128)(2,1)}), bf16[2048,3,64,2]{0,3,1,2:T(2,128)(2,1)S(1)}, u32[]{:S(2)}, u32[]{:S(2)}) async-start(bf16[2048,3,64,2]{0,3,1,2:T(2,128)(2,1)} %copy.47), calls=%async_computation.1 | async-start | bytes 3145728 | tf_op jit(solution)/shard_map/all_to_all | solution.py:160
  162.1 2.8 %copy-start.8 = (f32[6,2,4,64]{3,2,1,0:T(4,128)S(1)}, f32[6,2,4,64]{3,2,1,0:T(4,128)}, u32[]{:S(2)}) copy-start(f32[6,2,4,64]{3,2,1,0:T(4,128)} %param.8) | copy-start | bytes 36868
  162.1 2.8 %copy-start.9 = (f32[6,2,4,64]{3,2,1,0:T(4,128)S(1)}, f32[6,2,4,64]{3,2,1,0:T(4,128)}, u32[]{:S(2)}) copy-start(f32[6,2,4,64]{3,2,1,0:T(4,128)} %param.9) | copy-start | bytes 36868
  162.1 2.8 %copy-start.10 = (f32[6,2,4,64]{3,2,1,0:T(4,128)S(1)}, f32[6,2,4,64]{3,2,1,0:T(4,128)}, u32[]{:S(2)}) copy-start(f32[6,2,4,64]{3,2,1,0:T(4,128)} %param.10) | copy-start | bytes 36868

commit v10 on v9

--- a/solution.py
+++ b/solution.py
@@ -50,13 +50,13 @@
     return lax.dot_general(a, b, (((1,), (0,)), ((), ())), preferred_element_type=jnp.float32)
 
 
-def grads_kernel(minor_ref, *refs, scale, prods, outs, n_major, carry):
+def grads_kernel(minor_ref, *refs, scale, prods, outs, n_major):
+    n_out = len(outs)
     major = refs[:n_major]
-    noise_ref, spread_ref = refs[n_major:n_major + 2]
-    rest = refs[n_major + 2:]
-    prev_ref = rest[0] if carry else None
-    out_ref = rest[-1 - len(prods)]
-    accs = rest[-len(prods):]
+    noise_refs = refs[n_major:n_major + n_out]
+    spread_refs = refs[n_major + n_out:n_major + 2 * n_out]
+    out_ref = refs[n_major + 2 * n_out]
+    accs = refs[n_major + 2 * n_out + 1:]
     step = pl.program_id(0)
     n_s, nb, width, tb = minor_ref.shape
 
@@ -71,51 +71,37 @@
 
     @pl.when(step == pl.num_programs(0) - 1)
     def _():
-        done = set()
-        for f, k, r0, flip in outs:
-            done.add(f)
+        for q, (k, r0, flip) in enumerate(outs):
             full = accs[k][...]
             for b in range(nb):
                 grad = full[r0 + b * width:r0 + (b + 1) * width, b * width:(b + 1) * width]
                 if flip:
                     grad = grad.T
                 grad = grad * scale
-                out_ref[0, f, b] = grad
-                out_ref[1, f, b] = grad * noise_ref[f, b] * spread_ref[f, b]
-        if carry:
-            for f in range(noise_ref.shape[0]):
-                if f not in done:
-                    out_ref[:, f] = prev_ref[:, f]
+                out_ref[0, q, b] = grad
+                out_ref[1, q, b] = grad * noise_refs[q][0, b] * spread_refs[q][0, b]
 
 
-def grads_and_curvature(minor, major, noise, spread, scale, prods, outs, prev=None):
+def grads_and_curvature(minor, major, noise, spread, scale, prods, outs, factors):
     n_s, nb, width, tokens = minor.shape
     feats = major[0].shape[1]
     tb = min(TOKEN_BLOCK, tokens)
-    whole4 = pl.BlockSpec(noise.shape, lambda i: (0, 0, 0, 0))
-    whole5 = pl.BlockSpec((2,) + noise.shape, lambda i: (0, 0, 0, 0, 0))
+    shape = (len(factors), nb, width, width)
+    picks = [pl.BlockSpec((1, nb, width, width), lambda i, f=f: (f, 0, 0, 0)) for f in factors]
     in_specs = (
         [pl.BlockSpec((n_s, nb, width, tb), lambda i: (0, 0, 0, i))]
         + [pl.BlockSpec((tb, feats), lambda i: (i, 0))] * len(major)
-        + [whole4, whole4]
+        + picks + picks
     )
-    operands = [minor] + list(major) + [noise, spread]
-    aliases = {}
-    if prev is not None:
-        in_specs.append(whole5)
-        aliases = {len(operands): 0}
-        operands.append(prev)
-    kernel = functools.partial(
-        grads_kernel, scale=scale, prods=prods, outs=outs, n_major=len(major), carry=prev is not None,
-    )
+    operands = [minor] + list(major) + [noise] * len(factors) + [spread] * len(factors)
+    kernel = functools.partial(grads_kernel, scale=scale, prods=prods, outs=outs, n_major=len(major))
     return pl.pallas_call(
         kernel,
         grid=(tokens // tb,),
         in_specs=in_specs,
-        out_specs=whole5,
-        out_shape=jax.ShapeDtypeStruct((2,) + noise.shape, jnp.float32),
+        out_specs=pl.BlockSpec((2,) + shape, lambda i: (0, 0, 0, 0, 0)),
+        out_shape=jax.ShapeDtypeStruct((2,) + shape, jnp.float32),
         scratch_shapes=[pltpu.VMEM((rows, feats), jnp.float32) for _, rows, _ in prods],
-        input_output_aliases=aliases,
         compiler_params=pltpu.CompilerParams(dimension_semantics=("arbitrary",)),
     )(*operands)
 
@@ -155,16 +141,19 @@
     early = grads_and_curvature(
         first_t, [flat(gate_grad), flat(value_grad), flat(hidden)], noise, spread, scale,
         prods=((0, 128, 0), (128, 128, 1), (256, 128, 2)),
-        outs=((1, 0, 0, False), (3, 1, 0, False), (4, 2, 0, True)),
+        outs=((0, 0, False), (1, 0, False), (2, 0, True)), factors=(1, 3, 4),
     )
     second = lax.all_to_all(
         jnp.stack([outer, back_left, back_right], axis=1), "mp", split_axis=2, concat_axis=3, tiled=True
     )
     second_t = token_minor(second)
-    stacked = grads_and_curvature(
+    late = grads_and_curvature(
         second_t, [inputs, out_grad], noise, spread, scale,
         prods=((128, 256, 0), (0, 128, 1)),
-        outs=((0, 0, 0, True), (2, 0, 128, True), (5, 1, 0, False)), prev=early,
+        outs=((0, 0, True), (0, 128, True), (1, 0, False)), factors=(0, 2, 5),
+    )
+    stacked = jnp.concatenate(
+        [late[:, 0:1], early[:, 0:1], late[:, 1:2], early[:, 1:2], early[:, 2:3], late[:, 2:3]], axis=1
     )
     sums = scatter_rows(stacked, groups)
     grad_avg = sums[0] / groups

time: 166 us -> 167 us (level)
  local copies, waits for them, and re-layouts: 20.2 us -> 22.1 us
    unnamed x26 -> x32, local copies, waits for them, and re-layouts: 3.82 us -> 5.85 us
where the time goes in v10:
time: 167 us; the launch traced here: 166 us
  blocking collectives  96 us (57%)
  waiting for transfers between devices  27.6 us (17%)
  local copies, waits for them, and re-layouts  22.1 us (13%)
  Pallas kernels  6.47 us (4%)
  starting transfers between devices  5.08 us (3%)
  matrix products  3.97 us (2%)
  other arithmetic  3.83 us (2%)
    all_to_all x1, blocking collectives, per_device(): lax.all_to_all(jnp.stack([y_left, y_right, back_outer], axis=1), 'mp', sp...  48.9 us
    all_to_all x1, waiting for transfers between devices, per_device(): lax.all_to_all(jnp.stack([outer, back_left, back_right], axis=1), 'mp', s...  27.6 us
    all_gather x1, blocking collectives, gather_rows(): full = lax.all_gather(moved, 'dp', axis=0, tiled=True)  26.6 us
    all_to_all x1, blocking collectives, scatter_rows(): got = lax.all_to_all(split, 'dp', split_axis=0, concat_axis=0, tiled=True)  20.5 us
    pallas_call x2, Pallas kernels, grads_and_curvature(): pl.pallas_call(kernel, grid=(tokens // tb,), in_specs=in_specs, out_specs...  6.47 us
    unnamed x32, local copies, waits for them, and re-layouts  5.85 us
    all_to_all x1, starting transfers between devices, per_device(): lax.all_to_all(jnp.stack([outer, back_left, back_right], axis=1), 'mp', s...  5.08 us
    reshape x3, local copies, waits for them, and re-layouts, per_device(): flat = lambda a: a.reshape(tokens, -1)  4.07 us
  transfers between devices with their start and end apart: 1, of which 1 were waited for; matrix products, arithmetic and copies ran while one was open for 3% of the time, Pallas kernels for 2%

profile of v10, /device:TPU:1, one launch (start us, length us, event | category | flops | bytes accessed | tf_op | source)
XLA Modules:
  0.0 166.0 jit_solution(17204871926832096964)
XLA Ops:
  0.6 0.0 copy-start
  0.6 1.3 copy.37
  1.9 0.8 copy_bitcast_fusion.4
  2.8 26.6 %all_gather.3 = f32[64,2,6,2,64]{4,3,2,1,0:T(2,128)S(1)} all-gather(f32[4,2,6,2,64]{4,3,2,1,0:T(2,128)S(1)} %maximum_bitcast_fusion), channel_id=1, replica_groups=mesh['dp'=16,'mp'=32] {'dp'}, dimensions={0}, use_global_device_ids=true | all-gather | bytes 417792 | tf_op jit(solution)/shard_map/all_gather | solution.py:30
  29.4 0.2 copy.66
  29.6 0.0 copy-start.2
  29.6 0.0 copy-done
  29.6 0.0 copy-start.5
  29.6 0.2 fusion.11
  29.8 0.7 copy-done.2
  30.5 0.0 copy-start.7
  30.5 0.3 fusion.1
  30.8 0.3 fusion
  31.2 0.0 copy-done.5
  31.2 0.2 copy.40
  31.4 0.3 fusion.2
  31.7 0.2 pad_maximum_fusion
  31.9 1.6 copy.41
  33.5 48.9 %all_to_all.41 = bf16[2048,3,64,2]{0,3,1,2:T(2,128)(2,1)S(1)} all-to-all(bf16[2048,3,64,2]{0,3,1,2:T(2,128)(2,1)S(1)} %copy.41), channel_id=1, replica_groups=mesh['dp'=16,'mp'=32] {'mp'}, dimensions={2} | all-to-all | bytes 3145728 | tf_op jit(solution)/shard_map/all_to_all | solution.py:125
  82.4 1.3 copy.64
  83.6 0.6 all_to_all.32
  84.3 0.0 copy-start.1
  84.3 0.3 convolution_bitcast_fusion
  84.6 0.0 copy-done.7
  84.6 0.3 convolution_bitcast_fusion.2
  84.9 0.5 copy-done.1
  85.4 0.0 copy-start.8
  85.4 1.5 multiply_convert_fusion.2
  87.0 0.0 copy-start.4
  87.0 0.0 copy-done.8
  87.0 0.3 fusion.3
  87.3 0.3 fusion.4
  87.6 0.3 fusion.5
  87.9 0.2 pad_maximum_fusion.1
  88.1 0.0 copy-done.4
  88.1 2.8 %copy.46 = bf16[2048,3,64,2]{0,3,1,2:T(2,128)(2,1)} copy(bf16[2048,3,64,2]{0,2,3,1:T(8,128)(2,1)S(1)} %pad_maximum_fusion.1) | data formatting | bytes 3145728 | tf_op jit(solution)/shard_map/stack | solution.py:147
  90.9 0.0 copy-start.3
  90.9 5.1 %all-to-all-start.1 = ((bf16[2048,3,64,2]{0,3,1,2:T(2,128)(2,1)}), bf16[2048,3,64,2]{0,3,1,2:T(2,128)(2,1)S(1)}, u32[]{:S(2)}, u32[]{:S(2)}) async-start(bf16[2048,3,64,2]{0,3,1,2:T(2,128)(2,1)} %copy.46), calls=%async_computation.1 | async-start | bytes 3145728 | tf_op jit(solution)/shard_map/all_to_all | solution.py:146
  95.9 0.0 copy-done.3
  95.9 0.9 fusion.9.refs_5_.refs_6_.refs_7_.refs_8_
  96.8 2.1 %copy.49.refs_1_ = bf16[2048,128]{1,0:T(8,128)(2,1)} copy(bf16[2048,128]{0,1:T(8,128)(2,1)} %bitcast.154) | data formatting | bytes 1048576 | tf_op jit(solution)/shard_map/reshape | solution.py:139
  98.9 1.0 copy.48.refs_0_
  99.9 1.0 copy.50.refs_2_
  100.9 3.3 %shard_map.86 = f32[2,3,2,64,64]{4,3,2,1,0:T(8,128)} custom-call(bf16[3,2,64,2048]{3,2,1,0:T(8,128)(2,1)} %bitcast.141, bf16[2048,128]{1,0:T(8,128)(2,1)} %copy.48.refs_0_, bf16[2048,128]{1,0:T(8,128)(2,1)} %copy.49.refs_1_, bf16[2048,128]{1,0:T(8,128)(2,1)} %copy.50.refs_2_, f32[6,2,64,64]{3,2,1,0:T(8,128)} %bitcast.135, f32[6,2,64,64]{3,2,1,0:T(8,128)} %bitcast.136, ...), custom_call_target="tpu_custom_call" | custom-call | tf_op jit(solution)/shard_map/pallas_call | solution.py:98
  104.2 27.6 %all-to-all-done.1 = bf16[2048,3,64,2]{0,3,1,2:T(2,128)(2,1)S(1)} async-done(((bf16[2048,3,64,2]{0,3,1,2:T(2,128)(2,1)}), bf16[2048,3,64,2]{0,3,1,2:T(2,128)(2,1)S(1)}, u32[]{:S(2)}, u32[]{:S(2)}) %all-to-all-start.1) | async-done | bytes 1572896 | tf_op jit(solution)/shard_map/all_to_all | solution.py:146
  131.8 1.3 copy.63
  133.1 2.0 %all_to_all.36 = bf16[2048,3,2,64]{0,3,2,1:T(8,128)(2,1)} reshape(bf16[2048,3,2,32,2]{0,4,3,2,1:T(2,128)(2,1)S(1)} %bitcast.145) | data formatting | bytes 3145728 | tf_op jit(solution)/shard_map/all_to_all | solution.py:146
  135.1 0.0 copy-start.6
  135.1 3.2 %shard_map.85 = f32[2,3,2,64,64]{4,3,2,1,0:T(8,128)} custom-call(bf16[3,2,64,2048]{3,2,1,0:T(8,128)(2,1)} %bitcast.146, bf16[2048,128]{1,0:T(8,128)(2,1)} %refs_0_.1, bf16[2048,128]{1,0:T(8,128)(2,1)} %refs_1_.1, f32[6,2,64,64]{3,2,1,0:T(8,128)} %bitcast.138, f32[6,2,64,64]{3,2,1,0:T(8,128)} %bitcast.139, f32[6,2,64,64]{3,2,1,0:T(8,128)} %bitcast.140, ...), custom_call_target="tpu_custom_call" | custom-call | tf_op jit(solution)/shard_map/pallas_call | solution.py:98
  138.3 0.9 slice_dynamic-update-slice_fusion.4
  139.2 0.0 copy-done.6
  139.2 0.9 slice_dynamic-update-slice_fusion.2
  140.2 0.9 slice_dynamic-update-slice_fusion.1
  141.1 0.2 copy.65
  141.3 0.7 reshape.41
  142.0 20.5 %all_to_all.42 = f32[16,1,6144]{2,1,0:T(1,128)S(1)} all-to-all(f32[16,1,6144]{2,1,0:T(1,128)S(1)} %reshape.41), channel_id=1, replica_groups=mesh['dp'=16,'mp'=32] {'dp'}, dimensions={0} | all-to-all | bytes 786432 | tf_op jit(solution)/shard_map/all_to_all | solution.py:39
  162.6 0.5 broadcast.39
  163.1 1.6 reduce
  164.7 0.5 reshape.42
  165.2 0.2 reduce_sum.9
  165.4 0.0 copy-done.9
  165.4 0.0 copy-done.10
  165.4 0.0 copy-done.11
  165.4 0.7 divide_subtract_fusion
  (6 shorter events, 0.1 us)
Async XLA Ops:
  0.6 29.0 %copy-start = (f32[1,6,2,64,64]{4,3,2,1,0:T(8,128)S(1)}, f32[1,6,2,64,64]{4,3,2,1,0:T(8,128)}, u32[]{:S(2)}) copy-start(f32[1,6,2,64,64]{4,3,2,1,0:T(8,128)} %param.11) | copy-start | bytes 589828
  29.6 0.9 copy-start.2
  29.6 1.6 copy-start.5
  30.5 54.1 %copy-start.7 = (bf16[6,2,64,64]{3,2,1,0:T(8,128)(2,1)}, bf16[6,2,64,64]{3,2,1,0:T(8,128)(2,1)S(1)}, u32[]{:S(2)}) copy-start(bf16[6,2,64,64]{3,2,1,0:T(8,128)(2,1)S(1)} %fusion.11) | copy-start | bytes 294916
  84.3 1.2 copy-start.1
  85.4 1.5 copy-start.8
  87.0 1.1 copy-start.4
  90.9 5.1 %copy-start.3 = (f32[64,2,6,2,64]{4,0,3,2,1:T(8,128)S(1)}, f32[64,2,6,2,64]{4,0,3,2,1:T(8,128)}, u32[]{:S(2)}) copy-start(f32[64,2,6,2,64]{4,0,3,2,1:T(8,128)} %copy-done.2) | copy-start | bytes 1179652
  90.9 40.9 %all-to-all-start.1 = ((bf16[2048,3,64,2]{0,3,1,2:T(2,128)(2,1)}), bf16[2048,3,64,2]{0,3,1,2:T(2,128)(2,1)S(1)}, u32[]{:S(2)}, u32[]{:S(2)}) async-start(bf16[2048,3,64,2]{0,3,1,2:T(2,128)(2,1)} %copy.46), calls=%async_computation.1 | async-start | bytes 3145728 | tf_op jit(solution)/shard_map/all_to_all | solution.py:146
  135.1 4.1 %copy-start.6 = (f32[2,3,2,64,64]{4,3,2,1,0:T(8,128)S(1)}, f32[2,3,2,64,64]{4,3,2,1,0:T(8,128)}, u32[]{:S(2)}) copy-start(f32[2,3,2,64,64]{4,3,2,1,0:T(8,128)} %shard_map.86) | copy-start | bytes 589828
  162.6 2.8 %copy-start.9 = (f32[6,2,4,64]{3,2,1,0:T(4,128)S(1)}, f32[6,2,4,64]{3,2,1,0:T(4,128)}, u32[]{:S(2)}) copy-start(f32[6,2,4,64]{3,2,1,0:T(4,128)} %param.8) | copy-start | bytes 36868
  162.6 2.8 %copy-start.10 = (f32[6,2,4,64]{3,2,1,0:T(4,128)S(1)}, f32[6,2,4,64]{3,2,1,0:T(4,128)}, u32[]{:S(2)}) copy-start(f32[6,2,4,64]{3,2,1,0:T(4,128)} %param.9) | copy-start | bytes 36868
  162.6 2.8 %copy-start.11 = (f32[6,2,4,64]{3,2,1,0:T(4,128)S(1)}, f32[6,2,4,64]{3,2,1,0:T(4,128)}, u32[]{:S(2)}) copy-start(f32[6,2,4,64]{3,2,1,0:T(4,128)} %param.10) | copy-start | bytes 36868

commit v11 on v8

--- a/solution.py
+++ b/solution.py
@@ -36,8 +36,9 @@
     split = stacked.reshape(s, f, b, groups, r // groups, w)
     split = jnp.moveaxis(split, 3, 0)
     if REDUCE_MODE == "a2a":
-        got = lax.all_to_all(split, "dp", split_axis=0, concat_axis=0, tiled=True)
-        summed = jnp.sum(got, axis=0)
+        dense = split.reshape(groups, -1, 128)
+        got = lax.all_to_all(dense, "dp", split_axis=0, concat_axis=0, tiled=True)
+        summed = jnp.sum(got, axis=0).reshape(split.shape[1:])
     else:
         summed = lax.psum_scatter(split, "dp", scatter_dimension=0, tiled=False)
     return summed

time: 167 us -> 164 us (0.982)
  other arithmetic: 3.83 us -> 2.11 us
    unnamed x26 -> x24, local copies, waits for them, and re-layouts: 3.82 us -> 2.6 us
where the time goes in v11:
time: 164 us; the launch traced here: 163 us
  blocking collectives  96 us (59%)
  waiting for transfers between devices  27.2 us (17%)
  local copies, waits for them, and re-layouts  19.2 us (12%)
  Pallas kernels  7.5 us (5%)
  starting transfers between devices  5.07 us (3%)
  matrix products  4.8 us (3%)
  other arithmetic  2.11 us (1%)
    all_to_all x1, blocking collectives, per_device(): lax.all_to_all(jnp.stack([y_left, y_right, back_outer], axis=1), 'mp', sp...  48.9 us
    all_to_all x1, waiting for transfers between devices, per_device(): lax.all_to_all(jnp.stack([outer, back_left, back_right], axis=1), 'mp', s...  27.2 us
    all_gather x1, blocking collectives, gather_rows(): full = lax.all_gather(moved, 'dp', axis=0, tiled=True)  26.6 us
    all_to_all x1, blocking collectives, scatter_rows(): got = lax.all_to_all(dense, 'dp', split_axis=0, concat_axis=0, tiled=True)  20.5 us
    pallas_call x2, Pallas kernels, grads_and_curvature(): pl.pallas_call(kernel, grid=(tokens // tb,), in_specs=in_specs, out_specs...  7.5 us
    all_to_all x1, starting transfers between devices, per_device(): lax.all_to_all(jnp.stack([outer, back_left, back_right], axis=1), 'mp', s...  5.07 us
    dot_general x9, matrix products, bdot(): return jnp.einsum(form, left, right, preferred_element_type=jnp.float32)  4.8 us
    reshape x3, local copies, waits for them, and re-layouts, per_device(): flat = lambda a: a.reshape(tokens, -1)  4.1 us
  transfers between devices with their start and end apart: 1, of which 1 were waited for; matrix products, arithmetic and copies ran while one was open for 3% of the time, Pallas kernels for 2%

profile of v11, /device:TPU:1, one launch (start us, length us, event | category | flops | bytes accessed | tf_op | source)
XLA Modules:
  0.0 162.9 jit_solution(18191479403179693994)
XLA Ops:
  0.6 0.0 copy-start.3
  0.6 1.3 copy.39
  1.9 0.8 copy_bitcast_fusion.4
  2.8 26.6 %all_gather.3 = f32[64,2,6,2,64]{4,3,2,1,0:T(2,128)S(1)} all-gather(f32[4,2,6,2,64]{4,3,2,1,0:T(2,128)S(1)} %maximum_bitcast_fusion), channel_id=1, replica_groups=mesh['dp'=16,'mp'=32] {'dp'}, dimensions={0}, use_global_device_ids=true | all-gather | bytes 417792 | tf_op jit(solution)/shard_map/all_gather | solution.py:30
  29.4 0.2 copy.68
  29.6 0.0 copy-start.1
  29.6 0.9 copy-done.1
  30.5 0.0 copy-done.3
  30.5 0.0 copy-start.4
  30.5 0.2 fusion.11
  30.7 0.0 copy-start.6
  30.7 0.3 fusion.1
  31.0 0.3 fusion
  31.4 0.2 copy-done.4
  31.5 0.2 copy.42
  31.7 0.0 copy-done.6
  31.7 0.3 fusion.2
  32.0 0.2 pad_maximum_fusion
  32.2 1.6 copy.43
  33.8 48.9 %all_to_all.41 = bf16[2048,3,64,2]{0,3,1,2:T(2,128)(2,1)S(1)} all-to-all(bf16[2048,3,64,2]{0,3,1,2:T(2,128)(2,1)S(1)} %copy.43), channel_id=1, replica_groups=mesh['dp'=16,'mp'=32] {'mp'}, dimensions={2} | all-to-all | bytes 3145728 | tf_op jit(solution)/shard_map/all_to_all | solution.py:140
  82.7 1.3 copy.66
  84.0 0.6 all_to_all.32
  84.6 0.0 copy-start
  84.6 0.0 copy-start.7
  84.6 1.2 convolution_bitcast_fusion
  85.8 1.1 convolution_bitcast_fusion.2
  86.9 0.0 copy-done
  86.9 0.0 copy-done.7
  86.9 0.7 multiply_convert_fusion.2
  87.6 0.0 copy-start.5
  87.6 0.3 fusion.3
  88.0 0.3 fusion.4
  88.3 0.3 fusion.5
  88.6 0.2 pad_maximum_fusion.1
  88.7 0.0 copy-done.5
  88.7 2.8 %copy.48 = bf16[2048,3,64,2]{0,3,1,2:T(2,128)(2,1)} copy(bf16[2048,3,64,2]{0,2,3,1:T(8,128)(2,1)S(1)} %pad_maximum_fusion.1) | data formatting | bytes 3145728 | tf_op jit(solution)/shard_map/stack | solution.py:161
  91.5 0.0 copy-start.2
  91.5 5.1 %all-to-all-start.1 = ((bf16[2048,3,64,2]{0,3,1,2:T(2,128)(2,1)}), bf16[2048,3,64,2]{0,3,1,2:T(2,128)(2,1)S(1)}, u32[]{:S(2)}, u32[]{:S(2)}) async-start(bf16[2048,3,64,2]{0,3,1,2:T(2,128)(2,1)} %copy.48), calls=%async_computation.1 | async-start | bytes 3145728 | tf_op jit(solution)/shard_map/all_to_all | solution.py:160
  96.6 0.0 copy-done.2
  96.6 0.9 fusion.9.refs_5_.refs_4_
  97.5 2.0 %copy.51.refs_2_ = bf16[2048,128]{1,0:T(8,128)(2,1)} copy(bf16[2048,128]{0,1:T(8,128)(2,1)} %bitcast.130) | data formatting | bytes 1048576 | tf_op jit(solution)/shard_map/reshape | solution.py:154
  99.5 1.0 copy.50.refs_1_
  100.6 1.0 copy.52.refs_3_
  101.6 3.6 %shard_map.85.refs_5_ = f32[2,6,2,64,64]{4,3,2,1,0:T(8,128)} custom-call(bf16[3,2,64,2048]{3,2,1,0:T(8,128)(2,1)} %bitcast.114, bf16[2048,128]{1,0:T(8,128)(2,1)} %copy.50.refs_1_, bf16[2048,128]{1,0:T(8,128)(2,1)} %copy.51.refs_2_, bf16[2048,128]{1,0:T(8,128)(2,1)} %copy.52.refs_3_, f32[6,2,64,64]{3,2,1,0:T(8,128)} %bitcast.125, ...), custom_call_target="tpu_custom_call" | custom-call | tf_op jit(solution)/shard_map/pallas_call | solution.py:112
  105.2 27.2 %all-to-all-done.1 = bf16[2048,3,64,2]{0,3,1,2:T(2,128)(2,1)S(1)} async-done(((bf16[2048,3,64,2]{0,3,1,2:T(2,128)(2,1)}), bf16[2048,3,64,2]{0,3,1,2:T(2,128)(2,1)S(1)}, u32[]{:S(2)}, u32[]{:S(2)}) %all-to-all-start.1) | async-done | bytes 1572896 | tf_op jit(solution)/shard_map/all_to_all | solution.py:160
  132.5 1.3 copy.65
  133.7 2.0 %all_to_all.36 = bf16[2048,3,2,64]{0,3,2,1:T(8,128)(2,1)} reshape(bf16[2048,3,2,32,2]{0,4,3,2,1:T(2,128)(2,1)S(1)} %bitcast.120) | data formatting | bytes 3145728 | tf_op jit(solution)/shard_map/all_to_all | solution.py:160
  135.8 3.9 %shard_map.86 = f32[2,6,2,64,64]{4,3,2,1,0:T(8,128)} custom-call(bf16[3,2,64,2048]{3,2,1,0:T(8,128)(2,1)} %bitcast.117, bf16[2048,128]{1,0:T(8,128)(2,1)} %refs_1_.1, bf16[2048,128]{1,0:T(8,128)(2,1)} %refs_2_.1, f32[6,2,64,64]{3,2,1,0:T(8,128)} %bitcast.126, f32[6,2,64,64]{3,2,1,0:T(8,128)} %fusion.9.refs_5_.refs_4_, ...), custom_call_target="tpu_custom_call", output_to_operand_aliasing={{}: (5, {})} | custom-call | tf_op jit(solution)/shard_map/pallas_call | solution.py:112
  139.6 1.3 copy.67
  141.0 0.0 copy-start.8
  141.0 0.0 copy-start.9
  141.0 0.0 copy-start.10
  141.0 0.4 reshape.49
  141.4 20.5 %all_to_all.42 = f32[16,48,128]{2,1,0:T(8,128)S(1)} all-to-all(f32[16,48,128]{2,1,0:T(8,128)S(1)} %reshape.49), channel_id=1, replica_groups=mesh['dp'=16,'mp'=32] {'dp'}, dimensions={0} | all-to-all | bytes 786432 | tf_op jit(solution)/shard_map/all_to_all | solution.py:40
  162.0 0.1 mul.75
  162.1 0.1 div.24
  162.1 0.1 mul.71
  162.2 0.0 copy-done.8
  162.2 0.0 copy-done.9
  162.2 0.0 copy-done.10
  162.2 0.7 divide_subtract_fusion
  (3 shorter events, 0.1 us)
Async XLA Ops:
  0.6 29.8 %copy-start.3 = (f32[1,6,2,64,64]{4,3,2,1,0:T(8,128)S(1)}, f32[1,6,2,64,64]{4,3,2,1,0:T(8,128)}, u32[]{:S(2)}) copy-start(f32[1,6,2,64,64]{4,3,2,1,0:T(8,128)} %param.11) | copy-start | bytes 589828
  29.6 0.9 copy-start.1
  30.5 1.0 copy-start.4
  30.7 1.1 copy-start.6
  84.6 2.3 %copy-start = (bf16[2048,3,2,64]{0,3,2,1:T(8,128)(2,1)}, bf16[2048,3,2,64]{0,3,2,1:T(8,128)(2,1)S(1)}, u32[]{:S(2)}) copy-start(bf16[2048,3,2,64]{0,3,2,1:T(8,128)(2,1)S(1)} %all_to_all.32) | copy-start | bytes 4718596
  84.6 2.3 %copy-start.7 = (bf16[6,2,64,64]{3,2,1,0:T(8,128)(2,1)S(1)}, bf16[6,2,64,64]{3,2,1,0:T(8,128)(2,1)}, u32[]{:S(2)}) copy-start(bf16[6,2,64,64]{3,2,1,0:T(8,128)(2,1)} %copy-done.6) | copy-start | bytes 294916
  87.6 1.1 copy-start.5
  91.5 5.1 %copy-start.2 = (f32[64,2,6,2,64]{4,0,3,2,1:T(8,128)S(1)}, f32[64,2,6,2,64]{4,0,3,2,1:T(8,128)}, u32[]{:S(2)}) copy-start(f32[64,2,6,2,64]{4,0,3,2,1:T(8,128)} %copy-done.1) | copy-start | bytes 1179652
  91.5 40.9 %all-to-all-start.1 = ((bf16[2048,3,64,2]{0,3,1,2:T(2,128)(2,1)}), bf16[2048,3,64,2]{0,3,1,2:T(2,128)(2,1)S(1)}, u32[]{:S(2)}, u32[]{:S(2)}) async-start(bf16[2048,3,64,2]{0,3,1,2:T(2,128)(2,1)} %copy.48), calls=%async_computation.1 | async-start | bytes 3145728 | tf_op jit(solution)/shard_map/all_to_all | solution.py:160
  141.0 21.2 %copy-start.8 = (f32[6,2,4,64]{3,2,1,0:T(4,128)S(1)}, f32[6,2,4,64]{3,2,1,0:T(4,128)}, u32[]{:S(2)}) copy-start(f32[6,2,4,64]{3,2,1,0:T(4,128)} %param.8) | copy-start | bytes 36868
  141.0 21.2 %copy-start.9 = (f32[6,2,4,64]{3,2,1,0:T(4,128)S(1)}, f32[6,2,4,64]{3,2,1,0:T(4,128)}, u32[]{:S(2)}) copy-start(f32[6,2,4,64]{3,2,1,0:T(4,128)} %param.9) | copy-start | bytes 36868
  141.0 21.2 %copy-start.10 = (f32[6,2,4,64]{3,2,1,0:T(4,128)S(1)}, f32[6,2,4,64]{3,2,1,0:T(4,128)}, u32[]{:S(2)}) copy-start(f32[6,2,4,64]{3,2,1,0:T(4,128)} %param.10) | copy-start | bytes 36868

commit v12 on v11

--- a/solution.py
+++ b/solution.py
@@ -26,9 +26,10 @@
 
 
 def gather_rows(stacked, groups):
-    moved = jnp.moveaxis(stacked, 3, 0)
-    full = lax.all_gather(moved, "dp", axis=0, tiled=True)
-    return jnp.moveaxis(full, 0, 3)
+    shape = stacked.shape
+    full = lax.all_gather(stacked.reshape(-1, 128), "dp", axis=0, tiled=True)
+    full = jnp.moveaxis(full.reshape((groups,) + shape), 0, 3)
+    return full.reshape(shape[:3] + (groups * shape[3], shape[4]))
 
 
 def scatter_rows(stacked, groups):

time: 164 us -> 161 us (0.982)
  waiting for transfers between devices: 27.2 us -> 29.2 us
    all_to_all x1, waiting for transfers between devices: 27.2 us -> 29.2 us  [per_device(): lax.all_to_all(jnp.stack([outer, back_left, back_right], axis=1), 'mp', s...]
  transfers between devices with their start and end apart: 1 -> 1, of which waited for: 1 -> 1; matrix products, arithmetic and copies ran while one was open for 3% -> 2% of each run, Pallas kernels for 2% -> 2%
where the time goes in v12:
time: 161 us
  blocking collectives  94.9 us (59%)
  waiting for transfers between devices  29.2 us (18%)
  local copies, waits for them, and re-layouts  17.9 us (11%)
  Pallas kernels  7.52 us (5%)
  starting transfers between devices  4.93 us (3%)
  matrix products  3.17 us (2%)
  other arithmetic  2 us (1%)
    all_to_all x1, blocking collectives, per_device(): lax.all_to_all(jnp.stack([y_left, y_right, back_outer], axis=1), 'mp', sp...  48.9 us
    all_to_all x1, waiting for transfers between devices, per_device(): lax.all_to_all(jnp.stack([outer, back_left, back_right], axis=1), 'mp', s...  29.2 us
    all_gather x1, blocking collectives, gather_rows(): full = lax.all_gather(stacked.reshape(-1, 128), 'dp', axis=0, tiled=True)  25.5 us
    all_to_all x1, blocking collectives, scatter_rows(): got = lax.all_to_all(dense, 'dp', split_axis=0, concat_axis=0, tiled=True)  20.5 us
    pallas_call x2, Pallas kernels, grads_and_curvature(): pl.pallas_call(kernel, grid=(tokens // tb,), in_specs=in_specs, out_specs...  7.52 us
    all_to_all x1, starting transfers between devices, per_device(): lax.all_to_all(jnp.stack([outer, back_left, back_right], axis=1), 'mp', s...  4.93 us
    all_to_all x2, local copies, waits for them, and re-layouts, per_device(): lax.all_to_all(jnp.stack([outer, back_left, back_right], axis=1), 'mp', s...  3.31 us
  transfers between devices with their start and end apart: 1, of which 1 were waited for; matrix products, arithmetic and copies ran while one was open for 2% of the time, Pallas kernels for 2%

profile of v12, /device:TPU:1, one launch (start us, length us, event | category | flops | bytes accessed | tf_op | source)
XLA Modules:
  0.0 160.6 jit_solution(2968591017758087102)
XLA Ops:
  0.6 0.8 pad_maximum_fusion.2
  1.4 0.1 reshape.54
  1.5 25.5 %all_gather.3 = f32[768,128]{1,0:T(8,128)S(1)} all-gather(f32[48,128]{1,0:T(8,128)S(1)} %reshape.54), channel_id=1, replica_groups=mesh['dp'=16,'mp'=32] {'dp'}, dimensions={0}, use_global_device_ids=true | all-gather | bytes 417792 | tf_op jit(solution)/shard_map/all_gather | solution.py:30
  27.0 0.4 reshape.55
  27.4 0.5 copy.85
  27.9 0.0 copy-start.4
  27.9 0.1 fusion.8
  28.0 0.0 copy-start.2
  28.0 0.2 copy.57
  28.2 0.0 copy-start.1
  28.2 0.2 copy.56
  28.4 0.6 copy-done.4
  28.9 0.2 copy.58
  29.1 0.0 copy-done.2
  29.1 0.0 copy-start.3
  29.1 0.1 add_convert_fusion
  29.2 0.0 copy-done.1
  29.2 0.0 copy-start.5
  29.2 0.3 fusion.1
  29.6 0.3 fusion
  29.9 0.3 copy-done.3
  30.3 0.2 copy.61
  30.5 0.0 copy-done.5
  30.5 0.3 fusion.2
  30.8 0.2 pad_maximum_fusion
  30.9 1.6 %copy.62 = bf16[2048,3,64,2]{0,3,1,2:T(2,128)(2,1)S(1)} copy(bf16[2048,3,64,2]{0,2,3,1:T(8,128)(2,1)S(1)} %pad_maximum_fusion) | data formatting | bytes 3145728 | tf_op jit(solution)/shard_map/stack | solution.py:142
  32.6 48.9 %all_to_all.41 = bf16[2048,3,64,2]{0,3,1,2:T(2,128)(2,1)S(1)} all-to-all(bf16[2048,3,64,2]{0,3,1,2:T(2,128)(2,1)S(1)} %copy.62), channel_id=1, replica_groups=mesh['dp'=16,'mp'=32] {'mp'}, dimensions={2} | all-to-all | bytes 3145728 | tf_op jit(solution)/shard_map/all_to_all | solution.py:141
  81.4 1.3 copy.83
  82.7 0.0 copy-start.6
  82.7 0.6 all_to_all.32
  83.4 0.3 copy-done.6
  83.6 0.0 copy-start
  83.6 0.3 convolution_bitcast_fusion
  83.9 0.3 convolution_bitcast_fusion.2
  84.3 0.5 copy-done
  84.8 0.7 multiply_convert_fusion.2
  85.5 0.3 fusion.3
  85.8 0.3 fusion.4
  86.1 0.3 fusion.5
  86.4 0.2 pad_maximum_fusion.1
  86.6 2.8 %copy.67 = bf16[2048,3,64,2]{0,3,1,2:T(2,128)(2,1)} copy(bf16[2048,3,64,2]{0,2,3,1:T(8,128)(2,1)S(1)} %pad_maximum_fusion.1) | data formatting | bytes 3145728 | tf_op jit(solution)/shard_map/stack | solution.py:162
  89.4 4.9 %all-to-all-start.1 = ((bf16[2048,3,64,2]{0,3,1,2:T(2,128)(2,1)}), bf16[2048,3,64,2]{0,3,1,2:T(2,128)(2,1)S(1)}, u32[]{:S(2)}, u32[]{:S(2)}) async-start(bf16[2048,3,64,2]{0,3,1,2:T(2,128)(2,1)} %copy.67), calls=%async_computation.1 | async-start | bytes 3145728 | tf_op jit(solution)/shard_map/all_to_all | solution.py:161
  94.3 1.0 copy.70.refs_2_
  95.3 1.0 copy.69.refs_1_
  96.3 1.0 copy.71.refs_3_
  97.3 3.7 %shard_map.85.refs_5_ = f32[2,6,2,64,64]{4,3,2,1,0:T(8,128)} custom-call(bf16[3,2,64,2048]{3,2,1,0:T(8,128)(2,1)} %bitcast.102, bf16[2048,128]{1,0:T(8,128)(2,1)} %copy.69.refs_1_, bf16[2048,128]{1,0:T(8,128)(2,1)} %copy.70.refs_2_, bf16[2048,128]{1,0:T(8,128)(2,1)} %copy.71.refs_3_, f32[6,2,64,64]{3,2,1,0:T(8,128)} %bitcast.114, f32[6,2,64,64]{3,2,1,0:T(8,128)} %bitcast.110), custom_call_target="tpu_custom_call" | custom-call | tf_op jit(solution)/shard_map/pallas_call | solution.py:113
  101.0 29.2 %all-to-all-done.1 = bf16[2048,3,64,2]{0,3,1,2:T(2,128)(2,1)S(1)} async-done(((bf16[2048,3,64,2]{0,3,1,2:T(2,128)(2,1)}), bf16[2048,3,64,2]{0,3,1,2:T(2,128)(2,1)S(1)}, u32[]{:S(2)}, u32[]{:S(2)}) %all-to-all-start.1) | async-done | bytes 1572896 | tf_op jit(solution)/shard_map/all_to_all | solution.py:161
  130.1 1.3 copy.82
  131.4 2.0 %all_to_all.36 = bf16[2048,3,2,64]{0,3,2,1:T(8,128)(2,1)} reshape(bf16[2048,3,2,32,2]{0,4,3,2,1:T(2,128)(2,1)S(1)} %bitcast.108) | data formatting | bytes 3145728 | tf_op jit(solution)/shard_map/all_to_all | solution.py:161
  133.5 3.9 %shard_map.86 = f32[2,6,2,64,64]{4,3,2,1,0:T(8,128)} custom-call(bf16[3,2,64,2048]{3,2,1,0:T(8,128)(2,1)} %bitcast.105, bf16[2048,128]{1,0:T(8,128)(2,1)} %refs_1_.1, bf16[2048,128]{1,0:T(8,128)(2,1)} %refs_2_.1, f32[6,2,64,64]{3,2,1,0:T(8,128)} %bitcast.115, f32[6,2,64,64]{3,2,1,0:T(8,128)} %bitcast.111, ...), custom_call_target="tpu_custom_call", output_to_operand_aliasing={{}: (5, {})} | custom-call | tf_op jit(solution)/shard_map/pallas_call | solution.py:113
  137.3 1.3 copy.84
  138.7 0.0 copy-start.7
  138.7 0.0 copy-start.8
  138.7 0.0 copy-start.9
  138.7 0.4 reshape.62
  139.1 20.5 %all_to_all.42 = f32[16,48,128]{2,1,0:T(8,128)S(1)} all-to-all(f32[16,48,128]{2,1,0:T(8,128)S(1)} %reshape.62), channel_id=1, replica_groups=mesh['dp'=16,'mp'=32] {'dp'}, dimensions={0} | all-to-all | bytes 786432 | tf_op jit(solution)/shard_map/all_to_all | solution.py:41
  159.7 0.1 mul.75
  159.8 0.1 div.24
  159.8 0.1 mul.71
  159.9 0.0 copy-done.7
  159.9 0.0 copy-done.8
  159.9 0.0 copy-done.9
  159.9 0.7 divide_subtract_fusion
  (2 shorter events, 0.0 us)
Async XLA Ops:
  27.9 1.0 copy-start.4
  28.0 1.1 copy-start.2
  28.2 1.0 copy-start.1
  29.1 1.1 copy-start.3
  29.2 1.2 copy-start.5
  82.7 0.9 copy-start.6
  83.6 1.1 copy-start
  89.4 40.8 %all-to-all-start.1 = ((bf16[2048,3,64,2]{0,3,1,2:T(2,128)(2,1)}), bf16[2048,3,64,2]{0,3,1,2:T(2,128)(2,1)S(1)}, u32[]{:S(2)}, u32[]{:S(2)}) async-start(bf16[2048,3,64,2]{0,3,1,2:T(2,128)(2,1)} %copy.67), calls=%async_computation.1 | async-start | bytes 3145728 | tf_op jit(solution)/shard_map/all_to_all | solution.py:161
  138.7 21.2 %copy-start.7 = (f32[6,2,4,64]{3,2,1,0:T(4,128)S(1)}, f32[6,2,4,64]{3,2,1,0:T(4,128)}, u32[]{:S(2)}) copy-start(f32[6,2,4,64]{3,2,1,0:T(4,128)} %param.8) | copy-start | bytes 36868
  138.7 21.2 %copy-start.8 = (f32[6,2,4,64]{3,2,1,0:T(4,128)S(1)}, f32[6,2,4,64]{3,2,1,0:T(4,128)}, u32[]{:S(2)}) copy-start(f32[6,2,4,64]{3,2,1,0:T(4,128)} %param.9) | copy-start | bytes 36868
  138.7 21.2 %copy-start.9 = (f32[6,2,4,64]{3,2,1,0:T(4,128)S(1)}, f32[6,2,4,64]{3,2,1,0:T(4,128)}, u32[]{:S(2)}) copy-start(f32[6,2,4,64]{3,2,1,0:T(4,128)} %param.10) | copy-start | bytes 36868

commit v13 on v12

--- a/solution.py
+++ b/solution.py
@@ -52,13 +52,12 @@
     return lax.dot_general(a, b, (((1,), (0,)), ((), ())), preferred_element_type=jnp.float32)
 
 
-def grads_kernel(*refs, scale, pairs, n_minor, n_major, carry):
-    minor = refs[:n_minor]
-    major = refs[n_minor:n_minor + n_major]
-    noise_ref, spread_ref = refs[n_minor + n_major:n_minor + n_major + 2]
-    rest = refs[n_minor + n_major + 2:]
-    prev_ref = rest[0] if carry else None
-    out_ref, acc_ref = rest[-2], rest[-1]
+def grads_kernel(*refs, scale, pairs, n_major, n_out, carry):
+    minor_ref = refs[0]
+    major = refs[1:1 + n_major]
+    noise_refs = refs[1 + n_major:1 + n_major + n_out]
+    spread_refs = refs[1 + n_major + n_out:1 + n_major + 2 * n_out]
+    out_ref, acc_ref = refs[-2], refs[-1]
     step = pl.program_id(0)
     nb, width = acc_ref.shape[1], acc_ref.shape[2]
 
@@ -68,54 +67,47 @@
 
     for b in range(nb):
         cols = slice(b * width, (b + 1) * width)
-        for k, (f, lhs, rhs, flip) in enumerate(pairs):
-            acc_ref[k, b] += nn_dot(minor[0][lhs, b], major[rhs][:, cols])
+        for k, (q, lhs, rhs, flip) in enumerate(pairs):
+            acc_ref[k, b] += nn_dot(minor_ref[lhs, b], major[rhs][:, cols])
 
     @pl.when(step == pl.num_programs(0) - 1)
     def _():
-        done = set()
-        for k, (f, lhs, rhs, flip) in enumerate(pairs):
-            done.add(f)
+        for k, (q, lhs, rhs, flip) in enumerate(pairs):
             for b in range(nb):
                 grad = acc_ref[k, b]
                 if flip:
                     grad = grad.T
                 grad = grad * scale
-                out_ref[0, f, b] = grad
-                out_ref[1, f, b] = grad * noise_ref[f, b] * spread_ref[f, b]
-        if carry:
-            for f in range(noise_ref.shape[0]):
-                if f not in done:
-                    out_ref[:, f] = prev_ref[:, f]
+                out_ref[0, q, b] = grad
+                out_ref[1, q, b] = grad * noise_refs[q][0, b] * spread_refs[q][0, b]
 
 
-def grads_and_curvature(minor, major, noise, spread, scale, pairs, prev=None):
+def grads_and_curvature(minor, major, noise, spread, scale, pairs, factors, half, prev=None):
     n_minor, nb, width, tokens = minor.shape
     feats = major[0].shape[1]
     tb = min(TOKEN_BLOCK, tokens)
-    whole4 = pl.BlockSpec(noise.shape, lambda i: (0, 0, 0, 0))
-    whole5 = pl.BlockSpec((2,) + noise.shape, lambda i: (0, 0, 0, 0, 0))
+    n_out = len(factors)
+    picks = [pl.BlockSpec((1, nb, width, width), lambda i, f=f: (f, 0, 0, 0)) for f in factors]
     in_specs = (
         [pl.BlockSpec((n_minor, nb, width, tb), lambda i: (0, 0, 0, i))]
         + [pl.BlockSpec((tb, feats), lambda i: (i, 0))] * len(major)
-        + [whole4, whole4]
+        + picks + picks
     )
-    operands = [minor] + list(major) + [noise, spread]
+    operands = [minor] + list(major) + [noise] * n_out + [spread] * n_out
     aliases = {}
     if prev is not None:
-        in_specs.append(whole5)
+        in_specs.append(pl.BlockSpec(memory_space=pl.ANY))
         aliases = {len(operands): 0}
         operands.append(prev)
     kernel = functools.partial(
-        grads_kernel, scale=scale, pairs=pairs, n_minor=1, n_major=len(major),
-        carry=prev is not None,
+        grads_kernel, scale=scale, pairs=pairs, n_major=len(major), n_out=n_out, carry=prev is not None,
     )
     return pl.pallas_call(
         kernel,
         grid=(tokens // tb,),
         in_specs=in_specs,
-        out_specs=whole5,
-        out_shape=jax.ShapeDtypeStruct((2,) + noise.shape, jnp.float32),
+        out_specs=pl.BlockSpec((2, n_out, nb, width, width), lambda i: (0, half, 0, 0, 0)),
+        out_shape=jax.ShapeDtypeStruct((2, 2 * n_out, nb, width, width), jnp.float32),
         scratch_shapes=[pltpu.VMEM((len(pairs), nb, width, width), jnp.float32)],
         input_output_aliases=aliases,
         compiler_params=pltpu.CompilerParams(dimension_semantics=("arbitrary",)),
@@ -156,7 +148,8 @@
     first_t = token_minor(first)
     early = grads_and_curvature(
         first_t, [flat(gate_grad), flat(value_grad), flat(hidden)],
-        noise, spread, scale, pairs=((1, 0, 0, False), (3, 1, 1, False), (4, 2, 2, True)),
+        noise, spread, scale, pairs=((0, 0, 0, False), (1, 1, 1, False), (2, 2, 2, True)),
+        factors=(1, 3, 4), half=1,
     )
     second = lax.all_to_all(
         jnp.stack([outer, back_left, back_right], axis=1), "mp", split_axis=2, concat_axis=3, tiled=True
@@ -164,9 +157,13 @@
     second_t = token_minor(second)
     stacked = grads_and_curvature(
         second_t, [inputs, out_grad],
-        noise, spread, scale, pairs=((0, 1, 0, True), (2, 2, 0, True), (5, 0, 1, False)), prev=early,
+        noise, spread, scale, pairs=((0, 1, 0, True), (1, 2, 0, True), (2, 0, 1, False)),
+        factors=(0, 2, 5), half=0, prev=early,
     )
-    sums = scatter_rows(stacked, groups)
+    slots = scatter_rows(stacked, groups)
+    sums = jnp.concatenate(
+        [slots[:, 0:1], slots[:, 3:4], slots[:, 1:2], slots[:, 4:5], slots[:, 5:6], slots[:, 2:3]], axis=1
+    )
     grad_avg = sums[0] / groups
     hess_avg = sums[1] / groups
     new_grad = BETA_GRAD * grad_state + (1.0 - BETA_GRAD) * grad_avg

time: 161 us -> 160 us (level)
  no operation moved by 1% of the time
where the time goes in v13:
time: 160 us
  blocking collectives  94.9 us (59%)
  waiting for transfers between devices  29.5 us (18%)
  local copies, waits for them, and re-layouts  17.5 us (11%)
  Pallas kernels  6.63 us (4%)
  starting transfers between devices  4.94 us (3%)
  matrix products  3.17 us (2%)
  other arithmetic  2 us (1%)
    all_to_all x1, blocking collectives, per_device(): lax.all_to_all(jnp.stack([y_left, y_right, back_outer], axis=1), 'mp', sp...  48.9 us
    all_to_all x1, waiting for transfers between devices, per_device(): lax.all_to_all(jnp.stack([outer, back_left, back_right], axis=1), 'mp', s...  29.5 us
    all_gather x1, blocking collectives, gather_rows(): full = lax.all_gather(stacked.reshape(-1, 128), 'dp', axis=0, tiled=True)  25.5 us
    all_to_all x1, blocking collectives, scatter_rows(): got = lax.all_to_all(dense, 'dp', split_axis=0, concat_axis=0, tiled=True)  20.5 us
    pallas_call x2, Pallas kernels, grads_and_curvature(): pl.pallas_call(kernel, grid=(tokens // tb,), in_specs=in_specs, out_specs...  6.63 us
    all_to_all x1, starting transfers between devices, per_device(): lax.all_to_all(jnp.stack([outer, back_left, back_right], axis=1), 'mp', s...  4.94 us
    all_to_all x2, local copies, waits for them, and re-layouts, per_device(): lax.all_to_all(jnp.stack([outer, back_left, back_right], axis=1), 'mp', s...  3.31 us
  transfers between devices with their start and end apart: 1, of which 1 were waited for; matrix products, arithmetic and copies ran while one was open for 2% of the time, Pallas kernels for 2%

profile of v13, /device:TPU:1, one launch (start us, length us, event | category | flops | bytes accessed | tf_op | source)
XLA Modules:
  0.0 159.6 jit_solution(15491274178183589185)
XLA Ops:
  0.6 0.8 pad_maximum_fusion.2
  1.4 0.1 reshape.52
  1.5 25.5 %all_gather.3 = f32[768,128]{1,0:T(8,128)S(1)} all-gather(f32[48,128]{1,0:T(8,128)S(1)} %reshape.52), channel_id=1, replica_groups=mesh['dp'=16,'mp'=32] {'dp'}, dimensions={0}, use_global_device_ids=true | all-gather | bytes 417792 | tf_op jit(solution)/shard_map/all_gather | solution.py:30
  27.0 0.4 reshape.53
  27.4 0.5 copy.85
  27.9 0.0 copy-start.4
  27.9 0.1 fusion.8
  28.0 0.0 copy-start.1
  28.0 0.2 copy.57
  28.2 0.0 copy-start
  28.2 0.2 copy.56
  28.4 0.6 copy-done.4
  28.9 0.2 copy.58
  29.1 0.0 copy-done.1
  29.1 0.0 copy-start.3
  29.1 0.1 add_convert_fusion
  29.2 0.0 copy-done
  29.2 0.3 fusion.1
  29.6 0.3 fusion
  29.9 0.3 copy-done.3
  30.2 0.2 copy.61
  30.4 0.3 fusion.2
  30.7 0.2 pad_maximum_fusion
  30.9 1.6 %copy.62 = bf16[2048,3,64,2]{0,3,1,2:T(2,128)(2,1)S(1)} copy(bf16[2048,3,64,2]{0,2,3,1:T(8,128)(2,1)S(1)} %pad_maximum_fusion) | data formatting | bytes 3145728 | tf_op jit(solution)/shard_map/stack | solution.py:134
  32.5 48.9 %all_to_all.41 = bf16[2048,3,64,2]{0,3,1,2:T(2,128)(2,1)S(1)} all-to-all(bf16[2048,3,64,2]{0,3,1,2:T(2,128)(2,1)S(1)} %copy.62), channel_id=1, replica_groups=mesh['dp'=16,'mp'=32] {'mp'}, dimensions={2} | all-to-all | bytes 3145728 | tf_op jit(solution)/shard_map/all_to_all | solution.py:133
  81.4 1.3 copy.83
  82.6 0.6 all_to_all.32
  83.3 0.0 copy-start.2
  83.3 0.3 convolution_bitcast_fusion
  83.6 0.3 convolution_bitcast_fusion.2
  83.9 0.5 copy-done.2
  84.4 0.7 multiply_convert_fusion.2
  85.1 0.3 fusion.3
  85.5 0.3 fusion.4
  85.8 0.3 fusion.5
  86.1 0.2 pad_maximum_fusion.1
  86.2 2.8 %copy.67 = bf16[2048,3,64,2]{0,3,1,2:T(2,128)(2,1)} copy(bf16[2048,3,64,2]{0,2,3,1:T(8,128)(2,1)S(1)} %pad_maximum_fusion.1) | data formatting | bytes 3145728 | tf_op jit(solution)/shard_map/stack | solution.py:155
  89.0 4.9 %all-to-all-start.1 = ((bf16[2048,3,64,2]{0,3,1,2:T(2,128)(2,1)}), bf16[2048,3,64,2]{0,3,1,2:T(2,128)(2,1)S(1)}, u32[]{:S(2)}, u32[]{:S(2)}) async-start(bf16[2048,3,64,2]{0,3,1,2:T(2,128)(2,1)} %copy.67), calls=%async_computation.1 | async-start | bytes 3145728 | tf_op jit(solution)/shard_map/all_to_all | solution.py:154
  94.0 1.0 copy.70.refs_2_
  95.0 1.0 copy.69.refs_1_
  96.0 1.0 copy.71.refs_3_
  97.0 3.3 %shard_map.85.refs_9_ = f32[2,6,2,64,64]{4,3,2,1,0:T(8,128)} custom-call(bf16[3,2,64,2048]{3,2,1,0:T(8,128)(2,1)} %bitcast.136, bf16[2048,128]{1,0:T(8,128)(2,1)} %copy.69.refs_1_, bf16[2048,128]{1,0:T(8,128)(2,1)} %copy.70.refs_2_, bf16[2048,128]{1,0:T(8,128)(2,1)} %copy.71.refs_3_, f32[6,2,64,64]{3,2,1,0:T(8,128)} %bitcast.130, ...), custom_call_target="tpu_custom_call" | custom-call | tf_op jit(solution)/shard_map/pallas_call | solution.py:105
  100.3 29.5 %all-to-all-done.1 = bf16[2048,3,64,2]{0,3,1,2:T(2,128)(2,1)S(1)} async-done(((bf16[2048,3,64,2]{0,3,1,2:T(2,128)(2,1)}), bf16[2048,3,64,2]{0,3,1,2:T(2,128)(2,1)S(1)}, u32[]{:S(2)}, u32[]{:S(2)}) %all-to-all-start.1) | async-done | bytes 1572896 | tf_op jit(solution)/shard_map/all_to_all | solution.py:154
  129.8 1.3 copy.82
  131.1 2.0 %all_to_all.36 = bf16[2048,3,2,64]{0,3,2,1:T(8,128)(2,1)} reshape(bf16[2048,3,2,32,2]{0,4,3,2,1:T(2,128)(2,1)S(1)} %bitcast.141) | data formatting | bytes 3145728 | tf_op jit(solution)/shard_map/all_to_all | solution.py:154
  133.1 3.3 %shard_map.86 = f32[2,6,2,64,64]{4,3,2,1,0:T(8,128)} custom-call(bf16[3,2,64,2048]{3,2,1,0:T(8,128)(2,1)} %bitcast.142, bf16[2048,128]{1,0:T(8,128)(2,1)} %refs_1_.1, bf16[2048,128]{1,0:T(8,128)(2,1)} %refs_2_.1, f32[6,2,64,64]{3,2,1,0:T(8,128)} %bitcast.133, f32[6,2,64,64]{3,2,1,0:T(8,128)} %bitcast.134, ...), custom_call_target="tpu_custom_call", output_to_operand_aliasing={{}: (9, {})} | custom-call | tf_op jit(solution)/shard_map/pallas_call | solution.py:105
  136.4 1.3 copy.84
  137.8 0.0 copy-start.5
  137.8 0.0 copy-start.6
  137.8 0.0 copy-start.7
  137.8 0.4 reshape.60
  138.2 20.5 %all_to_all.42 = f32[16,48,128]{2,1,0:T(8,128)S(1)} all-to-all(f32[16,48,128]{2,1,0:T(8,128)S(1)} %reshape.60), channel_id=1, replica_groups=mesh['dp'=16,'mp'=32] {'dp'}, dimensions={0} | all-to-all | bytes 786432 | tf_op jit(solution)/shard_map/all_to_all | solution.py:41
  158.7 0.1 reshape.61
  158.9 0.0 copy-done.5
  158.9 0.0 copy-done.6
  158.9 0.0 copy-done.7
  158.9 0.7 divide_subtract_fusion
  (6 shorter events, 0.1 us)
Async XLA Ops:
  27.9 1.0 copy-start.4
  28.0 1.1 copy-start.1
  28.2 1.0 copy-start
  29.1 1.0 copy-start.3
  83.3 1.2 copy-start.2
  89.0 40.8 %all-to-all-start.1 = ((bf16[2048,3,64,2]{0,3,1,2:T(2,128)(2,1)}), bf16[2048,3,64,2]{0,3,1,2:T(2,128)(2,1)S(1)}, u32[]{:S(2)}, u32[]{:S(2)}) async-start(bf16[2048,3,64,2]{0,3,1,2:T(2,128)(2,1)} %copy.67), calls=%async_computation.1 | async-start | bytes 3145728 | tf_op jit(solution)/shard_map/all_to_all | solution.py:154
  137.8 21.1 %copy-start.5 = (f32[6,2,4,64]{3,2,1,0:T(4,128)S(1)}, f32[6,2,4,64]{3,2,1,0:T(4,128)}, u32[]{:S(2)}) copy-start(f32[6,2,4,64]{3,2,1,0:T(4,128)} %param.8) | copy-start | bytes 36868
  137.8 21.1 %copy-start.6 = (f32[6,2,4,64]{3,2,1,0:T(4,128)S(1)}, f32[6,2,4,64]{3,2,1,0:T(4,128)}, u32[]{:S(2)}) copy-start(f32[6,2,4,64]{3,2,1,0:T(4,128)} %param.9) | copy-start | bytes 36868
  137.8 21.1 %copy-start.7 = (f32[6,2,4,64]{3,2,1,0:T(4,128)S(1)}, f32[6,2,4,64]{3,2,1,0:T(4,128)}, u32[]{:S(2)}) copy-start(f32[6,2,4,64]{3,2,1,0:T(4,128)} %param.10) | copy-start | bytes 36868

commit v14 on v13

--- a/solution.py
+++ b/solution.py
@@ -82,10 +82,10 @@
                 out_ref[1, q, b] = grad * noise_refs[q][0, b] * spread_refs[q][0, b]
 
 
-def grads_and_curvature(minor, major, noise, spread, scale, pairs, factors, half, prev=None):
+def grads_and_curvature(minor, major, noise, spread, scale, pairs, factors, half, prev=None, block=TOKEN_BLOCK):
     n_minor, nb, width, tokens = minor.shape
     feats = major[0].shape[1]
-    tb = min(TOKEN_BLOCK, tokens)
+    tb = min(block, tokens)
     n_out = len(factors)
     picks = [pl.BlockSpec((1, nb, width, width), lambda i, f=f: (f, 0, 0, 0)) for f in factors]
     in_specs = (
@@ -158,7 +158,7 @@
     stacked = grads_and_curvature(
         second_t, [inputs, out_grad],
         noise, spread, scale, pairs=((0, 1, 0, True), (1, 2, 0, True), (2, 0, 1, False)),
-        factors=(0, 2, 5), half=0, prev=early,
+        factors=(0, 2, 5), half=0, prev=early, block=TOKEN_BLOCK // 2,
     )
     slots = scatter_rows(stacked, groups)
     sums = jnp.concatenate(

time: 160 us -> 161 us (level)
  no operation moved by 1% of the time
where the time goes in v14:
time: 161 us
  blocking collectives  94.9 us (59%)
  waiting for transfers between devices  29.5 us (18%)
  local copies, waits for them, and re-layouts  17.5 us (11%)
  Pallas kernels  7.64 us (5%)
  starting transfers between devices  4.94 us (3%)
  matrix products  3.17 us (2%)
  other arithmetic  2 us (1%)
    all_to_all x1, blocking collectives, per_device(): lax.all_to_all(jnp.stack([y_left, y_right, back_outer], axis=1), 'mp', sp...  48.9 us
    all_to_all x1, waiting for transfers between devices, per_device(): lax.all_to_all(jnp.stack([outer, back_left, back_right], axis=1), 'mp', s...  29.5 us
    all_gather x1, blocking collectives, gather_rows(): full = lax.all_gather(stacked.reshape(-1, 128), 'dp', axis=0, tiled=True)  25.5 us
    all_to_all x1, blocking collectives, scatter_rows(): got = lax.all_to_all(dense, 'dp', split_axis=0, concat_axis=0, tiled=True)  20.5 us
    pallas_call x2, Pallas kernels, grads_and_curvature(): pl.pallas_call(kernel, grid=(tokens // tb,), in_specs=in_specs, out_specs...  7.64 us
    all_to_all x1, starting transfers between devices, per_device(): lax.all_to_all(jnp.stack([outer, back_left, back_right], axis=1), 'mp', s...  4.94 us
    all_to_all x2, local copies, waits for them, and re-layouts, per_device(): lax.all_to_all(jnp.stack([outer, back_left, back_right], axis=1), 'mp', s...  3.31 us
  transfers between devices with their start and end apart: 1, of which 1 were waited for; matrix products, arithmetic and copies ran while one was open for 2% of the time, Pallas kernels for 2%

profile of v14, /device:TPU:1, one launch (start us, length us, event | category | flops | bytes accessed | tf_op | source)
XLA Modules:
  0.0 160.6 jit_solution(18106332561572118269)
XLA Ops:
  0.6 0.8 pad_maximum_fusion.2
  1.4 0.1 reshape.52
  1.5 25.5 %all_gather.3 = f32[768,128]{1,0:T(8,128)S(1)} all-gather(f32[48,128]{1,0:T(8,128)S(1)} %reshape.52), channel_id=1, replica_groups=mesh['dp'=16,'mp'=32] {'dp'}, dimensions={0}, use_global_device_ids=true | all-gather | bytes 417792 | tf_op jit(solution)/shard_map/all_gather | solution.py:30
  27.0 0.4 reshape.53
  27.4 0.5 copy.85
  27.9 0.0 copy-start.4
  27.9 0.1 fusion.8
  28.0 0.0 copy-start.1
  28.0 0.2 copy.57
  28.2 0.0 copy-start
  28.2 0.2 copy.56
  28.4 0.6 copy-done.4
  28.9 0.2 copy.58
  29.1 0.0 copy-done.1
  29.1 0.0 copy-start.3
  29.1 0.1 add_convert_fusion
  29.2 0.0 copy-done
  29.2 0.3 fusion.1
  29.6 0.3 fusion
  29.9 0.3 copy-done.3
  30.2 0.2 copy.61
  30.4 0.3 fusion.2
  30.7 0.2 pad_maximum_fusion
  30.9 1.6 %copy.62 = bf16[2048,3,64,2]{0,3,1,2:T(2,128)(2,1)S(1)} copy(bf16[2048,3,64,2]{0,2,3,1:T(8,128)(2,1)S(1)} %pad_maximum_fusion) | data formatting | bytes 3145728 | tf_op jit(solution)/shard_map/stack | solution.py:134
  32.5 48.9 %all_to_all.41 = bf16[2048,3,64,2]{0,3,1,2:T(2,128)(2,1)S(1)} all-to-all(bf16[2048,3,64,2]{0,3,1,2:T(2,128)(2,1)S(1)} %copy.62), channel_id=1, replica_groups=mesh['dp'=16,'mp'=32] {'mp'}, dimensions={2} | all-to-all | bytes 3145728 | tf_op jit(solution)/shard_map/all_to_all | solution.py:133
  81.4 1.3 copy.83
  82.6 0.6 all_to_all.32
  83.3 0.0 copy-start.2
  83.3 0.3 convolution_bitcast_fusion
  83.6 0.3 convolution_bitcast_fusion.2
  83.9 0.5 copy-done.2
  84.4 0.7 multiply_convert_fusion.2
  85.1 0.3 fusion.3
  85.5 0.3 fusion.4
  85.8 0.3 fusion.5
  86.1 0.2 pad_maximum_fusion.1
  86.2 2.8 %copy.67 = bf16[2048,3,64,2]{0,3,1,2:T(2,128)(2,1)} copy(bf16[2048,3,64,2]{0,2,3,1:T(8,128)(2,1)S(1)} %pad_maximum_fusion.1) | data formatting | bytes 3145728 | tf_op jit(solution)/shard_map/stack | solution.py:155
  89.0 4.9 %all-to-all-start.1 = ((bf16[2048,3,64,2]{0,3,1,2:T(2,128)(2,1)}), bf16[2048,3,64,2]{0,3,1,2:T(2,128)(2,1)S(1)}, u32[]{:S(2)}, u32[]{:S(2)}) async-start(bf16[2048,3,64,2]{0,3,1,2:T(2,128)(2,1)} %copy.67), calls=%async_computation.1 | async-start | bytes 3145728 | tf_op jit(solution)/shard_map/all_to_all | solution.py:154
  94.0 1.0 copy.70.refs_2_
  95.0 1.0 copy.69.refs_1_
  96.0 1.0 copy.71.refs_3_
  97.0 3.3 %shard_map.85.refs_9_ = f32[2,6,2,64,64]{4,3,2,1,0:T(8,128)} custom-call(bf16[3,2,64,2048]{3,2,1,0:T(8,128)(2,1)} %bitcast.136, bf16[2048,128]{1,0:T(8,128)(2,1)} %copy.69.refs_1_, bf16[2048,128]{1,0:T(8,128)(2,1)} %copy.70.refs_2_, bf16[2048,128]{1,0:T(8,128)(2,1)} %copy.71.refs_3_, f32[6,2,64,64]{3,2,1,0:T(8,128)} %bitcast.130, ...), custom_call_target="tpu_custom_call" | custom-call | tf_op jit(solution)/shard_map/pallas_call | solution.py:105
  100.3 29.5 %all-to-all-done.1 = bf16[2048,3,64,2]{0,3,1,2:T(2,128)(2,1)S(1)} async-done(((bf16[2048,3,64,2]{0,3,1,2:T(2,128)(2,1)}), bf16[2048,3,64,2]{0,3,1,2:T(2,128)(2,1)S(1)}, u32[]{:S(2)}, u32[]{:S(2)}) %all-to-all-start.1) | async-done | bytes 1572896 | tf_op jit(solution)/shard_map/all_to_all | solution.py:154
  129.8 1.3 copy.82
  131.1 2.0 %all_to_all.36 = bf16[2048,3,2,64]{0,3,2,1:T(8,128)(2,1)} reshape(bf16[2048,3,2,32,2]{0,4,3,2,1:T(2,128)(2,1)S(1)} %bitcast.141) | data formatting | bytes 3145728 | tf_op jit(solution)/shard_map/all_to_all | solution.py:154
  133.1 4.3 %shard_map.86 = f32[2,6,2,64,64]{4,3,2,1,0:T(8,128)} custom-call(bf16[3,2,64,2048]{3,2,1,0:T(8,128)(2,1)} %bitcast.142, bf16[2048,128]{1,0:T(8,128)(2,1)} %refs_1_.1, bf16[2048,128]{1,0:T(8,128)(2,1)} %refs_2_.1, f32[6,2,64,64]{3,2,1,0:T(8,128)} %bitcast.133, f32[6,2,64,64]{3,2,1,0:T(8,128)} %bitcast.134, ...), custom_call_target="tpu_custom_call", output_to_operand_aliasing={{}: (9, {})} | custom-call | tf_op jit(solution)/shard_map/pallas_call | solution.py:105
  137.4 1.3 copy.84
  138.8 0.0 copy-start.5
  138.8 0.0 copy-start.6
  138.8 0.0 copy-start.7
  138.8 0.4 reshape.60
  139.2 20.5 %all_to_all.42 = f32[16,48,128]{2,1,0:T(8,128)S(1)} all-to-all(f32[16,48,128]{2,1,0:T(8,128)S(1)} %reshape.60), channel_id=1, replica_groups=mesh['dp'=16,'mp'=32] {'dp'}, dimensions={0} | all-to-all | bytes 786432 | tf_op jit(solution)/shard_map/all_to_all | solution.py:41
  159.7 0.1 reshape.61
  159.9 0.0 copy-done.5
  159.9 0.0 copy-done.6
  159.9 0.0 copy-done.7
  159.9 0.7 divide_subtract_fusion
  (6 shorter events, 0.1 us)
Async XLA Ops:
  27.9 1.0 copy-start.4
  28.0 1.1 copy-start.1
  28.2 1.0 copy-start
  29.1 1.0 copy-start.3
  83.3 1.2 copy-start.2
  89.0 40.8 %all-to-all-start.1 = ((bf16[2048,3,64,2]{0,3,1,2:T(2,128)(2,1)}), bf16[2048,3,64,2]{0,3,1,2:T(2,128)(2,1)S(1)}, u32[]{:S(2)}, u32[]{:S(2)}) async-start(bf16[2048,3,64,2]{0,3,1,2:T(2,128)(2,1)} %copy.67), calls=%async_computation.1 | async-start | bytes 3145728 | tf_op jit(solution)/shard_map/all_to_all | solution.py:154
  138.8 21.1 %copy-start.5 = (f32[6,2,4,64]{3,2,1,0:T(4,128)S(1)}, f32[6,2,4,64]{3,2,1,0:T(4,128)}, u32[]{:S(2)}) copy-start(f32[6,2,4,64]{3,2,1,0:T(4,128)} %param.8) | copy-start | bytes 36868
  138.8 21.1 %copy-start.6 = (f32[6,2,4,64]{3,2,1,0:T(4,128)S(1)}, f32[6,2,4,64]{3,2,1,0:T(4,128)}, u32[]{:S(2)}) copy-start(f32[6,2,4,64]{3,2,1,0:T(4,128)} %param.9) | copy-start | bytes 36868
  138.8 21.1 %copy-start.7 = (f32[6,2,4,64]{3,2,1,0:T(4,128)S(1)}, f32[6,2,4,64]{3,2,1,0:T(4,128)}, u32[]{:S(2)}) copy-start(f32[6,2,4,64]{3,2,1,0:T(4,128)} %param.10) | copy-start | bytes 36868
